TPU v7x, 256 devices: a whole 4x4x8 slice. The times are simulated.
256 devices in a mesh: ia: 8 (over y, core), ja: 8 (over z), ka: 4 (over x).
Axes of the slice: x: 4, y: 4, z: 8, core: 2. Of those that a mesh axis runs over, the one named last changes fastest.
Arguments:
- blocks: bfloat16 [256, 64, 64, 128], P(('ia', 'ja', 'ka')), may hold values from -6 to 6
- coords: int32 [3, 256], P(None, ('ia', 'ja', 'ka')), may hold values from 0 to 31, as said below
- live: int32 [256], P(('ia', 'ja', 'ka')), may hold values from 1 to 1, as said below
- factor_b: float32 [2048, 128], P('ja'), may hold values from -0.9 to 12
- factor_c: float32 [2048, 128], P('ka'), may hold values from -0.9 to 12
Outputs:
- loading_a: float32 [2048, 128], P('ia')
- loading_b: float32 [2048, 128], P('ja')
- loading_c: float32 [2048, 128], P('ka')
Inputs may be any that keep to these rules, and one draw needn't show every extreme that they name: `live`: slot d holds the block of device d (devices counted along ia, ja, ka, ia slowest). The slots of device (p, q, s) name blocks with coords[0] from p * 4 to p * 4 + 3, coords[1] from q * 4 to q * 4 + 3, coords[2] from s * 4 to s * 4 + 3; each device's slot names one block of its own 4 x 4 x 4 block region.
All inputs are finite; a program needn't handle non-finite values.
Results may differ from a plain program's by a relative error of at most 0.0057.
Values sent between devices are 32-bit elements; how exact they have to be, the bound alone decides.
No kernel may reach another device: no remote copies, remote signals or barrier semaphores. Data moves between devices by JAX's collectives and lax.ppermute only.
A program may use at most 64 MiB of HBM per device.

v0:
```python
import jax
import jax.numpy as jnp
from jax import lax
from jax.sharding import PartitionSpec as P

RANK = 128
BI = 64
BJ = 64
BK = 128
GI_DEV = 4
GJ_DEV = 4
GK_DEV = 4


RIDGE_SHARE = 0.3
EPSILON = 1e-06
HIGHEST = lax.Precision.HIGHEST
sweep_order = (0, 1, 2)


def factorize(gram_one, gram_two):
    merged = gram_one * gram_two
    order_rank = merged.shape[0]
    shift_value = RIDGE_SHARE * jnp.trace(merged) / order_rank
    lower_factor = jnp.linalg.cholesky(
        merged + shift_value * jnp.eye(order_rank, dtype=jnp.float32)
    )
    return lax.linalg.triangular_solve(
        lower_factor, jnp.eye(order_rank, dtype=jnp.float32), left_side=True, lower=True
    )


def apply_inverse(inverse_lower, values):
    middle = jnp.dot(values, inverse_lower.T, precision=HIGHEST, preferred_element_type=jnp.float32)
    return jnp.dot(middle, inverse_lower, precision=HIGHEST, preferred_element_type=jnp.float32)


def square_product(values):
    return jnp.dot(values.T, values, precision=HIGHEST, preferred_element_type=jnp.float32)


def grand_sum(values):
    return lax.psum(values, ("ia", "ja", "ka"))


def move_rows(mode_now, action, values):
    if mode_now == 0:
        if action == "reduce":
            return lax.psum_scatter(values, ("ja", "ka"), scatter_dimension=0, tiled=True)
        return lax.all_gather(values, ("ja", "ka"), axis=0, tiled=True)
    if mode_now == 1:
        if action == "reduce":
            return lax.psum_scatter(values, ("ia", "ka"), scatter_dimension=0, tiled=True)
        return lax.all_gather(values, ("ia", "ka"), axis=0, tiled=True)
    if action == "reduce":
        return lax.psum_scatter(values, ("ia", "ja"), scatter_dimension=0, tiled=True)
    return lax.all_gather(values, ("ia", "ja"), axis=0, tiled=True)


def group_place(mode_now):
    if mode_now == 0:
        return (lax.axis_index(("ja", "ka")), lax.axis_size(("ja", "ka")), lax.axis_size("ia"))
    if mode_now == 1:
        return (lax.axis_index(("ia", "ka")), lax.axis_size(("ia", "ka")), lax.axis_size("ja"))
    return (lax.axis_index(("ia", "ja")), lax.axis_size(("ia", "ja")), lax.axis_size("ka"))


def share_rows(values, group_index, group_size):
    share_width = values.shape[0] // group_size
    return lax.dynamic_slice_in_dim(values, group_index * share_width, share_width, 0)


def starting_gram(values, mode_now):
    group_index, group_size, mode_size = group_place(mode_now)
    share = share_rows(values, group_index, group_size)
    return grand_sum(square_product(share)) / (values.shape[0] * mode_size)


def normalize(stat_rows, count_rows, need_gram):
    squares = lax.psum(jnp.sum(stat_rows * stat_rows, axis=0), ("ia", "ja", "ka")) / count_rows
    scale = lax.rsqrt(squares + EPSILON)
    if not need_gram:
        return (scale, None)
    scaled = stat_rows * scale
    return (scale, grand_sum(square_product(scaled)) / count_rows)


def settle(mode_now, summed, inverse_lower, need_gram):
    group_index, group_size, mode_size = group_place(mode_now)
    count_rows = summed.shape[0] * mode_size
    solved = apply_inverse(inverse_lower, move_rows(mode_now, "reduce", summed))
    scale, gram_new = normalize(solved, count_rows, need_gram)
    return (move_rows(mode_now, "spread", solved * scale), gram_new)


def block_product(mode_now, tensor_block, rows_one, rows_two):
    khatri = (rows_one[:, None, :] * rows_two[None, :, :]).astype(jnp.bfloat16)
    kept_dims = tuple((axis_id for axis_id in range(3) if axis_id != mode_now))
    return lax.dot_general(
        tensor_block, khatri, ((kept_dims, (0, 1)), ((), ())), preferred_element_type=jnp.float32
    )


def local_mttkrp(mode_now, blocks, coords, live_count, factors, bases):
    extents = (BI, BJ, BK)
    spans = (BI * GI_DEV, BJ * GJ_DEV, BK * GK_DEV)
    others = tuple((axis_id for axis_id in range(3) if axis_id != mode_now))

    def visit(slot_index, summed):
        tensor_block = lax.dynamic_index_in_dim(blocks, slot_index, 0, keepdims=False)
        start_one = (coords[others[0], slot_index] - bases[others[0]]) * extents[others[0]]
        start_two = (coords[others[1], slot_index] - bases[others[1]]) * extents[others[1]]
        rows_one = lax.dynamic_slice_in_dim(factors[others[0]], start_one, extents[others[0]], 0)
        rows_two = lax.dynamic_slice_in_dim(factors[others[1]], start_two, extents[others[1]], 0)
        product_rows = block_product(mode_now, tensor_block, rows_one, rows_two)
        offset = (coords[mode_now, slot_index] - bases[mode_now]) * extents[mode_now]
        current = lax.dynamic_slice_in_dim(summed, offset, extents[mode_now], 0)
        return lax.dynamic_update_slice_in_dim(summed, current + product_rows, offset, 0)

    start_rows = jnp.zeros((spans[mode_now], RANK), jnp.float32)
    return lax.fori_loop(0, live_count, visit, start_rows)


def on_device(blocks, coords, live, factor_b, factor_c):
    bases = (
        lax.axis_index("ia") * GI_DEV,
        lax.axis_index("ja") * GJ_DEV,
        lax.axis_index("ka") * GK_DEV,
    )
    factors = [None, factor_b, factor_c]
    gram_list = [None, starting_gram(factor_b, 1), starting_gram(factor_c, 2)]
    for position, mode_now in enumerate(sweep_order):
        others = tuple((axis_id for axis_id in range(3) if axis_id != mode_now))
        summed = local_mttkrp(mode_now, blocks, coords, live[0], factors, bases)
        inverse_lower = factorize(gram_list[others[0]], gram_list[others[1]])
        factors[mode_now], gram_list[mode_now] = settle(
            mode_now, summed, inverse_lower, position < 2
        )
    return (factors[0], factors[1], factors[2])


def solution(mesh):
    placed = (
        P(("ia", "ja", "ka"), None, None, None),
        P(None, ("ia", "ja", "ka")),
        P(("ia", "ja", "ka")),
        P("ja", None),
        P("ka", None),
    )
    return jax.shard_map(
        on_device,
        mesh=mesh,
        in_specs=placed,
        out_specs=(P("ia", None), P("ja", None), P("ka", None)),
        check_vma=False,
    )
```

profile of v0, /device:TPU:8, one launch (start us, length us, event | category | flops | bytes accessed | tf_op | source)
XLA Modules:
  0.0 1530.3 jit_solution(2056919965706999280)
XLA Ops:
  7.2 1.7 fusion.37
  8.9 0.9 fusion.35
  9.9 1.4 fusion.46
  14.1 2.0 fusion.10
  16.1 1.4 while.42
  22.0 241.1 %all-reduce.21.cloned.1.call-done = (f32[128,128]{0,1:T(8,128)}, f32[128,128]{0,1:T(8,128)}) async-done(((f32[128,128]{0,1:T(8,128)}, f32[128,128]{0,1:T(8,128)}), (f32[128,128]{0,1:T(8,128)}, f32[128,128]{0,1:T(8,128)})) %all-reduce.21.cloned.1.call-update) | async-done | bytes 131088 | tf_op jit(solution)/shard_map/psum | solution.py:43
  263.1 1.5 select_reduce_fusion.5
  265.3 0.9 select_add_fusion.2
  266.3 11.7 cholesky.59
  279.3 9.8 custom-call.7
  289.4 117.0 %all-reduce.15.cloned.1.call-done = f32[256,128]{1,0:T(8,128)} async-done(((f32[256,128]{1,0:T(8,128)}), f32[256,128]{1,0:T(8,128)}) %all-reduce.15.cloned.1.call-update) | async-done | bytes 131088
  407.6 73.4 %psum.51 = f32[128]{0:T(128)S(1)} all-reduce(f32[128]{0:T(128)S(1)} %get-tuple-element.553), channel_id=1, replica_groups=mesh['ia'=8,'ja'=8,'ka'=4] {'ia','ja','ka'}, use_global_device_ids=true, to_apply=%region_9.12 | all-reduce | flops 128 | bytes 1024 | tf_op jit(solution)/shard_map/psum | solution.py:80
  481.0 0.9 fusion.47
  481.9 41.7 %all_gather.9 = f32[256,128]{1,0:T(8,128)S(1)} all-gather(f32[8,128]{1,0:T(8,128)S(1)} %broadcast_multiply_fusion.2), channel_id=1, replica_groups=mesh['ia'=8,'ja'=8,'ka'=4] {'ja','ka'}, dimensions={0}, use_global_device_ids=true | all-gather | bytes 135168 | tf_op jit(solution)/shard_map/all_gather | solution.py:50
  524.2 1.3 while.43
  526.5 235.4 %all-reduce.11.cloned.1.call-done = f32[128,128]{0,1:T(8,128)} async-done(((f32[128,128]{0,1:T(8,128)}), f32[128,128]{0,1:T(8,128)}) %all-reduce.11.cloned.1.call-update) | async-done | bytes 65552 | tf_op jit(solution)/shard_map/psum | solution.py:43
  761.9 1.5 select_reduce_fusion.4
  764.0 0.9 select_add_fusion.1
  765.0 11.7 cholesky.70
  778.0 9.8 custom-call.8
  788.1 85.6 %all-reduce.17.cloned.1.call-done = f32[256,128]{1,0:T(8,128)} async-done(((f32[256,128]{1,0:T(8,128)}), f32[256,128]{1,0:T(8,128)}) %all-reduce.17.cloned.1.call-update) | async-done | bytes 131088
  874.8 75.8 %psum.53 = f32[128]{0:T(128)S(1)} all-reduce(f32[128]{0:T(128)S(1)} %get-tuple-element.555), channel_id=1, replica_groups=mesh['ia'=8,'ja'=8,'ka'=4] {'ia','ja','ka'}, use_global_device_ids=true, to_apply=%region_16.19 | all-reduce | flops 128 | bytes 1024 | tf_op jit(solution)/shard_map/psum | solution.py:80
  950.6 0.9 fusion.48
  951.5 32.2 %all_gather.10 = f32[256,128]{1,0:T(8,128)S(1)} all-gather(f32[8,128]{1,0:T(8,128)S(1)} %broadcast_multiply_fusion.1), channel_id=1, replica_groups=mesh['ia'=8,'ja'=8,'ka'=4] {'ia','ka'}, dimensions={0}, use_global_device_ids=true | all-gather | bytes 135168 | tf_op jit(solution)/shard_map/all_gather | solution.py:54
  984.4 1.6 while.44
  986.7 237.7 %all-reduce.13.cloned.1.call-done = f32[128,128]{0,1:T(8,128)} async-done(((f32[128,128]{0,1:T(8,128)}), f32[128,128]{0,1:T(8,128)}) %all-reduce.13.cloned.1.call-update) | async-done | bytes 65552 | tf_op jit(solution)/shard_map/psum | solution.py:43
  1224.3 1.5 select_reduce_fusion.3
  1227.4 11.7 cholesky.81
  1240.5 9.8 custom-call.9
  1250.6 151.4 %all-reduce.19.cloned.1.call-done = f32[512,128]{1,0:T(8,128)} async-done(((f32[512,128]{1,0:T(8,128)}), f32[512,128]{1,0:T(8,128)}) %all-reduce.19.cloned.1.call-update) | async-done | bytes 262160
  1403.1 74.7 %psum.55 = f32[128]{0:T(128)S(1)} all-reduce(f32[128]{0:T(128)S(1)} %get-tuple-element.557), channel_id=1, replica_groups=mesh['ia'=8,'ja'=8,'ka'=4] {'ia','ja','ka'}, use_global_device_ids=true, to_apply=%region_23.26 | all-reduce | flops 128 | bytes 1024 | tf_op jit(solution)/shard_map/psum | solution.py:80
  1477.8 43.7 %all_gather.11 = f32[512,128]{1,0:T(8,128)S(1)} all-gather(f32[8,128]{1,0:T(8,128)S(1)} %broadcast_multiply_fusion), channel_id=1, replica_groups=mesh['ia'=8,'ja'=8,'ka'=4] {'ia','ja'}, dimensions={0}, use_global_device_ids=true | all-gather | bytes 266240 | tf_op jit(solution)/shard_map/all_gather | solution.py:57
  (81 shorter events, 17.5 us)
Async XLA Ops:
  7.2 1.8 copy-start
  7.2 255.9 %all-reduce.21.cloned.1.call-start = ((), (), s32[]{:S(2)}) async-start(), calls=%async_computation.5 | async-start | bytes 262144 | tf_op jit(solution)/shard_map/psum | solution.py:43
  9.9 396.6 %all-reduce.15.cloned.1.call-start = ((), (), s32[]{:S(2)}) async-start(), calls=%async_computation.2 | async-start | bytes 262144
  14.0 4.2 copy-start.9
  14.0 4.9 copy-start.8
  14.1 6.7 copy-start.7
  16.1 507.6 %copy-start.6 = (bf16[1,64,64,128]{3,2,1,0:T(8,128)(2,1)S(1)}, bf16[1,64,64,128]{3,2,1,0:T(8,128)(2,1)}, u32[]{:S(2)}) copy-start(bf16[1,64,64,128]{3,2,1,0:T(8,128)(2,1)} %param.14) | copy-start | bytes 3145732
  17.5 0.7 copy-start.2
  18.2 743.6 %all-reduce.11.cloned.1.call-start = ((), (), s32[]{:S(2)}) async-start(), calls=%async_computation | async-start | bytes 131072 | tf_op jit(solution)/shard_map/psum | solution.py:43
  523.6 350.1 %all-reduce.17.cloned.1.call-start = ((), (), s32[]{:S(2)}) async-start(), calls=%async_computation.3 | async-start | bytes 262144
  523.7 238.2 %copy-start.4 = (f32[128,128]{0,1:T(8,128)S(1)}, f32[128,128]{0,1:T(8,128)}, u32[]{:S(2)}) copy-start(f32[128,128]{0,1:T(8,128)} %get-tuple-element.548) | copy-start | bytes 196612
  525.5 0.7 copy-start.3
  526.2 698.1 %all-reduce.13.cloned.1.call-start = ((), (), s32[]{:S(2)}) async-start(), calls=%async_computation.1 | async-start | bytes 131072 | tf_op jit(solution)/shard_map/psum | solution.py:43
  983.7 418.3 %all-reduce.19.cloned.1.call-start = ((), (), s32[]{:S(2)}) async-start(), calls=%async_computation.4 | async-start | bytes 524288
  984.3 240.0 %copy-start.5 = (f32[128,128]{0,1:T(8,128)S(1)}, f32[128,128]{0,1:T(8,128)}, u32[]{:S(2)}) copy-start(f32[128,128]{0,1:T(8,128)} %all-reduce.11.cloned.1.call-done) | copy-start | bytes 196612
  985.9 0.7 copy-start.1
Sparse Core Ops, SparseCore 0:
  14.2 248.9 all-reduce.20
  267.1 139.2 all-reduce.14
  523.7 238.0 all-reduce.10
  765.5 108.1 all-reduce.16
  983.9 240.4 all-reduce.12
  1228.2 173.7 all-reduce.18
where the time goes:
time: 1530 us
  waiting for transfers between devices  1070 us (70%)
  blocking collectives  341 us (22%)
  other arithmetic  75.7 us (5%)
  between operations  20.2 us (1%)
    psum x3, waiting for transfers between devices, grand_sum(): return lax.psum(values, ('ia', 'ja', 'ka'))  714 us
    unnamed x9, waiting for transfers between devices  354 us
    psum x3, blocking collectives, normalize(): lax.psum(jnp.sum(stat_rows * stat_rows, axis=0), ('ia', 'ja', 'ka'))  224 us
    all_gather x1, blocking collectives, move_rows(): return lax.all_gather(values, ('ia', 'ja'), axis=0, tiled=True)  43.7 us
    all_gather x1, blocking collectives, move_rows(): return lax.all_gather(values, ('ja', 'ka'), axis=0, tiled=True)  41.7 us
    another operation x9, other arithmetic, factorize(): jnp.linalg.cholesky(merged + shift_value * jnp.eye(order_rank, dtype=jnp....  37.2 us
    all_gather x1, blocking collectives, move_rows(): return lax.all_gather(values, ('ia', 'ka'), axis=0, tiled=True)  32.2 us
    another operation x6, other arithmetic, factorize(): lax.linalg.triangular_solve(lower_factor, jnp.eye(order_rank, dtype=jnp.f...  31.4 us
  transfers between devices with their start and end apart: 6, of which 6 were waited for; matrix products, arithmetic and copies ran while one was open for 5% of the time, Pallas kernels for 0%

commit v1 on v0

v1 whole, which is shorter than its diff:
```python
import jax
import jax.numpy as jnp
from jax import lax
from jax.sharding import PartitionSpec as P

RANK = 128
BI = 64
BJ = 64
BK = 128
GI_DEV = 4
GJ_DEV = 4
GK_DEV = 4
SLOTS = 4

RIDGE_SHARE = 0.3
EPSILON = 1e-06
HIGHEST = lax.Precision.HIGHEST


def factorize(merged):
    order_rank = merged.shape[0]
    shift_value = RIDGE_SHARE * jnp.trace(merged) / order_rank
    lower_factor = jnp.linalg.cholesky(
        merged + shift_value * jnp.eye(order_rank, dtype=jnp.float32)
    )
    return lax.linalg.triangular_solve(
        lower_factor, jnp.eye(order_rank, dtype=jnp.float32), left_side=True, lower=True
    )


def exact_dot(left, right):
    return jnp.dot(left, right, precision=HIGHEST, preferred_element_type=jnp.float32)


def apply_inverse(inverse_lower, values):
    return exact_dot(exact_dot(values, inverse_lower.T), inverse_lower)


def gram(rows):
    return exact_dot(rows.T, rows)


def block_product(mode_now, tensor_block, rows_one, rows_two, split):
    product = rows_one[:, None, :] * rows_two[None, :, :]
    kept = tuple(axis_id for axis_id in range(3) if axis_id != mode_now)
    dims = ((kept, (0, 1)), ((), ()))
    high = product.astype(jnp.bfloat16)
    total = lax.dot_general(tensor_block, high, dims, preferred_element_type=jnp.float32)
    if split:
        low = (product - high.astype(jnp.float32)).astype(jnp.bfloat16)
        total = total + lax.dot_general(
            tensor_block, low, dims, preferred_element_type=jnp.float32
        )
    return total


def exchange(values, axes):
    return lax.all_to_all(values, axes, 0, 0, tiled=True)


def scatter_sum(parts, slot_ids):
    rows = []
    for slot in range(SLOTS):
        picked = jnp.where((slot_ids == slot)[:, None, None], parts, 0.0)
        rows.append(jnp.sum(picked, axis=0))
    return jnp.concatenate(rows, axis=0)


def reduce_rows(axes, count, partial, slot, extras):
    pieces = [partial.reshape(count, 2, RANK)]
    pieces += [extra.reshape(count, -1, RANK) for extra in extras]
    pieces.append(jnp.full((count, 1, RANK), slot.astype(jnp.float32)))
    used = sum(piece.shape[1] for piece in pieces)
    if used % 8:
        pieces.append(jnp.zeros((count, 8 - used % 8, RANK), jnp.float32))
    got = exchange(jnp.concatenate(pieces, axis=1), axes)
    slot_ids = got[:, used - 1, 0].astype(jnp.int32)
    own = scatter_sum(got[:, 0:2], slot_ids)
    sums = jnp.sum(got[:, 2 : used - 1], axis=0)
    return own, sums


def spread_rows(axes, count, own):
    return exchange(jnp.broadcast_to(own[None], (count,) + own.shape), axes)


def in_order(rows):
    count = rows.shape[0]
    return rows.reshape(count, SLOTS, 2, RANK).transpose(1, 0, 2, 3).reshape(-1, RANK)


def slot_rows(rows, slot):
    count = rows.shape[0]
    return lax.dynamic_slice_in_dim(rows, slot * 2, 2, 1).reshape(count * 2, RANK)


def on_device(blocks, coords, live, factor_b, factor_c):
    at_i, at_j, at_k = (lax.axis_index(name) for name in ("ia", "ja", "ka"))
    slot_i = coords[0, 0] - at_i * GI_DEV
    slot_j = coords[1, 0] - at_j * GJ_DEV
    slot_k = coords[2, 0] - at_k * GK_DEV
    block = blocks[0]
    eye = jnp.eye(RANK, dtype=jnp.float32)
    upper = jnp.triu(jnp.ones((RANK, RANK), jnp.bool_))

    rows_b = lax.dynamic_slice_in_dim(factor_b, slot_j * BJ, BJ, 0)
    rows_c = lax.dynamic_slice_in_dim(factor_c, slot_k * BK, BK, 0)
    partial = block_product(0, block, rows_b, rows_c, False)
    part_b = gram(lax.dynamic_slice_in_dim(factor_b, at_k * 64, 64, 0)) / 2048
    part_c = gram(lax.dynamic_slice_in_dim(factor_c, at_j * 64, 64, 0)) / 2048
    packed = jnp.where(upper, part_b, part_c)
    diagonal = jnp.sum(part_c * eye, axis=0)
    own, sums = reduce_rows(
        ("ja", "ka"), 32, partial, slot_i, [packed, jnp.tile(diagonal[None], (32, 1))]
    )
    got = spread_rows(("ja", "ka"), 32, jnp.concatenate([own, sums[0:4]], axis=0))
    packed = got[:, 8:12].reshape(RANK, RANK)
    strict = jnp.logical_and(upper, eye == 0.0)
    gram_b = jnp.where(upper, packed, packed.T)
    gram_c = jnp.where(strict, packed.T, jnp.where(upper, sums[4][None, :] * eye, packed))
    inverse_lower = factorize(gram_b * gram_c)
    solved_a = apply_inverse(inverse_lower, got[:, 0:8].reshape(256, RANK)).reshape(32, 8, RANK)
    own_a = slot_rows(solved_a, slot_i)

    partial = block_product(1, block, own_a, rows_c, True)
    share = lax.dynamic_slice_in_dim(solved_a, at_k * 8, 8, 0).reshape(64, RANK)
    own, sums = reduce_rows(("ia", "ka"), 32, partial, slot_j, [gram(share)])
    got = spread_rows(("ia", "ka"), 32, jnp.concatenate([own, sums], axis=0))
    raw = got[:, 8:12].reshape(RANK, RANK) / 2048
    scale_a = lax.rsqrt(jnp.sum(raw * eye, axis=0) + EPSILON)
    gram_a = raw * scale_a[:, None] * scale_a[None, :]
    inverse_lower = factorize(gram_a * gram_c)
    solved_b = apply_inverse(
        inverse_lower, got[:, 0:8].reshape(256, RANK) * scale_a
    ).reshape(32, 8, RANK)
    own_b = slot_rows(solved_b, slot_j)

    partial = block_product(2, block, own_a * scale_a, own_b, True)
    share = lax.dynamic_slice_in_dim(solved_b, at_i * 4, 4, 0).reshape(32, RANK)
    own, sums = reduce_rows(("ia", "ja"), 64, partial, slot_k, [gram(share)])
    got = spread_rows(("ia", "ja"), 64, jnp.concatenate([own, sums], axis=0))
    raw = got[:, 8:10].reshape(RANK, RANK) / 2048
    scale_b = lax.rsqrt(jnp.sum(raw * eye, axis=0) + EPSILON)
    gram_b = raw * scale_b[:, None] * scale_b[None, :]
    inverse_lower = factorize(gram_a * gram_b)
    solved_c = apply_inverse(inverse_lower, got[:, 0:8].reshape(512, RANK) * scale_b)
    squares = jnp.sum(solved_c * solved_c, axis=0, keepdims=True)
    total = squares
    for step in (1, 2, 3):
        total = total + lax.ppermute(squares, "ka", [(n, (n + step) % 4) for n in range(4)])
    scale_c = lax.rsqrt(total / 2048 + EPSILON)

    loading_a = in_order(solved_a * scale_a)
    loading_b = in_order(solved_b * scale_b)
    loading_c = in_order((solved_c * scale_c).reshape(64, 8, RANK))
    return (loading_a, loading_b, loading_c)


def solution(mesh):
    placed = (
        P(("ia", "ja", "ka"), None, None, None),
        P(None, ("ia", "ja", "ka")),
        P(("ia", "ja", "ka")),
        P("ja", None),
        P("ka", None),
    )
    return jax.shard_map(
        on_device,
        mesh=mesh,
        in_specs=placed,
        out_specs=(P("ia", None), P("ja", None), P("ka", None)),
        check_vma=False,
    )
```

time: 1530 us -> 218 us (0.14)
  waiting for transfers between devices: 1070 us -> 38.2 us
  blocking collectives: 341 us -> 51.4 us
  starting transfers between devices: 0.43 us -> 19.4 us
    psum x3 -> x0, waiting for transfers between devices: 714 us -> none  [grand_sum(): return lax.psum(values, ('ia', 'ja', 'ka'))]
    unnamed x9 -> x0, waiting for transfers between devices: 354 us -> none
    psum x3 -> x0, blocking collectives: 224 us -> none  [normalize(): lax.psum(jnp.sum(stat_rows * stat_rows, axis=0), ('ia', 'ja', 'ka'))]
    all_gather x3 -> x0, blocking collectives: 118 us -> none  [the longest x1 43.7 us: move_rows(): return lax.all_gather(values, ('ia', 'ja'), axis=0, tiled=True)]
    all_to_all x0 -> x3, blocking collectives: none -> 51.4 us  [exchange(): return lax.all_to_all(values, axes, 0, 0, tiled=True)]
    all_to_all x0 -> x3, waiting for transfers between devices: none -> 36.3 us  [exchange(): return lax.all_to_all(values, axes, 0, 0, tiled=True)]
  transfers between devices with their start and end apart: 6 -> 6, of which waited for: 6 -> 5; matrix products, arithmetic and copies ran while one was open for 5% -> 1% of each run, Pallas kernels for 0% -> 0%
where the time goes in v1:
time: 218 us; the launch traced here: 214 us
  other arithmetic  81.9 us (38%)
  blocking collectives  51.4 us (24%)
  waiting for transfers between devices  38.2 us (18%)
  starting transfers between devices  19.4 us (9%)
  matrix products  8.77 us (4%)
  local copies, waits for them, and re-layouts  8.33 us (4%)
  between operations  5.54 us (3%)
    all_to_all x3, blocking collectives, exchange(): return lax.all_to_all(values, axes, 0, 0, tiled=True)  51.4 us
    another operation x9, other arithmetic, factorize(): jnp.linalg.cholesky(merged + shift_value * jnp.eye(order_rank, dtype=jnp....  37.2 us
    all_to_all x3, waiting for transfers between devices, exchange(): return lax.all_to_all(values, axes, 0, 0, tiled=True)  36.3 us
    another operation x6, other arithmetic, factorize(): lax.linalg.triangular_solve(lower_factor, jnp.eye(order_rank, dtype=jnp.f...  31.4 us
    all_to_all x3, starting transfers between devices, exchange(): return lax.all_to_all(values, axes, 0, 0, tiled=True)  15.2 us
    eq x3, other arithmetic, scatter_sum(): picked = jnp.where((slot_ids == slot)[:, None, None], parts, 0.0)  9.38 us
  transfers between devices with their start and end apart: 6, of which 5 were waited for; matrix products, arithmetic and copies ran while one was open for 1% of the time, Pallas kernels for 0%

profile of v1, /device:TPU:8, one launch (start us, length us, event | category | flops | bytes accessed | tf_op | source)
XLA Modules:
  0.0 213.6 jit_solution(9409927189555439326)
XLA Ops:
  0.7 1.4 fusion.76
  3.7 0.8 constant_dynamic-slice_fusion.3
  4.5 1.1 fusion.15
  6.5 2.0 fusion.3
  8.6 21.6 %all_to_all.30 = f32[32,8,128]{2,1,0:T(8,128)S(1)} all-to-all(f32[32,8,128]{2,1,0:T(8,128)S(1)} %maximum_maximum_fusion.1), channel_id=1, replica_groups=mesh['ia'=8,'ja'=8,'ka'=4] {'ja','ka'}, dimensions={0} | all-to-all | bytes 262144 | tf_op jit(solution)/shard_map/all_to_all | solution.py:58
  30.2 2.4 %compare_reduce_fusion.8 = (pred[32]{0:T(512)(128)(4,1)S(1)}, pred[32]{0:T(512)(128)(4,1)S(1)}, pred[32]{0:T(512)(128)(4,1)S(1)}, pred[32]{0:T(512)(128)(4,1)S(1)}) fusion(f32[32,8,128]{2,1,0:T(8,128)S(1)} %all_to_all.30), kind=kLoop, calls=%fused_computation.113 | loop fusion | flops 160 | bytes 256 | tf_op jit(solution)/shard_map/eq | solution.py:64
  32.8 0.7 broadcast_in_dim.187
  33.5 4.0 %all-to-all-start.1 = ((f32[32,12,128]{2,1,0:T(8,128)}), f32[32,12,128]{2,1,0:T(8,128)S(1)}, u32[]{:S(2)}, u32[]{:S(2)}) async-start(f32[32,12,128]{2,1,0:T(8,128)} %broadcast_in_dim.187), calls=%async_computation.1 | async-start | bytes 524288 | tf_op jit(solution)/shard_map/all_to_all | solution.py:58
  37.8 11.8 %all-to-all-done.1 = f32[32,12,128]{2,1,0:T(8,128)S(1)} async-done(((f32[32,12,128]{2,1,0:T(8,128)}), f32[32,12,128]{2,1,0:T(8,128)S(1)}, u32[]{:S(2)}, u32[]{:S(2)}) %all-to-all-start.1) | async-done | bytes 196640 | tf_op jit(solution)/shard_map/all_to_all | solution.py:58
  51.3 11.7 %cholesky.59 = f32[128,128]{1,0:T(8,128)S(1)} custom-call(f32[128,128]{1,0:T(8,128)S(1)} %fusion.50), custom_call_target="Cholesky" | custom-call | tf_op jit(solution)/shard_map/jit(cholesky)/cholesky | solution.py:23
  64.3 9.8 %custom-call.7 = f32[1,128,128]{1,2,0:T(8,128)S(1)} custom-call(f32[1,128,128]{2,1,0:T(8,128)S(1)} %fusion.41), custom_call_target="InvertDiagBlocksLowerTriangular" | custom-call | tf_op jit(solution)/shard_map/triangular_solve/custom-call.0 | solution.py:26
  76.6 12.2 %all_to_all.31 = f32[32,8,128]{2,1,0:T(8,128)S(1)} all-to-all(f32[32,8,128]{2,1,0:T(8,128)S(1)} %copy.80), channel_id=1, replica_groups=mesh['ia'=8,'ja'=8,'ka'=4] {'ia','ka'}, dimensions={0} | all-to-all | bytes 262144 | tf_op jit(solution)/shard_map/all_to_all | solution.py:58
  88.8 2.4 %compare_reduce_fusion.4 = (pred[32]{0:T(512)(128)(4,1)S(1)}, pred[32]{0:T(512)(128)(4,1)S(1)}, pred[32]{0:T(512)(128)(4,1)S(1)}, pred[32]{0:T(512)(128)(4,1)S(1)}) fusion(f32[32,8,128]{2,1,0:T(8,128)S(1)} %all_to_all.31), kind=kLoop, calls=%fused_computation.109 | loop fusion | flops 160 | bytes 256 | tf_op jit(solution)/shard_map/eq | solution.py:64
  91.5 0.7 broadcast_in_dim.198
  92.2 5.5 %all-to-all-start.3 = ((f32[32,12,128]{2,1,0:T(8,128)}), f32[32,12,128]{2,1,0:T(8,128)S(1)}, u32[]{:S(2)}, u32[]{:S(2)}) async-start(f32[32,12,128]{2,1,0:T(8,128)} %broadcast_in_dim.198), calls=%async_computation.3 | async-start | bytes 524288 | tf_op jit(solution)/shard_map/all_to_all | solution.py:58
  97.8 7.4 %all-to-all-done.3 = f32[32,12,128]{2,1,0:T(8,128)S(1)} async-done(((f32[32,12,128]{2,1,0:T(8,128)}), f32[32,12,128]{2,1,0:T(8,128)S(1)}, u32[]{:S(2)}, u32[]{:S(2)}) %all-to-all-start.3) | async-done | bytes 196640 | tf_op jit(solution)/shard_map/all_to_all | solution.py:58
  105.5 0.7 select_reduce_fusion.8
  107.0 11.7 %cholesky.70 = f32[128,128]{1,0:T(8,128)S(1)} custom-call(f32[128,128]{1,0:T(8,128)S(1)} %fusion.48), custom_call_target="Cholesky" | custom-call | tf_op jit(solution)/shard_map/jit(cholesky)/cholesky | solution.py:23
  120.0 9.8 %custom-call.8 = f32[1,128,128]{1,2,0:T(8,128)S(1)} custom-call(f32[1,128,128]{2,1,0:T(8,128)S(1)} %fusion.42), custom_call_target="InvertDiagBlocksLowerTriangular" | custom-call | tf_op jit(solution)/shard_map/triangular_solve/custom-call.0 | solution.py:26
  132.3 17.7 %all_to_all.32 = f32[64,8,128]{2,1,0:T(8,128)S(1)} all-to-all(f32[64,8,128]{2,1,0:T(8,128)S(1)} %maximum_maximum_fusion), channel_id=1, replica_groups=mesh['ia'=8,'ja'=8,'ka'=4] {'ia','ja'}, dimensions={0} | all-to-all | bytes 524288 | tf_op jit(solution)/shard_map/all_to_all | solution.py:58
  150.0 4.6 %compare_reduce_fusion = (pred[64]{0:T(512)(128)(4,1)S(1)}, pred[64]{0:T(512)(128)(4,1)S(1)}, pred[64]{0:T(512)(128)(4,1)S(1)}, pred[64]{0:T(512)(128)(4,1)S(1)}) fusion(f32[64,8,128]{2,1,0:T(8,128)S(1)} %all_to_all.32), kind=kLoop, calls=%fused_computation.55 | loop fusion | flops 320 | bytes 512 | tf_op jit(solution)/shard_map/eq | solution.py:64
  155.1 0.8 broadcast_in_dim.210
  155.9 5.7 %all-to-all-start.5 = ((f32[64,10,128]{2,1,0:T(8,128)}), f32[64,10,128]{2,1,0:T(8,128)S(1)}, u32[]{:S(2)}, u32[]{:S(2)}) async-start(f32[64,10,128]{2,1,0:T(8,128)} %broadcast_in_dim.210), calls=%async_computation.5 | async-start | bytes 1048576 | tf_op jit(solution)/shard_map/all_to_all | solution.py:58
  162.5 17.1 %all-to-all-done.5 = f32[64,10,128]{2,1,0:T(8,128)S(1)} async-done(((f32[64,10,128]{2,1,0:T(8,128)}), f32[64,10,128]{2,1,0:T(8,128)S(1)}, u32[]{:S(2)}, u32[]{:S(2)}) %all-to-all-start.5) | async-done | bytes 327712 | tf_op jit(solution)/shard_map/all_to_all | solution.py:58
  179.8 0.8 select_reduce_fusion.3
  181.6 11.7 %cholesky.81 = f32[128,128]{1,0:T(8,128)S(1)} custom-call(f32[128,128]{1,0:T(8,128)S(1)} %fusion.46), custom_call_target="Cholesky" | custom-call | tf_op jit(solution)/shard_map/jit(cholesky)/cholesky | solution.py:23
  194.6 9.8 %custom-call.9 = f32[1,128,128]{1,2,0:T(8,128)S(1)} custom-call(f32[1,128,128]{2,1,0:T(8,128)S(1)} %fusion.43), custom_call_target="InvertDiagBlocksLowerTriangular" | custom-call | tf_op jit(solution)/shard_map/triangular_solve/custom-call.0 | solution.py:26
  206.1 2.6 %collective-permute-start.1 = (f32[1,128]{1,0:T(1,128)S(1)}, f32[1,128]{1,0:T(1,128)S(1)}, u32[]{:S(2)}, u32[]{:S(2)}) collective-permute-start(f32[1,128]{1,0:T(1,128)S(1)} %bitcast.166), channel_id=1, source_target_pairs={{0,2},{1,3},{2,0},{3,1},{4,6},{5,7},{6,4},{7,5},{8,10},{9,11},{10,... | collective-permute-start | bytes 1544 | tf_op jit(solution)/shard_map/ppermute | solution.py:150
  208.7 0.9 collective-permute-start.2
  210.4 0.8 collective-permute-done.1
  211.2 1.1 collective-permute-done.2
  212.3 0.8 copy.90
  (92 shorter events, 15.9 us)
Async XLA Ops:
  0.6 2.7 %copy-start = (f32[512,128]{1,0:T(8,128)S(1)}, f32[512,128]{1,0:T(8,128)}, u32[]{:S(2)}) copy-start(f32[512,128]{1,0:T(8,128)} %param.11) | copy-start | bytes 786436
  33.5 16.1 %all-to-all-start.1 = ((f32[32,12,128]{2,1,0:T(8,128)}), f32[32,12,128]{2,1,0:T(8,128)S(1)}, u32[]{:S(2)}, u32[]{:S(2)}) async-start(f32[32,12,128]{2,1,0:T(8,128)} %broadcast_in_dim.187), calls=%async_computation.1 | async-start | bytes 524288 | tf_op jit(solution)/shard_map/all_to_all | solution.py:58
  37.6 37.4 %copy-start.1 = (bf16[1,64,64,128]{3,2,1,0:T(8,128)(2,1)S(1)}, bf16[1,64,64,128]{3,2,1,0:T(8,128)(2,1)}, u32[]{:S(2)}) copy-start(bf16[1,64,64,128]{3,2,1,0:T(8,128)(2,1)} %param.8) | copy-start | bytes 3145732
  92.2 13.1 %all-to-all-start.3 = ((f32[32,12,128]{2,1,0:T(8,128)}), f32[32,12,128]{2,1,0:T(8,128)S(1)}, u32[]{:S(2)}, u32[]{:S(2)}) async-start(f32[32,12,128]{2,1,0:T(8,128)} %broadcast_in_dim.198), calls=%async_computation.3 | async-start | bytes 524288 | tf_op jit(solution)/shard_map/all_to_all | solution.py:58
  155.9 23.7 %all-to-all-start.5 = ((f32[64,10,128]{2,1,0:T(8,128)}), f32[64,10,128]{2,1,0:T(8,128)S(1)}, u32[]{:S(2)}, u32[]{:S(2)}) async-start(f32[64,10,128]{2,1,0:T(8,128)} %broadcast_in_dim.210), calls=%async_computation.5 | async-start | bytes 1048576 | tf_op jit(solution)/shard_map/all_to_all | solution.py:58
  205.5 4.9 %collective-permute-start = (f32[1,128]{1,0:T(1,128)S(1)}, f32[1,128]{1,0:T(1,128)S(1)}, u32[]{:S(2)}, u32[]{:S(2)}) collective-permute-start(f32[1,128]{1,0:T(1,128)S(1)} %bitcast.165), channel_id=1, source_target_pairs={{0,1},{1,2},{2,3},{3,0},{4,5},{5,6},{6,7},{7,4},{8,9},{9,10},{10,1... | collective-permute-start | bytes 1544 | tf_op jit(solution)/shard_map/ppermute | solution.py:150
  206.1 5.1 %collective-permute-start.1 = (f32[1,128]{1,0:T(1,128)S(1)}, f32[1,128]{1,0:T(1,128)S(1)}, u32[]{:S(2)}, u32[]{:S(2)}) collective-permute-start(f32[1,128]{1,0:T(1,128)S(1)} %bitcast.166), channel_id=1, source_target_pairs={{0,2},{1,3},{2,0},{3,1},{4,6},{5,7},{6,4},{7,5},{8,10},{9,11},{10,... | collective-permute-start | bytes 1544 | tf_op jit(solution)/shard_map/ppermute | solution.py:150
  208.7 3.6 %collective-permute-start.2 = (f32[1,128]{1,0:T(1,128)S(1)}, f32[1,128]{1,0:T(1,128)S(1)}, u32[]{:S(2)}, u32[]{:S(2)}) collective-permute-start(f32[1,128]{1,0:T(1,128)S(1)} %bitcast.167), channel_id=1, source_target_pairs={{0,3},{1,0},{2,1},{3,2},{4,7},{5,4},{6,5},{7,6},{8,11},{9,8},{10,9... | collective-permute-start | bytes 1544 | tf_op jit(solution)/shard_map/ppermute | solution.py:150

commit v2 on v0

v2 whole, which is shorter than its diff:
```python
import functools

import jax
import jax.numpy as jnp
from jax import lax
from jax.experimental import pallas as pl
from jax.experimental.pallas import tpu as pltpu
from jax.sharding import PartitionSpec as P

RANK = 128
BI = 64
BJ = 64
BK = 128
GI_DEV = 4
GJ_DEV = 4
GK_DEV = 4
SLOTS = 4
ROWS = 2048

RIDGE_SHARE = 0.3
EPSILON = 1e-06
HIGHEST = lax.Precision.HIGHEST
F32 = jnp.float32
BF16 = jnp.bfloat16


def exact_dot(left, right):
    return jnp.dot(left, right, precision=HIGHEST, preferred_element_type=F32)


def gram(rows):
    return lax.dot_general(
        rows, rows, (((0,), (0,)), ((), ())), precision=HIGHEST, preferred_element_type=F32
    )


def halves(values):
    high = values.astype(BF16)
    return high, (values - high.astype(F32)).astype(BF16)


def iotas():
    shape = (RANK, RANK)
    return lax.broadcasted_iota(jnp.int32, shape, 0), lax.broadcasted_iota(jnp.int32, shape, 1)


def inverse(matrix):
    count = RANK // 8
    rows = [matrix[8 * n : 8 * n + 8, :] for n in range(count)]
    lane = lax.broadcasted_iota(jnp.int32, (8, RANK), 1)
    sub = lax.broadcasted_iota(jnp.int32, (8, RANK), 0)

    def over_lanes(tile, at):
        return jnp.broadcast_to(tile[:, at : at + 1], (8, RANK))

    def over_rows(tile, at):
        return jnp.broadcast_to(tile[at : at + 1, :], (8, RANK))

    for k in range(count):
        panel = rows[k]
        columns = [over_lanes(panel, 8 * k + t) for t in range(8)]
        inside = (lane >= 8 * k) & (lane < 8 * k + 8)
        panel = jnp.where(inside, jnp.where(lane - 8 * k == sub, 1.0, 0.0), panel)
        for s in range(8):
            pivot = 1.0 / over_rows(columns[s], s)
            factor = columns[s]
            lead = over_rows(panel, s) * pivot
            panel = jnp.where(sub == s, lead, panel - factor * lead)
            for t in range(s + 1, 8):
                lead = over_rows(columns[t], s) * pivot
                columns[t] = jnp.where(sub == s, lead, columns[t] - factor * lead)
        leads = [over_rows(panel, s) for s in range(8)]
        for step in range(count - 1):
            n = (k + 1 + step) % count
            terms = [over_lanes(rows[n], 8 * k + s) * leads[s] for s in range(8)]
            while len(terms) > 1:
                terms = [terms[i] + terms[i + 1] for i in range(0, len(terms), 2)]
            rows[n] = jnp.where(inside, 0.0, rows[n]) - terms[0]
        rows[k] = panel
    return jnp.concatenate(rows, axis=0)


def system_inverse(merged):
    row, col = iotas()
    shift = jnp.sum(jnp.where(row == col, merged, 0.0)) * (RIDGE_SHARE / RANK)
    return inverse(merged + jnp.where(row == col, shift, 0.0))


def strided(ref, start, count, step):
    return ref[pl.ds(start, count, stride=step), :]


def put(ref, start, count, step, value):
    ref[pl.ds(start, count, stride=step), :] = value


def scaled_gram(raw):
    row, col = iotas()
    diagonal = jnp.where(row == col, raw, 0.0)
    across = lax.rsqrt(jnp.sum(diagonal, axis=0, keepdims=True) + EPSILON)
    down = lax.rsqrt(jnp.sum(diagonal, axis=1, keepdims=True) + EPSILON)
    return across, raw * down * across


def places(coords_ref):
    at = [lax.axis_index(name) for name in ("ia", "ja", "ka")]
    return at, [coords_ref[n, 0] - 4 * at[n] for n in range(3)]


def some_rows(ref, index, size):
    return ref[pl.ds(pl.multiple_of(index * size, size), size), :]


def first_kernel(coords_ref, block_ref, b_ref, c_ref, chunk_ref, y_ref):
    at, slot = places(coords_ref)
    high, low = halves(some_rows(c_ref, slot[2], BK))
    block = block_ref[...].reshape(BI * BJ, BK)
    y_ref[...] = jnp.dot(
        jnp.concatenate([block, block], axis=1),
        jnp.concatenate([high, low], axis=0),
        preferred_element_type=F32,
    ).reshape(BI, BJ, RANK)
    rows_b = some_rows(b_ref, slot[1], BJ)
    partial = jnp.concatenate(
        [jnp.sum(y_ref[n] * rows_b, axis=0, keepdims=True) for n in range(BI)], axis=0
    )
    part_b = gram(some_rows(b_ref, at[2], 64)) * (1.0 / ROWS)
    part_c = gram(some_rows(c_ref, at[1], 64)) * (1.0 / ROWS)
    row, col = iotas()
    packed = jnp.where(row <= col, part_b, part_c)
    diagonal = jnp.sum(jnp.where(row == col, part_c, 0.0), axis=0, keepdims=True)
    for t in range(2):
        put(chunk_ref, t, 32, 8, partial[32 * t : 32 * t + 32])
    for t in range(4):
        put(chunk_ref, 2 + t, 32, 8, packed[32 * t : 32 * t + 32])
    put(chunk_ref, 6, 32, 8, jnp.broadcast_to(diagonal, (32, RANK)))
    put(chunk_ref, 7, 32, 8, jnp.full((32, RANK), slot[0].astype(F32)))


def collect(got_ref, count, extras):
    ids = strided(got_ref, 7, count, 8)
    rows = []
    for slot in range(SLOTS):
        for t in range(2):
            picked = jnp.where(ids == slot, strided(got_ref, t, count, 8), 0.0)
            rows.append(jnp.sum(picked, axis=0, keepdims=True))
    for t in range(extras):
        rows.append(jnp.sum(strided(got_ref, 2 + t, count, 8), axis=0, keepdims=True))
    return rows


def repeat_rows(ref, rows, copies):
    width = len(rows)
    unit = 1
    while width * unit % 8:
        unit *= 2
    tile = jnp.concatenate(rows * unit, axis=0)
    for n in range(copies // unit):
        ref[n * width * unit : (n + 1) * width * unit, :] = tile


def collect_first_kernel(got_ref, spread_ref, diagonal_ref):
    rows = collect(got_ref, 32, 5)
    repeat_rows(spread_ref, rows[:12], 32)
    diagonal_ref[...] = jnp.broadcast_to(rows[12], (8, RANK))


def collect_kernel(count, extras, got_ref, spread_ref):
    repeat_rows(spread_ref, collect(got_ref, count, extras), count)


def natural(got_ref, count, step, first, last):
    return jnp.concatenate([strided(got_ref, t, count, step) for t in range(first, last)], axis=0)


def second_kernel(coords_ref, got_ref, diagonal_ref, y_ref, solved_ref, chunk_ref, gram_c_ref):
    at, slot = places(coords_ref)
    packed = natural(got_ref, 32, 12, 8, 12)
    flipped = packed.T
    row, col = iotas()
    gram_b = jnp.where(row <= col, packed, flipped)
    gram_c = jnp.where(row < col, flipped, packed)
    gram_c = jnp.where(row == col, diagonal_ref[0:1, :], gram_c)
    gram_c_ref[...] = gram_c
    solver = system_inverse(gram_b * gram_c)
    solved_ref[...] = exact_dot(natural(got_ref, 32, 12, 0, 8), solver)
    raw = gram(some_rows(solved_ref, at[2], 64)) * (1.0 / ROWS)
    own = some_rows(solved_ref, slot[0], BI)
    sums = [jnp.zeros((BJ, RANK), F32) for _ in range(2)]
    for n in range(BI):
        sums[n % 2] = sums[n % 2] + own[n : n + 1, :] * y_ref[n]
    partial = sums[0] + sums[1]
    for t in range(2):
        put(chunk_ref, t, 32, 8, partial[32 * t : 32 * t + 32])
    for t in range(4):
        put(chunk_ref, 2 + t, 32, 8, raw[32 * t : 32 * t + 32])
    put(chunk_ref, 6, 32, 8, jnp.zeros((32, RANK), F32))
    put(chunk_ref, 7, 32, 8, jnp.full((32, RANK), slot[1].astype(F32)))


def third_kernel(
    coords_ref, got_ref, gram_c_ref, solved_a_ref, block_ref,
    loading_a_ref, solved_ref, chunk_ref, gram_a_ref, khatri_ref,
):
    at, slot = places(coords_ref)
    scale, gram_a = scaled_gram(natural(got_ref, 32, 12, 8, 12))
    gram_a_ref[...] = gram_a
    loading_a_ref[...] = solved_a_ref[...] * scale
    solver = system_inverse(gram_a * gram_c_ref[...])
    solved_ref[...] = exact_dot(natural(got_ref, 32, 12, 0, 8) * scale, solver)
    raw = gram(some_rows(solved_ref, at[0], 32)) * (1.0 / ROWS)
    own_a = some_rows(loading_a_ref, slot[0], BI)
    own_b = some_rows(solved_ref, slot[1], BJ)
    for n in range(BI):
        khatri_ref[n * BJ : (n + 1) * BJ, :] = (own_a[n : n + 1, :] * own_b).astype(BF16)
    partial = lax.dot_general(
        block_ref[...].reshape(BI * BJ, BK),
        khatri_ref[...],
        (((0,), (0,)), ((), ())),
        preferred_element_type=F32,
    )
    for t in range(2):
        put(chunk_ref, t, 64, 8, partial[64 * t : 64 * t + 64])
    for t in range(2):
        put(chunk_ref, 2 + t, 64, 8, raw[64 * t : 64 * t + 64])
    for t in range(4, 7):
        put(chunk_ref, t, 64, 8, jnp.zeros((64, RANK), F32))
    put(chunk_ref, 7, 64, 8, jnp.full((64, RANK), slot[2].astype(F32)))


def fourth_kernel(got_ref, gram_a_ref, solved_b_ref, loading_b_ref, solved_ref, squares_ref):
    scale, gram_b = scaled_gram(natural(got_ref, 64, 10, 8, 10))
    loading_b_ref[...] = solved_b_ref[...] * scale
    solver = system_inverse(gram_a_ref[...] * gram_b)
    solved = exact_dot(natural(got_ref, 64, 10, 0, 8) * scale, solver)
    solved_ref[...] = solved
    squares_ref[...] = jnp.sum(solved * solved, axis=0, keepdims=True)


def call(kernel, operands, outs, name, scalars=0, scratch=()):
    vmem = pl.BlockSpec(memory_space=pltpu.VMEM)
    smem = pl.BlockSpec(memory_space=pltpu.SMEM)
    return pl.pallas_call(
        kernel,
        out_shape=[jax.ShapeDtypeStruct(shape, F32) for shape in outs],
        in_specs=[smem] * scalars + [vmem] * (len(operands) - scalars),
        out_specs=[vmem] * len(outs),
        scratch_shapes=scratch,
        compiler_params=pltpu.CompilerParams(vmem_limit_bytes=32 << 20),
        name=name,
    )(*operands)


def exchange(values, axes, *chunk):
    shape = values.shape
    return lax.all_to_all(values.reshape(chunk), axes, 0, 0, tiled=True).reshape(shape)


def on_device(blocks, coords, live, factor_b, factor_c):
    block = blocks[0]
    full = (RANK, RANK)

    chunk, y = call(
        first_kernel, (coords, block, factor_b, factor_c), [(256, RANK), (BI, BJ, RANK)], "first", 1
    )
    got = exchange(chunk, ("ja", "ka"), 32, 8, RANK)
    spread, diagonal = call(collect_first_kernel, (got,), [(384, RANK), (8, RANK)], "collect_a")
    got = exchange(spread, ("ja", "ka"), 32, 3, 4, RANK)

    solved_a, chunk, gram_c = call(
        second_kernel, (coords, got, diagonal, y), [(256, RANK), (256, RANK), full], "second", 1
    )
    got = exchange(chunk, ("ia", "ka"), 32, 8, RANK)
    (spread,) = call(functools.partial(collect_kernel, 32, 4), (got,), [(384, RANK)], "collect_b")
    got = exchange(spread, ("ia", "ka"), 32, 3, 4, RANK)

    loading_a, solved_b, chunk, gram_a = call(
        third_kernel,
        (coords, got, gram_c, solved_a, block),
        [(256, RANK), (256, RANK), (512, RANK), full],
        "third",
        1,
        [pltpu.VMEM((BI * BJ, RANK), BF16)],
    )
    got = exchange(chunk, ("ia", "ja"), 64, 8, RANK)
    (spread,) = call(functools.partial(collect_kernel, 64, 2), (got,), [(640, RANK)], "collect_c")
    got = exchange(spread, ("ia", "ja"), 64, 5, 2, RANK)

    loading_b, solved_c, squares = call(
        fourth_kernel, (got, gram_a, solved_b), [(256, RANK), (512, RANK), (1, RANK)], "fourth"
    )
    total = squares
    for step in (1, 2, 3):
        total = total + lax.ppermute(squares, "ka", [(n, (n + step) % 4) for n in range(4)])
    loading_c = solved_c * lax.rsqrt(total / ROWS + EPSILON)
    return (loading_a, loading_b, loading_c)


def solution(mesh):
    placed = (
        P(("ia", "ja", "ka"), None, None, None),
        P(None, ("ia", "ja", "ka")),
        P(("ia", "ja", "ka")),
        P("ja", None),
        P("ka", None),
    )
    return jax.shard_map(
        on_device,
        mesh=mesh,
        in_specs=placed,
        out_specs=(P("ia", None), P("ja", None), P("ka", None)),
        check_vma=False,
    )
```

time: 1530 us -> 128 us (0.08)
  waiting for transfers between devices: 1070 us -> 4.43 us
  blocking collectives: 341 us -> 97.1 us
  other arithmetic: 75.7 us -> 0.74 us
  between operations: 20.2 us -> 0.68 us
  Pallas kernels: 0 us -> 18.2 us
    psum x3 -> x0, waiting for transfers between devices: 714 us -> none  [grand_sum(): return lax.psum(values, ('ia', 'ja', 'ka'))]
    unnamed x9 -> x0, waiting for transfers between devices: 354 us -> none
    psum x3 -> x0, blocking collectives: 224 us -> none  [normalize(): lax.psum(jnp.sum(stat_rows * stat_rows, axis=0), ('ia', 'ja', 'ka'))]
    all_gather x3 -> x0, blocking collectives: 118 us -> none  [the longest x1 43.7 us: move_rows(): return lax.all_gather(values, ('ia', 'ja'), axis=0, tiled=True)]
    all_to_all x0 -> x6, blocking collectives: none -> 97.1 us  [exchange(): lax.all_to_all(values.reshape(chunk), axes, 0, 0, tiled=True).reshape(shape)]
    another operation x15 -> x0, other arithmetic: 68.6 us -> none  [the longest x9 37.2 us: factorize(): jnp.linalg.cholesky(merged + shift_value * jnp.eye(order_rank, dtype=jnp....]
    pallas_call x0 -> x7, Pallas kernels: none -> 18.2 us  [call(): pl.pallas_call(kernel, out_shape=[jax.ShapeDtypeStruct(shape, F32) for sh...]
  transfers between devices with their start and end apart: 6 -> 3, of which waited for: 6 -> 3; matrix products, arithmetic and copies ran while one was open for 5% -> 0% of each run, Pallas kernels for 0% -> 0%
where the time goes in v2:
time: 128 us
  blocking collectives  97.1 us (76%)
  Pallas kernels  18.2 us (14%)
  waiting for transfers between devices  4.43 us (3%)
  local copies, waits for them, and re-layouts  3.83 us (3%)
  starting transfers between devices  2.89 us (2%)
    all_to_all x6, blocking collectives, exchange(): lax.all_to_all(values.reshape(chunk), axes, 0, 0, tiled=True).reshape(shape)  97.1 us
    pallas_call x7, Pallas kernels, call(): pl.pallas_call(kernel, out_shape=[jax.ShapeDtypeStruct(shape, F32) for sh...  18.2 us
    ppermute x3, waiting for transfers between devices, on_device(): lax.ppermute(squares, 'ka', [(n, (n + step) % 4) for n in range(4)])  4.43 us
    unnamed x9, local copies, waits for them, and re-layouts  3.83 us
    ppermute x3, starting transfers between devices, on_device(): lax.ppermute(squares, 'ka', [(n, (n + step) % 4) for n in range(4)])  2.89 us
  transfers between devices with their start and end apart: 3, of which 3 were waited for; matrix products, arithmetic and copies ran while one was open for 0% of the time, Pallas kernels for 0%

profile of v2, /device:TPU:8, one launch (start us, length us, event | category | flops | bytes accessed | tf_op | source)
XLA Modules:
  0.0 127.9 jit_solution(9569967670141539282)
XLA Ops:
  0.6 0.7 copy.9.coords_ref
  1.4 0.0 copy-start
  1.4 1.2 copy-done
  2.6 0.0 copy-start.2
  2.6 0.9 copy-done.2
  3.5 0.0 copy-start.3
  3.5 0.9 copy-done.3
  4.5 1.4 %first.1 = (f32[256,128]{1,0:T(8,128)S(1)}, f32[64,64,128]{2,1,0:T(8,128)S(1)}) custom-call(s32[3,1]{1,0:T(4,128)S(1)} %copy.9.coords_ref, bf16[64,64,128]{2,1,0:T(8,128)(2,1)S(1)} %bitcast.15, f32[256,128]{1,0:T(8,128)S(1)} %copy-done.3, f32[512,128]{1,0:T(8,128)S(1)} %copy-done.2), custom_call_target="tpu_custom_call" | custom-call | tf_op jit(solution)/shard_map/first/pallas_call | solution.py:243
  5.8 0.0 copy-start.1
  5.9 21.7 %all_to_all.30 = f32[32,8,128]{2,1,0:T(8,128)S(1)} all-to-all(f32[32,8,128]{2,1,0:T(8,128)S(1)} %bitcast.28), channel_id=1, replica_groups=mesh['ia'=8,'ja'=8,'ka'=4] {'ja','ka'}, dimensions={0} | all-to-all | bytes 262144 | tf_op jit(solution)/shard_map/all_to_all | solution.py:256
  27.6 14.5 %all_to_all.31 = f32[32,3,4,128]{3,2,1,0:T(4,128)S(1)} all-to-all(f32[32,3,4,128]{3,2,1,0:T(4,128)S(1)} %bitcast.26), channel_id=1, replica_groups=mesh['ia'=8,'ja'=8,'ka'=4] {'ja','ka'}, dimensions={0} | all-to-all | bytes 393216 | tf_op jit(solution)/shard_map/all_to_all | solution.py:256
  42.1 5.4 %second.1 = (f32[256,128]{1,0:T(8,128)S(1)}, f32[256,128]{1,0:T(8,128)S(1)}, f32[128,128]{1,0:T(8,128)S(1)}) custom-call(s32[3,1]{1,0:T(4,128)S(1)} %copy.9.coords_ref, f32[384,128]{1,0:T(8,128)S(1)} %bitcast.22, f32[8,128]{1,0:T(8,128)S(1)} %get-tuple-element.19.diagonal_ref, f32[64,64,128]{2,1,0:T(8,128)S(1)} %get-tuple-element.20.y_ref), custom_call_target="tpu_custom_call" | custom-call | tf_op jit(solution)/shard_map/second/pallas_call | solution.py:243
  47.5 12.1 %all_to_all.32 = f32[32,8,128]{2,1,0:T(8,128)S(1)} all-to-all(f32[32,8,128]{2,1,0:T(8,128)S(1)} %bitcast.27), channel_id=1, replica_groups=mesh['ia'=8,'ja'=8,'ka'=4] {'ia','ka'}, dimensions={0} | all-to-all | bytes 262144 | tf_op jit(solution)/shard_map/all_to_all | solution.py:256
  59.6 12.0 %all_to_all.33 = f32[32,3,4,128]{3,2,1,0:T(4,128)S(1)} all-to-all(f32[32,3,4,128]{3,2,1,0:T(4,128)S(1)} %bitcast.20), channel_id=1, replica_groups=mesh['ia'=8,'ja'=8,'ka'=4] {'ia','ka'}, dimensions={0} | all-to-all | bytes 393216 | tf_op jit(solution)/shard_map/all_to_all | solution.py:256
  71.6 0.0 copy-done.1
  71.6 6.1 %third.1 = (f32[256,128]{1,0:T(8,128)}, f32[256,128]{1,0:T(8,128)S(1)}, f32[512,128]{1,0:T(8,128)S(1)}, f32[128,128]{1,0:T(8,128)S(1)}) custom-call(s32[3,1]{1,0:T(4,128)S(1)} %copy.9.coords_ref, f32[384,128]{1,0:T(8,128)S(1)} %bitcast.21, f32[128,128]{1,0:T(8,128)S(1)} %get-tuple-element.22.gram_c_ref, f32[256,128]{1,0:T(8,128)S(1)} %get-tuple-element.23.solved_a_ref, ...), custom_call_target="tpu_custom_call" | custom-call | tf_op jit(solution)/shard_map/third/pallas_call | solution.py:243
  77.8 17.6 %all_to_all.34 = f32[64,8,128]{2,1,0:T(8,128)S(1)} all-to-all(f32[64,8,128]{2,1,0:T(8,128)S(1)} %bitcast.25), channel_id=1, replica_groups=mesh['ia'=8,'ja'=8,'ka'=4] {'ia','ja'}, dimensions={0} | all-to-all | bytes 524288 | tf_op jit(solution)/shard_map/all_to_all | solution.py:256
  95.4 0.1 collect_c.1
  95.5 19.2 %all_to_all.35 = f32[64,5,2,128]{3,2,1,0:T(2,128)S(1)} all-to-all(f32[64,5,2,128]{3,2,1,0:T(2,128)S(1)} %bitcast.18), channel_id=1, replica_groups=mesh['ia'=8,'ja'=8,'ka'=4] {'ia','ja'}, dimensions={0} | all-to-all | bytes 655360 | tf_op jit(solution)/shard_map/all_to_all | solution.py:256
  114.7 5.1 %fourth.1 = (f32[256,128]{1,0:T(8,128)}, f32[512,128]{1,0:T(8,128)S(1)}, f32[1,128]{1,0:T(1,128)S(1)}) custom-call(f32[640,128]{1,0:T(8,128)S(1)} %bitcast.17, f32[128,128]{1,0:T(8,128)S(1)} %get-tuple-element.26.gram_a_ref, f32[256,128]{1,0:T(8,128)S(1)} %get-tuple-element.27.solved_b_ref), custom_call_target="tpu_custom_call" | custom-call | tf_op jit(solution)/shard_map/fourth/pallas_call | solution.py:243
  119.8 1.6 %collective-permute-start.2 = (f32[1,128]{1,0:T(1,128)S(1)}, f32[1,128]{1,0:T(1,128)S(1)}, u32[]{:S(2)}, u32[]{:S(2)}) collective-permute-start(f32[1,128]{1,0:T(1,128)S(1)} %get-tuple-element.30), channel_id=1, source_target_pairs={{0,3},{1,0},{2,1},{3,2},{4,7},{5,4},{6,5},{7,6},{8,11},{9,8},{10,9... | collective-permute-start | bytes 1544 | tf_op jit(solution)/shard_map/ppermute | solution.py:294
  121.5 0.9 collective-permute-start.1
  122.4 0.4 collective-permute-start
  122.7 0.7 collective-permute-done.2
  123.4 3.2 %collective-permute-done.1 = f32[1,128]{1,0:T(1,128)S(1)} collective-permute-done((f32[1,128]{1,0:T(1,128)S(1)}, f32[1,128]{1,0:T(1,128)S(1)}, u32[]{:S(2)}, u32[]{:S(2)}) %collective-permute-start.1) | collective-permute-done | bytes 544 | tf_op jit(solution)/shard_map/ppermute | solution.py:294
  126.5 0.6 collective-permute-done
  127.1 0.7 broadcast_multiply_fusion
  (3 shorter events, 0.1 us)
Async XLA Ops:
  1.4 1.2 copy-start
  2.6 0.9 copy-start.2
  3.5 0.9 copy-start.3
  5.8 65.8 %copy-start.1 = (bf16[1,64,64,128]{3,2,1,0:T(8,128)(2,1)S(1)}, bf16[1,64,64,128]{3,2,1,0:T(8,128)(2,1)}, u32[]{:S(2)}) copy-start(bf16[1,64,64,128]{3,2,1,0:T(8,128)(2,1)} %param.5) | copy-start | bytes 3145732
  119.8 3.6 %collective-permute-start.2 = (f32[1,128]{1,0:T(1,128)S(1)}, f32[1,128]{1,0:T(1,128)S(1)}, u32[]{:S(2)}, u32[]{:S(2)}) collective-permute-start(f32[1,128]{1,0:T(1,128)S(1)} %get-tuple-element.30), channel_id=1, source_target_pairs={{0,3},{1,0},{2,1},{3,2},{4,7},{5,4},{6,5},{7,6},{8,11},{9,8},{10,9... | collective-permute-start | bytes 1544 | tf_op jit(solution)/shard_map/ppermute | solution.py:294
  121.5 5.1 %collective-permute-start.1 = (f32[1,128]{1,0:T(1,128)S(1)}, f32[1,128]{1,0:T(1,128)S(1)}, u32[]{:S(2)}, u32[]{:S(2)}) collective-permute-start(f32[1,128]{1,0:T(1,128)S(1)} %get-tuple-element.30), channel_id=1, source_target_pairs={{0,2},{1,3},{2,0},{3,1},{4,6},{5,7},{6,4},{7,5},{8,10},{9,11},{10,... | collective-permute-start | bytes 1544 | tf_op jit(solution)/shard_map/ppermute | solution.py:294
  122.4 4.8 %collective-permute-start = (f32[1,128]{1,0:T(1,128)S(1)}, f32[1,128]{1,0:T(1,128)S(1)}, u32[]{:S(2)}, u32[]{:S(2)}) collective-permute-start(f32[1,128]{1,0:T(1,128)S(1)} %get-tuple-element.30), channel_id=1, source_target_pairs={{0,1},{1,2},{2,3},{3,0},{4,5},{5,6},{6,7},{7,4},{8,9},{9,10},{10,1... | collective-permute-start | bytes 1544 | tf_op jit(solution)/shard_map/ppermute | solution.py:294

commit v3 on v2

v3 whole, which is shorter than its diff:
```python
import jax
import jax.numpy as jnp
from jax import lax
from jax.experimental import pallas as pl
from jax.experimental.pallas import tpu as pltpu
from jax.sharding import PartitionSpec as P

RANK = 128
BI = 64
BJ = 64
BK = 128
GI_DEV = 4
GJ_DEV = 4
GK_DEV = 4
SLOTS = 4
ROWS = 2048
IA = ("iy", "ic")

RIDGE_SHARE = 0.3
EPSILON = 1e-06
HIGHEST = lax.Precision.HIGHEST
F32 = jnp.float32
BF16 = jnp.bfloat16


def exact_dot(left, right):
    return jnp.dot(left, right, precision=HIGHEST, preferred_element_type=F32)


def gram(rows):
    return lax.dot_general(
        rows, rows, (((0,), (0,)), ((), ())), precision=HIGHEST, preferred_element_type=F32
    )


def halves(values):
    high = values.astype(BF16)
    return high, (values - high.astype(F32)).astype(BF16)


def iotas():
    shape = (RANK, RANK)
    return lax.broadcasted_iota(jnp.int32, shape, 0), lax.broadcasted_iota(jnp.int32, shape, 1)


def inverse(matrix):
    count = RANK // 8
    rows = [matrix[8 * n : 8 * n + 8, :] for n in range(count)]
    lane = lax.broadcasted_iota(jnp.int32, (8, RANK), 1)
    sub = lax.broadcasted_iota(jnp.int32, (8, RANK), 0)

    def over_lanes(tile, at):
        return jnp.broadcast_to(tile[:, at : at + 1], (8, RANK))

    def over_rows(tile, at):
        return jnp.broadcast_to(tile[at : at + 1, :], (8, RANK))

    one = jnp.clip(rows[0], 1.0, 1.0)
    for k in range(count):
        panel = rows[k]
        columns = [over_lanes(panel, 8 * k + t) * one for t in range(8)]
        inside = (lane >= 8 * k) & (lane < 8 * k + 8)
        panel = jnp.where(inside, jnp.where(lane - 8 * k == sub, 1.0, 0.0), panel)
        for s in range(8):
            pivot = over_rows(1.0 / columns[s], s)
            factor = jnp.where(sub == s, 0.0, columns[s]) * pivot
            keep = jnp.where(sub == s, pivot, 1.0)
            panel = panel * keep - factor * over_rows(panel, s)
            for t in range(s + 1, 8):
                columns[t] = columns[t] * keep - factor * over_rows(columns[t], s)
        leads = [over_rows(panel, s) for s in range(8)]
        for step in range(count - 1):
            n = (k + 1 + step) % count
            terms = [over_lanes(rows[n], 8 * k + s) * leads[s] for s in range(8)]
            while len(terms) > 1:
                terms = [terms[i] + terms[i + 1] for i in range(0, len(terms), 2)]
            rows[n] = jnp.where(inside, 0.0, rows[n]) - terms[0]
        rows[k] = panel
    return jnp.concatenate(rows, axis=0)


def system_inverse(merged):
    row, col = iotas()
    shift = jnp.sum(jnp.where(row == col, merged, 0.0)) * (RIDGE_SHARE / RANK)
    return inverse(merged + jnp.where(row == col, shift, 0.0))


def strided(ref, start, count, step):
    return ref[pl.ds(start, count, stride=step), :]


def put(ref, start, count, step, value):
    ref[pl.ds(start, count, stride=step), :] = value


def scaled_gram(raw):
    row, col = iotas()
    diagonal = jnp.where(row == col, raw, 0.0)
    across = lax.rsqrt(jnp.sum(diagonal, axis=0, keepdims=True) + EPSILON)
    down = lax.rsqrt(jnp.sum(diagonal, axis=1, keepdims=True) + EPSILON)
    return across, raw * down * across


def places(coords_ref):
    at = [lax.axis_index(IA), lax.axis_index("ja"), lax.axis_index("ka")]
    return at, [coords_ref[n] - 4 * at[n] for n in range(3)]


def some_rows(ref, index, size):
    return ref[pl.ds(pl.multiple_of(index * size, size), size), :]


def first_kernel(
    coords_ref, block_ref, b_ref, c_ref, chunk_ref, y_ref,
    x_in, c_in, b_in, share_c, share_b, sems,
):
    at, slot = places(coords_ref)

    def window(ref, index, size):
        return ref.at[pl.ds(pl.multiple_of(index * size, size), size), :]

    small = [
        (window(c_ref, slot[2], BK), c_in),
        (window(b_ref, slot[1], BJ), b_in),
        (window(c_ref, at[1], 64), share_c),
        (window(b_ref, at[2], 64), share_b),
    ]
    parts = [pl.ds(n * (BI // 4), BI // 4) for n in range(4)]
    copies = [pltpu.make_async_copy(src, dst, sems.at[n]) for n, (src, dst) in enumerate(small)]
    copies += [
        pltpu.make_async_copy(block_ref.at[part], x_in.at[part], sems.at[4 + n])
        for n, part in enumerate(parts)
    ]
    for copy in copies:
        copy.start()
    for copy in copies[:4]:
        copy.wait()
    part_c = gram(share_c[...]) * (1.0 / ROWS)
    part_b = gram(share_b[...]) * (1.0 / ROWS)
    row, col = iotas()
    packed = jnp.where(row <= col, part_b, part_c)
    diagonal = jnp.sum(jnp.where(row == col, part_c, 0.0), axis=0, keepdims=True)
    for t in range(4):
        put(chunk_ref, 2 + t, 32, 8, packed[32 * t : 32 * t + 32])
    put(chunk_ref, 6, 32, 8, jnp.broadcast_to(diagonal, (32, RANK)))
    put(chunk_ref, 7, 32, 8, jnp.full((32, RANK), slot[0].astype(F32)))
    high, low = halves(c_in[...])
    both = jnp.concatenate([high, low], axis=0)
    rows_b = b_in[...]
    partial = []
    for n, part in enumerate(parts):
        copies[4 + n].wait()
        block = x_in[part].reshape(BI // 4 * BJ, BK)
        y = jnp.dot(jnp.concatenate([block, block], axis=1), both, preferred_element_type=F32)
        y = y.reshape(BI // 4, BJ, RANK)
        y_ref[part] = y
        partial += [jnp.sum(y[m] * rows_b, axis=0, keepdims=True) for m in range(BI // 4)]
    for t in range(2):
        put(chunk_ref, t, 32, 8, jnp.concatenate(partial[32 * t : 32 * t + 32], axis=0))


def collect(got_ref, count, step, ids, extras):
    rows = []
    for slot in range(SLOTS):
        for t in range(2):
            picked = jnp.where(ids == slot, strided(got_ref, t, count, step), 0.0)
            rows.append(jnp.sum(picked, axis=0, keepdims=True))
    for t in range(extras):
        rows.append(jnp.sum(strided(got_ref, 2 + t, count, step), axis=0, keepdims=True))
    return rows


def lower_lanes(values):
    lane = lax.broadcasted_iota(jnp.int32, values.shape, 1)
    return jnp.where(lane < 64, values, pltpu.roll(values, 64, 1))


def mark(rows, slot):
    lane = lax.broadcasted_iota(jnp.int32, rows.shape, 1)
    return jnp.where(lane < 64, slot.astype(F32), rows)


def unmark(raw):
    row, col = iotas()
    return jnp.where((row >= 64) & (col < 64), raw.T, raw)


def repeat_rows(ref, rows, copies):
    width = len(rows)
    unit = 1
    while width * unit % 8:
        unit *= 2
    tile = jnp.concatenate(rows * unit, axis=0)
    for n in range(copies // unit):
        ref[n * width * unit : (n + 1) * width * unit, :] = tile


def collect_first_kernel(got_ref, spread_ref, diagonal_ref):
    rows = collect(got_ref, 32, 8, strided(got_ref, 7, 32, 8), 5)
    repeat_rows(spread_ref, rows[:12], 32)
    diagonal_ref[...] = jnp.broadcast_to(rows[12], (8, RANK))


def collect_second_kernel(got_ref, spread_ref):
    rows = collect(got_ref, 32, 6, lower_lanes(strided(got_ref, 5, 32, 6)), 4)
    repeat_rows(spread_ref, rows, 32)


def collect_third_kernel(got_ref, spread_ref):
    rows = collect(got_ref, 64, 4, lower_lanes(strided(got_ref, 3, 64, 4)), 2)
    repeat_rows(spread_ref, rows, 32)


def natural(got_ref, count, step, first, last):
    return jnp.concatenate([strided(got_ref, t, count, step) for t in range(first, last)], axis=0)


def second_kernel(coords_ref, got_ref, diagonal_ref, y_ref, solved_ref, chunk_ref, gram_c_ref):
    at, slot = places(coords_ref)
    packed = natural(got_ref, 32, 12, 8, 12)
    flipped = packed.T
    row, col = iotas()
    gram_b = jnp.where(row <= col, packed, flipped)
    gram_c = jnp.where(row < col, flipped, packed)
    gram_c = jnp.where(row == col, diagonal_ref[0:1, :], gram_c)
    gram_c_ref[...] = gram_c
    solver = system_inverse(gram_b * gram_c)
    solved_ref[...] = exact_dot(natural(got_ref, 32, 12, 0, 8), solver)
    raw = gram(some_rows(solved_ref, at[2], 64)) * (1.0 / ROWS)
    own = some_rows(solved_ref, slot[0], BI)
    sums = [jnp.zeros((BJ, RANK), F32) for _ in range(2)]
    for n in range(BI):
        sums[n % 2] = sums[n % 2] + own[n : n + 1, :] * y_ref[n]
    partial = sums[0] + sums[1]
    for t in range(2):
        put(chunk_ref, t, 32, 6, partial[32 * t : 32 * t + 32])
    for t in range(4):
        rows = raw[32 * t : 32 * t + 32]
        put(chunk_ref, 2 + t, 32, 6, rows if t < 2 else mark(rows, slot[1]))


def third_kernel(
    coords_ref, got_ref, gram_c_ref, solved_a_ref, block_ref,
    loading_a_ref, solved_ref, chunk_ref, gram_a_ref, khatri_ref,
):
    at, slot = places(coords_ref)
    scale, gram_a = scaled_gram(unmark(natural(got_ref, 32, 12, 8, 12)))
    gram_a_ref[...] = gram_a
    loading_a_ref[...] = solved_a_ref[...] * scale
    solver = system_inverse(gram_a * gram_c_ref[...])
    solved_ref[...] = exact_dot(natural(got_ref, 32, 12, 0, 8) * scale, solver)
    raw = gram(some_rows(solved_ref, at[0], 32)) * (1.0 / ROWS)
    own_a = some_rows(loading_a_ref, slot[0], BI)
    own_b = some_rows(solved_ref, slot[1], BJ)
    for n in range(BI):
        khatri_ref[n * BJ : (n + 1) * BJ, :] = (own_a[n : n + 1, :] * own_b).astype(BF16)
    partial = lax.dot_general(
        block_ref[...].reshape(BI * BJ, BK),
        khatri_ref[...],
        (((0,), (0,)), ((), ())),
        preferred_element_type=F32,
    )
    for t in range(2):
        put(chunk_ref, t, 64, 4, partial[64 * t : 64 * t + 64])
    put(chunk_ref, 2, 64, 4, raw[0:64])
    put(chunk_ref, 3, 64, 4, mark(raw[64:128], slot[2]))


def fourth_kernel(
    same_ref, other_ref, gram_a_ref, solved_b_ref, loading_b_ref, solved_ref, squares_ref, rows_ref
):
    core = lax.axis_index("ic")
    for ref, half in ((same_ref, core), (other_ref, 1 - core)):
        for t in range(10):
            for n in range(4):
                place = pl.multiple_of(64 * t + 16 * n + 8 * half, 8)
                rows_ref[pl.ds(place, 8), :] = strided(ref, 80 * n + t, 8, 10)
    scale, gram_b = scaled_gram(unmark(rows_ref[512:640, :]))
    loading_b_ref[...] = solved_b_ref[...] * scale
    solver = system_inverse(gram_a_ref[...] * gram_b)
    solved = exact_dot(rows_ref[0:512, :] * scale, solver)
    solved_ref[...] = solved
    squares_ref[...] = jnp.sum(solved * solved, axis=0, keepdims=True)


def call(kernel, operands, outs, name, scalars=0, scratch=(), space=pltpu.VMEM):
    vmem = pl.BlockSpec(memory_space=pltpu.VMEM)
    smem = pl.BlockSpec(memory_space=pltpu.SMEM)
    return pl.pallas_call(
        kernel,
        out_shape=[jax.ShapeDtypeStruct(shape, F32) for shape in outs],
        in_specs=[smem] * scalars + [pl.BlockSpec(memory_space=space)] * (len(operands) - scalars),
        out_specs=[vmem] * len(outs),
        scratch_shapes=scratch,
        compiler_params=pltpu.CompilerParams(vmem_limit_bytes=32 << 20),
        name=name,
    )(*operands)


def exchange(values, axes, *chunk):
    shape = values.shape
    return lax.all_to_all(values.reshape(chunk), axes, 0, 0, tiled=True).reshape(shape)


def on_device(blocks, coords, live, factor_b, factor_c):
    block = blocks[0]
    coords = coords.reshape(3)
    full = (RANK, RANK)

    chunk, y = call(
        first_kernel,
        (coords, block, factor_b, factor_c),
        [(256, RANK), (BI, BJ, RANK)],
        "first",
        1,
        [
            pltpu.VMEM((BI, BJ, BK), BF16),
            pltpu.VMEM((BK, RANK), F32),
            pltpu.VMEM((BJ, RANK), F32),
            pltpu.VMEM((64, RANK), F32),
            pltpu.VMEM((64, RANK), F32),
            pltpu.SemaphoreType.DMA((8,)),
        ],
        pl.ANY,
    )
    got = exchange(chunk, ("ja", "ka"), 32, 8, RANK)
    spread, diagonal = call(collect_first_kernel, (got,), [(384, RANK), (8, RANK)], "collect_a")
    got = exchange(spread, ("ja", "ka"), 32, 3, 4, RANK)

    solved_a, chunk, gram_c = call(
        second_kernel, (coords, got, diagonal, y), [(256, RANK), (192, RANK), full], "second", 1
    )
    got = exchange(chunk, (*IA, "ka"), 32, 3, 2, RANK)
    (spread,) = call(collect_second_kernel, (got,), [(384, RANK)], "collect_b")
    got = exchange(spread, (*IA, "ka"), 32, 3, 4, RANK)

    loading_a, solved_b, chunk, gram_a = call(
        third_kernel,
        (coords, got, gram_c, solved_a, block),
        [(256, RANK), (256, RANK), (256, RANK), full],
        "third",
        1,
        [pltpu.VMEM((BI * BJ, RANK), BF16)],
    )
    got = exchange(chunk, (*IA, "ja"), 64, 4, RANK)
    (spread,) = call(collect_third_kernel, (got,), [(320, RANK)], "collect_c")
    same = exchange(spread, ("iy", "ja"), 32, 5, 2, RANK)
    other = lax.ppermute(same, "ic", [(0, 1), (1, 0)])

    loading_b, solved_c, squares = call(
        fourth_kernel,
        (same, other, gram_a, solved_b),
        [(256, RANK), (512, RANK), (1, RANK)],
        "fourth",
        0,
        [pltpu.VMEM((640, RANK), F32)],
    )
    total = squares
    for step in (1, 2, 3):
        total = total + lax.ppermute(squares, "ka", [(n, (n + step) % 4) for n in range(4)])
    loading_c = solved_c * lax.rsqrt(total / ROWS + EPSILON)
    return (loading_a, loading_b, loading_c)


def solution(mesh):
    shape = mesh.devices.shape
    split = jax.sharding.Mesh(
        mesh.devices.reshape(shape[0] // 2, 2, *shape[1:]), (*IA, "ja", "ka")
    )
    every = (*IA, "ja", "ka")
    placed = (P(every, None, None, None), P(None, every), P(every), P("ja", None), P("ka", None))
    return jax.shard_map(
        on_device,
        mesh=split,
        in_specs=placed,
        out_specs=(P(IA, None), P("ja", None), P("ka", None)),
        check_vma=False,
    )
```

time: 128 us -> 123 us (0.961)
  blocking collectives: 97.1 us -> 89.3 us
  waiting for transfers between devices: 4.43 us -> 5.84 us
    all_to_all x6, blocking collectives: 97.1 us -> 89.3 us  [exchange(): lax.all_to_all(values.reshape(chunk), axes, 0, 0, tiled=True).reshape(shape)]
    ppermute x0 -> x1, waiting for transfers between devices: none -> 1.39 us  [on_device(): other = lax.ppermute(same, 'ic', [(0, 1), (1, 0)])]
    unnamed x9 -> x12, local copies, waits for them, and re-layouts: 3.83 us -> 3.74 us
  transfers between devices with their start and end apart: 3 -> 4, of which waited for: 3 -> 4; matrix products, arithmetic and copies ran while one was open for 0% -> 0% of each run, Pallas kernels for 0% -> 0%
where the time goes in v3:
time: 123 us; the launch traced here: 122 us
  blocking collectives  89.3 us (73%)
  Pallas kernels  18.8 us (15%)
  waiting for transfers between devices  5.84 us (5%)
  local copies, waits for them, and re-layouts  3.74 us (3%)
  starting transfers between devices  3.01 us (2%)
    all_to_all x6, blocking collectives, exchange(): lax.all_to_all(values.reshape(chunk), axes, 0, 0, tiled=True).reshape(shape)  89.3 us
    pallas_call x7, Pallas kernels, call(): pl.pallas_call(kernel, out_shape=[jax.ShapeDtypeStruct(shape, F32) for sh...  18.8 us
    ppermute x3, waiting for transfers between devices, on_device(): lax.ppermute(squares, 'ka', [(n, (n + step) % 4) for n in range(4)])  4.44 us
    unnamed x12, local copies, waits for them, and re-layouts  3.74 us
    ppermute x3, starting transfers between devices, on_device(): lax.ppermute(squares, 'ka', [(n, (n + step) % 4) for n in range(4)])  3.01 us
  transfers between devices with their start and end apart: 4, of which 4 were waited for; matrix products, arithmetic and copies ran while one was open for 0% of the time, Pallas kernels for 0%

profile of v3, /device:TPU:8, one launch (start us, length us, event | category | flops | bytes accessed | tf_op | source)
XLA Modules:
  0.0 122.1 jit_solution(16384500235396587029)
XLA Ops:
  0.6 0.0 copy-start.5
  0.6 0.0 copy-start
  0.7 1.2 copy-done
  1.9 0.0 copy-start.2
  1.9 0.9 copy-done.2
  2.8 0.9 copy-done.3
  3.7 0.0 copy-start.4
  3.7 0.7 copy-done.4
  4.4 3.0 %first.1 = (f32[256,128]{1,0:T(8,128)S(1)}, f32[64,64,128]{2,1,0:T(8,128)S(1)}) custom-call(s32[3]{0:T(128)S(1)} %bitcast.31, bf16[64,64,128]{2,1,0:T(8,128)(2,1)S(1)} %bitcast.16, f32[256,128]{1,0:T(8,128)S(1)} %copy-done.3, f32[512,128]{1,0:T(8,128)S(1)} %copy-done.2), custom_call_target="tpu_custom_call" | custom-call | tf_op jit(solution)/shard_map/first/pallas_call | solution.py:289
  7.4 0.0 copy-start.1
  7.4 21.7 %all_to_all.30 = f32[32,8,128]{2,1,0:T(8,128)S(1)} all-to-all(f32[32,8,128]{2,1,0:T(8,128)S(1)} %bitcast.29), channel_id=1, replica_groups=mesh['iy'=4,'ic'=2,'ja'=8,'ka'=4] {'ja','ka'}, dimensions={0} | all-to-all | bytes 262144 | tf_op jit(solution)/shard_map/all_to_all | solution.py:302
  29.1 14.5 %all_to_all.31 = f32[32,3,4,128]{3,2,1,0:T(4,128)S(1)} all-to-all(f32[32,3,4,128]{3,2,1,0:T(4,128)S(1)} %bitcast.27), channel_id=1, replica_groups=mesh['iy'=4,'ic'=2,'ja'=8,'ka'=4] {'ja','ka'}, dimensions={0} | all-to-all | bytes 393216 | tf_op jit(solution)/shard_map/all_to_all | solution.py:302
  43.6 0.0 copy-done.5
  43.6 5.2 %second.1 = (f32[256,128]{1,0:T(8,128)S(1)}, f32[192,128]{1,0:T(8,128)S(1)}, f32[128,128]{1,0:T(8,128)S(1)}) custom-call(s32[3]{0:T(128)S(1)} %bitcast.32, f32[384,128]{1,0:T(8,128)S(1)} %bitcast.18, f32[8,128]{1,0:T(8,128)S(1)} %get-tuple-element.19.diagonal_ref, f32[64,64,128]{2,1,0:T(8,128)S(1)} %get-tuple-element.20.y_ref), custom_call_target="tpu_custom_call" | custom-call | tf_op jit(solution)/shard_map/second/pallas_call | solution.py:289
  48.8 11.9 %all_to_all.32 = f32[32,3,2,128]{3,2,1,0:T(2,128)S(1)} all-to-all(f32[32,3,2,128]{3,2,1,0:T(2,128)S(1)} %bitcast.30), channel_id=1, replica_groups=mesh['iy'=4,'ic'=2,'ja'=8,'ka'=4] {'iy','ic','ka'}, dimensions={0} | all-to-all | bytes 196608 | tf_op jit(solution)/shard_map/all_to_all | solution.py:302
  60.7 0.1 collect_b.1
  60.8 11.8 %all_to_all.33 = f32[32,3,4,128]{3,2,1,0:T(4,128)S(1)} all-to-all(f32[32,3,4,128]{3,2,1,0:T(4,128)S(1)} %bitcast.19), channel_id=1, replica_groups=mesh['iy'=4,'ic'=2,'ja'=8,'ka'=4] {'iy','ic','ka'}, dimensions={0} | all-to-all | bytes 393216 | tf_op jit(solution)/shard_map/all_to_all | solution.py:302
  72.7 0.0 copy-done.1
  72.7 5.9 %third.1 = (f32[256,128]{1,0:T(8,128)}, f32[256,128]{1,0:T(8,128)S(1)}, f32[256,128]{1,0:T(8,128)S(1)}, f32[128,128]{1,0:T(8,128)S(1)}) custom-call(s32[3]{0:T(128)S(1)} %bitcast.33, f32[384,128]{1,0:T(8,128)S(1)} %bitcast.20, f32[128,128]{1,0:T(8,128)S(1)} %get-tuple-element.22.gram_c_ref, f32[256,128]{1,0:T(8,128)S(1)} %get-tuple-element.23.solved_a_ref, ...), custom_call_target="tpu_custom_call" | custom-call | tf_op jit(solution)/shard_map/third/pallas_call | solution.py:289
  78.6 15.2 %all_to_all.34 = f32[64,4,128]{2,1,0:T(4,128)S(1)} all-to-all(f32[64,4,128]{2,1,0:T(4,128)S(1)} %bitcast.28), channel_id=1, replica_groups=mesh['iy'=4,'ic'=2,'ja'=8,'ka'=4] {'iy','ic','ja'}, dimensions={0} | all-to-all | bytes 262144 | tf_op jit(solution)/shard_map/all_to_all | solution.py:302
  93.8 0.1 collect_c.1
  93.9 14.2 %all_to_all.35 = f32[32,5,2,128]{3,2,1,0:T(2,128)S(1)} all-to-all(f32[32,5,2,128]{3,2,1,0:T(2,128)S(1)} %bitcast.23), channel_id=1, replica_groups=mesh['iy'=4,'ic'=2,'ja'=8,'ka'=4] {'iy','ja'}, dimensions={0} | all-to-all | bytes 327680 | tf_op jit(solution)/shard_map/all_to_all | solution.py:302
  108.1 0.0 collective-permute-start
  108.1 1.4 %collective-permute-done.other_ref = f32[320,128]{1,0:T(8,128)S(1)} collective-permute-done((f32[320,128]{1,0:T(8,128)S(1)}, f32[320,128]{1,0:T(8,128)S(1)}, u32[]{:S(2)}, u32[]{:S(2)}) %collective-permute-start) | collective-permute-done | bytes 163872 | tf_op jit(solution)/shard_map/ppermute | solution.py:348
  109.5 4.4 %fourth.1 = (f32[256,128]{1,0:T(8,128)}, f32[512,128]{1,0:T(8,128)S(1)}, f32[1,128]{1,0:T(1,128)S(1)}) custom-call(f32[320,128]{1,0:T(8,128)S(1)} %bitcast.22, f32[320,128]{1,0:T(8,128)S(1)} %collective-permute-done.other_ref, f32[128,128]{1,0:T(8,128)S(1)} %get-tuple-element.26.gram_a_ref, f32[256,128]{1,0:T(8,128)S(1)} %get-tuple-element.27.solved_b_ref), custom_call_target="tpu_custom_call" | custom-call | tf_op jit(solution)/shard_map/fourth/pallas_call | solution.py:289
  113.9 1.8 %collective-permute-start.3 = (f32[1,128]{1,0:T(1,128)S(1)}, f32[1,128]{1,0:T(1,128)S(1)}, u32[]{:S(2)}, u32[]{:S(2)}) collective-permute-start(f32[1,128]{1,0:T(1,128)S(1)} %get-tuple-element.30), channel_id=1, source_target_pairs={{0,3},{1,0},{2,1},{3,2},{4,7},{5,4},{6,5},{7,6},{8,11},{9,8},{10,9... | collective-permute-start | bytes 1544 | tf_op jit(solution)/shard_map/ppermute | solution.py:360
  115.7 0.9 collective-permute-start.2
  116.6 0.3 collective-permute-start.1
  116.9 0.6 collective-permute-done.3
  117.5 3.2 %collective-permute-done.2 = f32[1,128]{1,0:T(1,128)S(1)} collective-permute-done((f32[1,128]{1,0:T(1,128)S(1)}, f32[1,128]{1,0:T(1,128)S(1)}, u32[]{:S(2)}, u32[]{:S(2)}) %collective-permute-start.2) | collective-permute-done | bytes 544 | tf_op jit(solution)/shard_map/ppermute | solution.py:360
  120.7 0.6 collective-permute-done.1
  121.3 0.7 broadcast_multiply_fusion
  (3 shorter events, 0.1 us)
Async XLA Ops:
  0.6 43.0 %copy-start.5 = (s32[3,1]{0,1:T(1,128)S(1)}, s32[3,1]{0,1:T(1,128)}, u32[]{:S(2)}) copy-start(s32[3,1]{0,1:T(1,128)} %param.6) | copy-start | bytes 40
  0.6 1.2 %copy-start = (bf16[1,64,64,128]{3,2,1,0:T(8,128)(2,1)S(1)}, bf16[1,64,64,128]{3,2,1,0:T(8,128)(2,1)}, u32[]{:S(2)}) copy-start(bf16[1,64,64,128]{3,2,1,0:T(8,128)(2,1)} %param.5) | copy-start | bytes 3145732
  1.9 0.9 copy-start.2
  2.8 0.9 copy-start.3
  3.7 0.7 copy-start.4
  7.4 65.3 %copy-start.1 = (bf16[1,64,64,128]{3,2,1,0:T(8,128)(2,1)S(1)}, bf16[1,64,64,128]{3,2,1,0:T(8,128)(2,1)}, u32[]{:S(2)}) copy-start(bf16[1,64,64,128]{3,2,1,0:T(8,128)(2,1)} %param.5) | copy-start | bytes 3145732
  108.1 1.4 %collective-permute-start = (f32[320,128]{1,0:T(8,128)S(1)}, f32[320,128]{1,0:T(8,128)S(1)}, u32[]{:S(2)}, u32[]{:S(2)}) collective-permute-start(f32[320,128]{1,0:T(8,128)S(1)} %bitcast.21), channel_id=1, source_target_pairs={{0,32},{32,0},{1,33},{33,1},{2,34},{34,2},{3,35},{35,3},{4,36},{36... | collective-permute-start | bytes 491528 | tf_op jit(solution)/shard_map/ppermute | solution.py:348
  113.9 3.6 %collective-permute-start.3 = (f32[1,128]{1,0:T(1,128)S(1)}, f32[1,128]{1,0:T(1,128)S(1)}, u32[]{:S(2)}, u32[]{:S(2)}) collective-permute-start(f32[1,128]{1,0:T(1,128)S(1)} %get-tuple-element.30), channel_id=1, source_target_pairs={{0,3},{1,0},{2,1},{3,2},{4,7},{5,4},{6,5},{7,6},{8,11},{9,8},{10,9... | collective-permute-start | bytes 1544 | tf_op jit(solution)/shard_map/ppermute | solution.py:360
  115.7 5.1 %collective-permute-start.2 = (f32[1,128]{1,0:T(1,128)S(1)}, f32[1,128]{1,0:T(1,128)S(1)}, u32[]{:S(2)}, u32[]{:S(2)}) collective-permute-start(f32[1,128]{1,0:T(1,128)S(1)} %get-tuple-element.30), channel_id=1, source_target_pairs={{0,2},{1,3},{2,0},{3,1},{4,6},{5,7},{6,4},{7,5},{8,10},{9,11},{10,... | collective-permute-start | bytes 1544 | tf_op jit(solution)/shard_map/ppermute | solution.py:360
  116.6 4.8 %collective-permute-start.1 = (f32[1,128]{1,0:T(1,128)S(1)}, f32[1,128]{1,0:T(1,128)S(1)}, u32[]{:S(2)}, u32[]{:S(2)}) collective-permute-start(f32[1,128]{1,0:T(1,128)S(1)} %get-tuple-element.30), channel_id=1, source_target_pairs={{0,1},{1,2},{2,3},{3,0},{4,5},{5,6},{6,7},{7,4},{8,9},{9,10},{10,1... | collective-permute-start | bytes 1544 | tf_op jit(solution)/shard_map/ppermute | solution.py:360

commit v4 on v3

--- a/solution.py
+++ b/solution.py
@@ -27,10 +27,14 @@
     return jnp.dot(left, right, precision=HIGHEST, preferred_element_type=F32)
 
 
+def across_rows(left, right):
+    return lax.dot_general(
+        left, right, (((0,), (0,)), ((), ())), precision=HIGHEST, preferred_element_type=F32
+    )
+
+
 def gram(rows):
-    return lax.dot_general(
-        rows, rows, (((0,), (0,)), ((), ())), precision=HIGHEST, preferred_element_type=F32
-    )
+    return across_rows(rows, rows)
 
 
 def halves(values):
@@ -48,6 +52,8 @@
     rows = [matrix[8 * n : 8 * n + 8, :] for n in range(count)]
     lane = lax.broadcasted_iota(jnp.int32, (8, RANK), 1)
     sub = lax.broadcasted_iota(jnp.int32, (8, RANK), 0)
+    one = jnp.clip(rows[0], 1.0, 1.0)
+    lefts, rights = [], []
 
     def over_lanes(tile, at):
         return jnp.broadcast_to(tile[:, at : at + 1], (8, RANK))
@@ -55,28 +61,38 @@
     def over_rows(tile, at):
         return jnp.broadcast_to(tile[at : at + 1, :], (8, RANK))
 
-    one = jnp.clip(rows[0], 1.0, 1.0)
-    for k in range(count):
-        panel = rows[k]
-        columns = [over_lanes(panel, 8 * k + t) * one for t in range(8)]
-        inside = (lane >= 8 * k) & (lane < 8 * k + 8)
-        panel = jnp.where(inside, jnp.where(lane - 8 * k == sub, 1.0, 0.0), panel)
-        for s in range(8):
-            pivot = over_rows(1.0 / columns[s], s)
-            factor = jnp.where(sub == s, 0.0, columns[s]) * pivot
-            keep = jnp.where(sub == s, pivot, 1.0)
-            panel = panel * keep - factor * over_rows(panel, s)
-            for t in range(s + 1, 8):
-                columns[t] = columns[t] * keep - factor * over_rows(columns[t], s)
-        leads = [over_rows(panel, s) for s in range(8)]
-        for step in range(count - 1):
-            n = (k + 1 + step) % count
-            terms = [over_lanes(rows[n], 8 * k + s) * leads[s] for s in range(8)]
+    for k in range(count // 2):
+        low = 16 * k
+        inside = (lane >= low) & (lane < low + 16)
+        unit = [jnp.where(lane - low - 8 * h == sub, 1.0, 0.0) for h in range(2)]
+        panel = rows[2 * k : 2 * k + 2]
+        lefts += [jnp.where(lane < low, panel[h], unit[h]) for h in range(2)]
+        columns = [[over_lanes(panel[h], low + t) * one for h in range(2)] for t in range(16)]
+        panel = [jnp.where(inside, unit[h], panel[h]) for h in range(2)]
+        for s in range(16):
+            h, q = divmod(s, 8)
+            pivot = over_rows(1.0 / columns[s][h], q)
+            keep = jnp.where(sub == q, pivot, 1.0)
+            here = jnp.where(sub == q, 0.0, columns[s][h]) * pivot
+            there = columns[s][1 - h] * pivot
+
+            def eliminate(pair):
+                lead = over_rows(pair[h], q)
+                result = [pair[h] * keep - here * lead, pair[1 - h] - there * lead]
+                return result if h == 0 else result[::-1]
+
+            panel = eliminate(panel)
+            for t in range(s + 1, 16):
+                columns[t] = eliminate(columns[t])
+        rights += [jnp.where(lane < low + 16, panel[h], 0.0) for h in range(2)]
+        rows[2 * k : 2 * k + 2] = panel
+        leads = [over_rows(panel[s // 8], s % 8) for s in range(16)]
+        for n in range(2 * k + 2, count):
+            terms = [over_lanes(rows[n], low + s) * leads[s] for s in range(16)]
             while len(terms) > 1:
                 terms = [terms[i] + terms[i + 1] for i in range(0, len(terms), 2)]
             rows[n] = jnp.where(inside, 0.0, rows[n]) - terms[0]
-        rows[k] = panel
-    return jnp.concatenate(rows, axis=0)
+    return across_rows(jnp.concatenate(lefts, axis=0), jnp.concatenate(rights, axis=0))
 
 
 def system_inverse(merged):
@@ -309,7 +325,7 @@
 
     chunk, y = call(
         first_kernel,
-        (coords, block, factor_b, factor_c),
+        [pltpu.with_memory_space_constraint(v, pltpu.HBM) for v in (coords, block, factor_b, factor_c)],
         [(256, RANK), (BI, BJ, RANK)],
         "first",
         1,
@@ -321,7 +337,7 @@
             pltpu.VMEM((64, RANK), F32),
             pltpu.SemaphoreType.DMA((8,)),
         ],
-        pl.ANY,
+        pltpu.HBM,
     )
     got = exchange(chunk, ("ja", "ka"), 32, 8, RANK)
     spread, diagonal = call(collect_first_kernel, (got,), [(384, RANK), (8, RANK)], "collect_a")

time: 123 us -> 118 us (0.959)
  local copies, waits for them, and re-layouts: 3.74 us -> 0.01 us
    unnamed x12 -> x4, local copies, waits for them, and re-layouts: 3.74 us -> 0.01 us
where the time goes in v4:
time: 118 us; the launch traced here: 117 us
  blocking collectives  89.1 us (76%)
  Pallas kernels  17.6 us (15%)
  waiting for transfers between devices  5.83 us (5%)
  starting transfers between devices  3.02 us (3%)
    all_to_all x6, blocking collectives, exchange(): lax.all_to_all(values.reshape(chunk), axes, 0, 0, tiled=True).reshape(shape)  89.1 us
    pallas_call x7, Pallas kernels, call(): pl.pallas_call(kernel, out_shape=[jax.ShapeDtypeStruct(shape, F32) for sh...  17.6 us
    ppermute x3, waiting for transfers between devices, on_device(): lax.ppermute(squares, 'ka', [(n, (n + step) % 4) for n in range(4)])  4.44 us
    ppermute x3, starting transfers between devices, on_device(): lax.ppermute(squares, 'ka', [(n, (n + step) % 4) for n in range(4)])  3.02 us
  transfers between devices with their start and end apart: 4, of which 4 were waited for; matrix products, arithmetic and copies ran while one was open for 0% of the time, Pallas kernels for 0%

profile of v4, /device:TPU:8, one launch (start us, length us, event | category | flops | bytes accessed | tf_op | source)
XLA Modules:
  0.0 117.0 jit_solution(14885834114449916220)
XLA Ops:
  0.6 0.0 copy-start.1
  0.6 3.8 %first.1 = (f32[256,128]{1,0:T(8,128)S(1)}, f32[64,64,128]{2,1,0:T(8,128)S(1)}) custom-call(s32[3]{0:T(128)} %bitcast.31, bf16[64,64,128]{2,1,0:T(8,128)(2,1)} %bitcast.16, f32[256,128]{1,0:T(8,128)} %b_ref.1, f32[512,128]{1,0:T(8,128)} %c_ref.1), custom_call_target="tpu_custom_call" | custom-call | tf_op jit(solution)/shard_map/first/pallas_call | solution.py:305
  4.4 0.0 copy-start
  4.4 21.9 %all_to_all.30 = f32[32,8,128]{2,1,0:T(8,128)S(1)} all-to-all(f32[32,8,128]{2,1,0:T(8,128)S(1)} %bitcast.29), channel_id=1, replica_groups=mesh['iy'=4,'ic'=2,'ja'=8,'ka'=4] {'ja','ka'}, dimensions={0} | all-to-all | bytes 262144 | tf_op jit(solution)/shard_map/all_to_all | solution.py:318
  26.4 14.4 %all_to_all.31 = f32[32,3,4,128]{3,2,1,0:T(4,128)S(1)} all-to-all(f32[32,3,4,128]{3,2,1,0:T(4,128)S(1)} %bitcast.27), channel_id=1, replica_groups=mesh['iy'=4,'ic'=2,'ja'=8,'ka'=4] {'ja','ka'}, dimensions={0} | all-to-all | bytes 393216 | tf_op jit(solution)/shard_map/all_to_all | solution.py:318
  40.8 0.0 copy-done.1
  40.8 4.6 %second.1 = (f32[256,128]{1,0:T(8,128)S(1)}, f32[192,128]{1,0:T(8,128)S(1)}, f32[128,128]{1,0:T(8,128)S(1)}) custom-call(s32[3]{0:T(128)S(1)} %bitcast.32, f32[384,128]{1,0:T(8,128)S(1)} %bitcast.18, f32[8,128]{1,0:T(8,128)S(1)} %get-tuple-element.19.diagonal_ref, f32[64,64,128]{2,1,0:T(8,128)S(1)} %get-tuple-element.20.y_ref), custom_call_target="tpu_custom_call" | custom-call | tf_op jit(solution)/shard_map/second/pallas_call | solution.py:305
  45.4 11.7 %all_to_all.32 = f32[32,3,2,128]{3,2,1,0:T(2,128)S(1)} all-to-all(f32[32,3,2,128]{3,2,1,0:T(2,128)S(1)} %bitcast.30), channel_id=1, replica_groups=mesh['iy'=4,'ic'=2,'ja'=8,'ka'=4] {'iy','ic','ka'}, dimensions={0} | all-to-all | bytes 196608 | tf_op jit(solution)/shard_map/all_to_all | solution.py:318
  57.1 0.1 collect_b.1
  57.2 11.8 %all_to_all.33 = f32[32,3,4,128]{3,2,1,0:T(4,128)S(1)} all-to-all(f32[32,3,4,128]{3,2,1,0:T(4,128)S(1)} %bitcast.19), channel_id=1, replica_groups=mesh['iy'=4,'ic'=2,'ja'=8,'ka'=4] {'iy','ic','ka'}, dimensions={0} | all-to-all | bytes 393216 | tf_op jit(solution)/shard_map/all_to_all | solution.py:318
  69.1 0.0 copy-done
  69.1 5.2 %third.1 = (f32[256,128]{1,0:T(8,128)}, f32[256,128]{1,0:T(8,128)S(1)}, f32[256,128]{1,0:T(8,128)S(1)}, f32[128,128]{1,0:T(8,128)S(1)}) custom-call(s32[3]{0:T(128)S(1)} %bitcast.33, f32[384,128]{1,0:T(8,128)S(1)} %bitcast.20, f32[128,128]{1,0:T(8,128)S(1)} %get-tuple-element.22.gram_c_ref, f32[256,128]{1,0:T(8,128)S(1)} %get-tuple-element.23.solved_a_ref, ...), custom_call_target="tpu_custom_call" | custom-call | tf_op jit(solution)/shard_map/third/pallas_call | solution.py:305
  74.3 15.0 %all_to_all.34 = f32[64,4,128]{2,1,0:T(4,128)S(1)} all-to-all(f32[64,4,128]{2,1,0:T(4,128)S(1)} %bitcast.28), channel_id=1, replica_groups=mesh['iy'=4,'ic'=2,'ja'=8,'ka'=4] {'iy','ic','ja'}, dimensions={0} | all-to-all | bytes 262144 | tf_op jit(solution)/shard_map/all_to_all | solution.py:318
  89.3 0.1 collect_c.1
  89.4 14.2 %all_to_all.35 = f32[32,5,2,128]{3,2,1,0:T(2,128)S(1)} all-to-all(f32[32,5,2,128]{3,2,1,0:T(2,128)S(1)} %bitcast.23), channel_id=1, replica_groups=mesh['iy'=4,'ic'=2,'ja'=8,'ka'=4] {'iy','ja'}, dimensions={0} | all-to-all | bytes 327680 | tf_op jit(solution)/shard_map/all_to_all | solution.py:318
  103.6 0.0 collective-permute-start
  103.6 1.4 %collective-permute-done.other_ref = f32[320,128]{1,0:T(8,128)S(1)} collective-permute-done((f32[320,128]{1,0:T(8,128)S(1)}, f32[320,128]{1,0:T(8,128)S(1)}, u32[]{:S(2)}, u32[]{:S(2)}) %collective-permute-start) | collective-permute-done | bytes 163872 | tf_op jit(solution)/shard_map/ppermute | solution.py:364
  105.0 3.8 %fourth.1 = (f32[256,128]{1,0:T(8,128)}, f32[512,128]{1,0:T(8,128)S(1)}, f32[1,128]{1,0:T(1,128)S(1)}) custom-call(f32[320,128]{1,0:T(8,128)S(1)} %bitcast.22, f32[320,128]{1,0:T(8,128)S(1)} %collective-permute-done.other_ref, f32[128,128]{1,0:T(8,128)S(1)} %get-tuple-element.26.gram_a_ref, f32[256,128]{1,0:T(8,128)S(1)} %get-tuple-element.27.solved_b_ref), custom_call_target="tpu_custom_call" | custom-call | tf_op jit(solution)/shard_map/fourth/pallas_call | solution.py:305
  108.8 1.8 %collective-permute-start.3 = (f32[1,128]{1,0:T(1,128)S(1)}, f32[1,128]{1,0:T(1,128)S(1)}, u32[]{:S(2)}, u32[]{:S(2)}) collective-permute-start(f32[1,128]{1,0:T(1,128)S(1)} %get-tuple-element.30), channel_id=1, source_target_pairs={{0,3},{1,0},{2,1},{3,2},{4,7},{5,4},{6,5},{7,6},{8,11},{9,8},{10,9... | collective-permute-start | bytes 1544 | tf_op jit(solution)/shard_map/ppermute | solution.py:376
  110.6 0.9 collective-permute-start.2
  111.5 0.3 collective-permute-start.1
  111.8 0.6 collective-permute-done.3
  112.4 3.2 %collective-permute-done.2 = f32[1,128]{1,0:T(1,128)S(1)} collective-permute-done((f32[1,128]{1,0:T(1,128)S(1)}, f32[1,128]{1,0:T(1,128)S(1)}, u32[]{:S(2)}, u32[]{:S(2)}) %collective-permute-start.2) | collective-permute-done | bytes 544 | tf_op jit(solution)/shard_map/ppermute | solution.py:376
  115.6 0.6 collective-permute-done.1
  116.3 0.7 broadcast_multiply_fusion
  (2 shorter events, 0.1 us)
Async XLA Ops:
  0.6 40.2 %copy-start.1 = (s32[3,1]{0,1:T(1,128)S(1)}, s32[3,1]{0,1:T(1,128)}, u32[]{:S(2)}) copy-start(s32[3,1]{0,1:T(1,128)} %param.6) | copy-start | bytes 40
  4.4 64.7 %copy-start = (bf16[1,64,64,128]{3,2,1,0:T(8,128)(2,1)S(1)}, bf16[1,64,64,128]{3,2,1,0:T(8,128)(2,1)}, u32[]{:S(2)}) copy-start(bf16[1,64,64,128]{3,2,1,0:T(8,128)(2,1)} %param.5) | copy-start | bytes 3145732
  103.6 1.4 %collective-permute-start = (f32[320,128]{1,0:T(8,128)S(1)}, f32[320,128]{1,0:T(8,128)S(1)}, u32[]{:S(2)}, u32[]{:S(2)}) collective-permute-start(f32[320,128]{1,0:T(8,128)S(1)} %bitcast.21), channel_id=1, source_target_pairs={{0,32},{32,0},{1,33},{33,1},{2,34},{34,2},{3,35},{35,3},{4,36},{36... | collective-permute-start | bytes 491528 | tf_op jit(solution)/shard_map/ppermute | solution.py:364
  108.8 3.6 %collective-permute-start.3 = (f32[1,128]{1,0:T(1,128)S(1)}, f32[1,128]{1,0:T(1,128)S(1)}, u32[]{:S(2)}, u32[]{:S(2)}) collective-permute-start(f32[1,128]{1,0:T(1,128)S(1)} %get-tuple-element.30), channel_id=1, source_target_pairs={{0,3},{1,0},{2,1},{3,2},{4,7},{5,4},{6,5},{7,6},{8,11},{9,8},{10,9... | collective-permute-start | bytes 1544 | tf_op jit(solution)/shard_map/ppermute | solution.py:376
  110.6 5.1 %collective-permute-start.2 = (f32[1,128]{1,0:T(1,128)S(1)}, f32[1,128]{1,0:T(1,128)S(1)}, u32[]{:S(2)}, u32[]{:S(2)}) collective-permute-start(f32[1,128]{1,0:T(1,128)S(1)} %get-tuple-element.30), channel_id=1, source_target_pairs={{0,2},{1,3},{2,0},{3,1},{4,6},{5,7},{6,4},{7,5},{8,10},{9,11},{10,... | collective-permute-start | bytes 1544 | tf_op jit(solution)/shard_map/ppermute | solution.py:376
  111.5 4.8 %collective-permute-start.1 = (f32[1,128]{1,0:T(1,128)S(1)}, f32[1,128]{1,0:T(1,128)S(1)}, u32[]{:S(2)}, u32[]{:S(2)}) collective-permute-start(f32[1,128]{1,0:T(1,128)S(1)} %get-tuple-element.30), channel_id=1, source_target_pairs={{0,1},{1,2},{2,3},{3,0},{4,5},{5,6},{6,7},{7,4},{8,9},{9,10},{10,1... | collective-permute-start | bytes 1544 | tf_op jit(solution)/shard_map/ppermute | solution.py:376

commit v5 on v4

--- a/solution.py
+++ b/solution.py
@@ -217,9 +217,21 @@
     diagonal_ref[...] = jnp.broadcast_to(rows[12], (8, RANK))
 
 
-def collect_second_kernel(got_ref, spread_ref):
-    rows = collect(got_ref, 32, 6, lower_lanes(strided(got_ref, 5, 32, 6)), 4)
-    repeat_rows(spread_ref, rows, 32)
+def collect_second_kernel(got_ref, half_ref):
+    sums = [jnp.zeros((32, RANK), F32) for _ in range(SLOTS)]
+    for n in range(16):
+        for part in range(2):
+            start = 88 * n + 32 * part
+            rows = got_ref[start : start + 32, :]
+            ids = got_ref[88 * n + 80 + part : 88 * n + 81 + part, :]
+            for slot in range(SLOTS):
+                sums[slot] = sums[slot] + jnp.where(ids == slot, rows, 0.0)
+    for slot in range(SLOTS):
+        half_ref[32 * slot : 32 * slot + 32, :] = sums[slot]
+    for share in range(4):
+        starts = [88 * (4 * n + share) + 64 for n in range(4)]
+        total = [got_ref[start : start + 16, :] for start in starts]
+        half_ref[128 + 16 * share : 144 + 16 * share, :] = (total[0] + total[1]) + (total[2] + total[3])
 
 
 def collect_third_kernel(got_ref, spread_ref):
@@ -231,7 +243,10 @@
     return jnp.concatenate([strided(got_ref, t, count, step) for t in range(first, last)], axis=0)
 
 
-def second_kernel(coords_ref, got_ref, diagonal_ref, y_ref, solved_ref, chunk_ref, gram_c_ref):
+def second_kernel(
+    coords_ref, got_ref, diagonal_ref, y_ref,
+    solved_ref, gram_c_ref, keep_ref, send_ref, partial_ref, raw_ref,
+):
     at, slot = places(coords_ref)
     packed = natural(got_ref, 32, 12, 8, 12)
     flipped = packed.T
@@ -241,30 +256,50 @@
     gram_c = jnp.where(row == col, diagonal_ref[0:1, :], gram_c)
     gram_c_ref[...] = gram_c
     solver = system_inverse(gram_b * gram_c)
-    solved_ref[...] = exact_dot(natural(got_ref, 32, 12, 0, 8), solver)
-    raw = gram(some_rows(solved_ref, at[2], 64)) * (1.0 / ROWS)
+    solved = exact_dot(natural(got_ref, 32, 12, 0, 8), solver)
+    solved_ref[...] = solved
+    raw_ref[...] = gram(solved) * (1.0 / ROWS)
     own = some_rows(solved_ref, slot[0], BI)
     sums = [jnp.zeros((BJ, RANK), F32) for _ in range(2)]
     for n in range(BI):
         sums[n % 2] = sums[n % 2] + own[n : n + 1, :] * y_ref[n]
-    partial = sums[0] + sums[1]
-    for t in range(2):
-        put(chunk_ref, t, 32, 6, partial[32 * t : 32 * t + 32])
-    for t in range(4):
-        rows = raw[32 * t : 32 * t + 32]
-        put(chunk_ref, 2 + t, 32, 6, rows if t < 2 else mark(rows, slot[1]))
+    partial_ref[...] = sums[0] + sums[1]
+    core = lax.axis_index("ic")
+    for ref, half in ((keep_ref, core), (send_ref, 1 - core)):
+        ref[0:32, :] = some_rows(partial_ref, half, 32)
+        ref[32:48, :] = some_rows(raw_ref, 4 * half + at[2], 16)
+        ref[48:56, :] = jnp.full((8, RANK), slot[1].astype(F32))
+
+
+def merge_kernel(keep_ref, other_ref, spread_ref):
+    first = lax.broadcasted_iota(jnp.int32, (8, RANK), 0) == 0
+    tile = [
+        keep_ref[0:32, :],
+        other_ref[0:32, :],
+        keep_ref[32:48, :] + other_ref[32:48, :],
+        jnp.where(first, keep_ref[48:56, :], other_ref[48:56, :]),
+    ]
+    tile = jnp.concatenate(tile, axis=0)
+    for n in range(16):
+        spread_ref[88 * n : 88 * n + 88, :] = tile
 
 
 def third_kernel(
-    coords_ref, got_ref, gram_c_ref, solved_a_ref, block_ref,
-    loading_a_ref, solved_ref, chunk_ref, gram_a_ref, khatri_ref,
+    coords_ref, same_ref, other_ref, gram_c_ref, solved_a_ref, block_ref,
+    loading_a_ref, solved_ref, chunk_ref, gram_a_ref, khatri_ref, rows_ref,
 ):
     at, slot = places(coords_ref)
-    scale, gram_a = scaled_gram(unmark(natural(got_ref, 32, 12, 8, 12)))
+    core = lax.axis_index("ic")
+    for ref, half in ((same_ref, core), (other_ref, 1 - core)):
+        for n in range(SLOTS):
+            place = pl.multiple_of(64 * n + 32 * half, 32)
+            rows_ref[pl.ds(place, 32), :] = ref[32 * n : 32 * n + 32, :]
+        rows_ref[pl.ds(pl.multiple_of(256 + 64 * half, 64), 64), :] = ref[128:192, :]
+    scale, gram_a = scaled_gram(rows_ref[256:384, :])
     gram_a_ref[...] = gram_a
     loading_a_ref[...] = solved_a_ref[...] * scale
     solver = system_inverse(gram_a * gram_c_ref[...])
-    solved_ref[...] = exact_dot(natural(got_ref, 32, 12, 0, 8) * scale, solver)
+    solved_ref[...] = exact_dot(rows_ref[0:256, :] * scale, solver)
     raw = gram(some_rows(solved_ref, at[0], 32)) * (1.0 / ROWS)
     own_a = some_rows(loading_a_ref, slot[0], BI)
     own_b = some_rows(solved_ref, slot[1], BJ)
@@ -318,6 +353,10 @@
     return lax.all_to_all(values.reshape(chunk), axes, 0, 0, tiled=True).reshape(shape)
 
 
+def swap_cores(values):
+    return lax.ppermute(values, "ic", [(0, 1), (1, 0)])
+
+
 def on_device(blocks, coords, live, factor_b, factor_c):
     block = blocks[0]
     coords = coords.reshape(3)
@@ -343,25 +382,30 @@
     spread, diagonal = call(collect_first_kernel, (got,), [(384, RANK), (8, RANK)], "collect_a")
     got = exchange(spread, ("ja", "ka"), 32, 3, 4, RANK)
 
-    solved_a, chunk, gram_c = call(
-        second_kernel, (coords, got, diagonal, y), [(256, RANK), (192, RANK), full], "second", 1
-    )
-    got = exchange(chunk, (*IA, "ka"), 32, 3, 2, RANK)
-    (spread,) = call(collect_second_kernel, (got,), [(384, RANK)], "collect_b")
-    got = exchange(spread, (*IA, "ka"), 32, 3, 4, RANK)
+    solved_a, gram_c, keep, send = call(
+        second_kernel,
+        (coords, got, diagonal, y),
+        [(256, RANK), full, (56, RANK), (56, RANK)],
+        "second",
+        1,
+        [pltpu.VMEM((BJ, RANK), F32), pltpu.VMEM(full, F32)],
+    )
+    (spread,) = call(merge_kernel, (keep, swap_cores(send)), [(1408, RANK)], "merge")
+    got = exchange(spread, ("iy", "ka"), 16, 88, RANK)
+    (half,) = call(collect_second_kernel, (got,), [(192, RANK)], "collect_b")
 
     loading_a, solved_b, chunk, gram_a = call(
         third_kernel,
-        (coords, got, gram_c, solved_a, block),
+        (coords, half, swap_cores(half), gram_c, solved_a, block),
         [(256, RANK), (256, RANK), (256, RANK), full],
         "third",
         1,
-        [pltpu.VMEM((BI * BJ, RANK), BF16)],
+        [pltpu.VMEM((BI * BJ, RANK), BF16), pltpu.VMEM((384, RANK), F32)],
     )
     got = exchange(chunk, (*IA, "ja"), 64, 4, RANK)
     (spread,) = call(collect_third_kernel, (got,), [(320, RANK)], "collect_c")
     same = exchange(spread, ("iy", "ja"), 32, 5, 2, RANK)
-    other = lax.ppermute(same, "ic", [(0, 1), (1, 0)])
+    other = swap_cores(same)
 
     loading_b, solved_c, squares = call(
         fourth_kernel,

time: 118 us -> 115 us (0.975)
  blocking collectives: 89.1 us -> 83.2 us
  waiting for transfers between devices: 5.83 us -> 8.64 us
    all_to_all x6 -> x5, blocking collectives: 89.1 us -> 83.2 us  [exchange(): lax.all_to_all(values.reshape(chunk), axes, 0, 0, tiled=True).reshape(shape)]
    ppermute x1 -> x3, waiting for transfers between devices: 1.39 us -> 3.87 us  [swap_cores(): return lax.ppermute(values, 'ic', [(0, 1), (1, 0)])]
    pallas_call x7 -> x8, Pallas kernels: 17.6 us -> 17.8 us  [call(): pl.pallas_call(kernel, out_shape=[jax.ShapeDtypeStruct(shape, F32) for sh...]
  transfers between devices with their start and end apart: 4 -> 6, of which waited for: 4 -> 6; matrix products, arithmetic and copies ran while one was open for 0% -> 0% of each run, Pallas kernels for 0% -> 0%
where the time goes in v5:
time: 115 us; the launch traced here: 114 us
  blocking collectives  83.2 us (72%)
  Pallas kernels  17.8 us (15%)
  waiting for transfers between devices  8.64 us (8%)
  starting transfers between devices  2.89 us (3%)
    all_to_all x5, blocking collectives, exchange(): lax.all_to_all(values.reshape(chunk), axes, 0, 0, tiled=True).reshape(shape)  83.2 us
    pallas_call x8, Pallas kernels, call(): pl.pallas_call(kernel, out_shape=[jax.ShapeDtypeStruct(shape, F32) for sh...  17.8 us
    ppermute x3, waiting for transfers between devices, on_device(): lax.ppermute(squares, 'ka', [(n, (n + step) % 4) for n in range(4)])  4.78 us
    ppermute x3, waiting for transfers between devices, swap_cores(): return lax.ppermute(values, 'ic', [(0, 1), (1, 0)])  3.87 us
    ppermute x3, starting transfers between devices, on_device(): lax.ppermute(squares, 'ka', [(n, (n + step) % 4) for n in range(4)])  2.71 us
  transfers between devices with their start and end apart: 6, of which 6 were waited for; matrix products, arithmetic and copies ran while one was open for 0% of the time, Pallas kernels for 0%

profile of v5, /device:TPU:8, one launch (start us, length us, event | category | flops | bytes accessed | tf_op | source)
XLA Modules:
  0.0 114.0 jit_solution(7401356252220283808)
XLA Ops:
  0.6 0.0 copy-start.1
  0.6 3.8 %first.1 = (f32[256,128]{1,0:T(8,128)S(1)}, f32[64,64,128]{2,1,0:T(8,128)S(1)}) custom-call(s32[3]{0:T(128)} %bitcast.27, bf16[64,64,128]{2,1,0:T(8,128)(2,1)} %bitcast.14, f32[256,128]{1,0:T(8,128)} %b_ref.1, f32[512,128]{1,0:T(8,128)} %c_ref.1), custom_call_target="tpu_custom_call" | custom-call | tf_op jit(solution)/shard_map/first/pallas_call | solution.py:340
  4.4 21.6 %all_to_all.25 = f32[32,8,128]{2,1,0:T(8,128)S(1)} all-to-all(f32[32,8,128]{2,1,0:T(8,128)S(1)} %bitcast.26), channel_id=1, replica_groups=mesh['iy'=4,'ic'=2,'ja'=8,'ka'=4] {'ja','ka'}, dimensions={0} | all-to-all | bytes 262144 | tf_op jit(solution)/shard_map/all_to_all | solution.py:353
  26.0 14.5 %all_to_all.26 = f32[32,3,4,128]{3,2,1,0:T(4,128)S(1)} all-to-all(f32[32,3,4,128]{3,2,1,0:T(4,128)S(1)} %bitcast.24), channel_id=1, replica_groups=mesh['iy'=4,'ic'=2,'ja'=8,'ka'=4] {'ja','ka'}, dimensions={0} | all-to-all | bytes 393216 | tf_op jit(solution)/shard_map/all_to_all | solution.py:353
  40.5 0.0 copy-done.1
  40.5 4.7 %second.1 = (f32[256,128]{1,0:T(8,128)S(1)}, f32[128,128]{1,0:T(8,128)S(1)}, f32[56,128]{1,0:T(8,128)S(1)}, f32[56,128]{1,0:T(8,128)S(1)}) custom-call(s32[3]{0:T(128)S(1)} %bitcast.28, f32[384,128]{1,0:T(8,128)S(1)} %bitcast.18, f32[8,128]{1,0:T(8,128)S(1)} %get-tuple-element.20.diagonal_ref, f32[64,64,128]{2,1,0:T(8,128)S(1)} %get-tuple-element.21.y_ref), custom_call_target="tpu_custom_call" | custom-call | tf_op jit(solution)/shard_map/second/pallas_call | solution.py:340
  45.2 0.0 copy-start
  45.2 0.1 collective-permute-start
  45.3 1.2 %collective-permute-done.other_ref = f32[56,128]{1,0:T(8,128)S(1)} collective-permute-done((f32[56,128]{1,0:T(8,128)S(1)}, f32[56,128]{1,0:T(8,128)S(1)}, u32[]{:S(2)}, u32[]{:S(2)}) %collective-permute-start) | collective-permute-done | bytes 28704 | tf_op jit(solution)/shard_map/ppermute | solution.py:357
  46.6 17.4 %all_to_all.27 = f32[16,88,128]{2,1,0:T(8,128)S(1)} all-to-all(f32[16,88,128]{2,1,0:T(8,128)S(1)} %bitcast.16), channel_id=1, replica_groups=mesh['iy'=4,'ic'=2,'ja'=8,'ka'=4] {'iy','ka'}, dimensions={0} | all-to-all | bytes 1441792 | tf_op jit(solution)/shard_map/all_to_all | solution.py:353
  64.0 0.3 collect_b.1.same_ref
  64.2 0.1 collective-permute-start.1
  64.3 1.3 %collective-permute-done.1.other_ref = f32[192,128]{1,0:T(8,128)S(1)} collective-permute-done((f32[192,128]{1,0:T(8,128)S(1)}, f32[192,128]{1,0:T(8,128)S(1)}, u32[]{:S(2)}, u32[]{:S(2)}) %collective-permute-start.1) | collective-permute-done | bytes 98336 | tf_op jit(solution)/shard_map/ppermute | solution.py:357
  65.6 0.0 copy-done
  65.6 5.1 %third.1 = (f32[256,128]{1,0:T(8,128)}, f32[256,128]{1,0:T(8,128)S(1)}, f32[256,128]{1,0:T(8,128)S(1)}, f32[128,128]{1,0:T(8,128)S(1)}) custom-call(s32[3]{0:T(128)S(1)} %bitcast.29, f32[192,128]{1,0:T(8,128)S(1)} %collect_b.1.same_ref, f32[192,128]{1,0:T(8,128)S(1)} %collective-permute-done.1.other_ref, f32[128,128]{1,0:T(8,128)S(1)} %get-tuple-element.24.gram_c_ref, ...), custom_call_target="tpu_custom_call" | custom-call | tf_op jit(solution)/shard_map/third/pallas_call | solution.py:340
  70.7 15.6 %all_to_all.28 = f32[64,4,128]{2,1,0:T(4,128)S(1)} all-to-all(f32[64,4,128]{2,1,0:T(4,128)S(1)} %bitcast.25), channel_id=1, replica_groups=mesh['iy'=4,'ic'=2,'ja'=8,'ka'=4] {'iy','ic','ja'}, dimensions={0} | all-to-all | bytes 262144 | tf_op jit(solution)/shard_map/all_to_all | solution.py:353
  86.3 0.1 collect_c.1
  86.4 14.2 %all_to_all.29 = f32[32,5,2,128]{3,2,1,0:T(2,128)S(1)} all-to-all(f32[32,5,2,128]{3,2,1,0:T(2,128)S(1)} %bitcast.21), channel_id=1, replica_groups=mesh['iy'=4,'ic'=2,'ja'=8,'ka'=4] {'iy','ja'}, dimensions={0} | all-to-all | bytes 327680 | tf_op jit(solution)/shard_map/all_to_all | solution.py:353
  100.6 0.0 collective-permute-start.2
  100.6 1.4 %collective-permute-done.2.other_ref = f32[320,128]{1,0:T(8,128)S(1)} collective-permute-done((f32[320,128]{1,0:T(8,128)S(1)}, f32[320,128]{1,0:T(8,128)S(1)}, u32[]{:S(2)}, u32[]{:S(2)}) %collective-permute-start.2) | collective-permute-done | bytes 163872 | tf_op jit(solution)/shard_map/ppermute | solution.py:357
  102.0 3.8 %fourth.1 = (f32[256,128]{1,0:T(8,128)}, f32[512,128]{1,0:T(8,128)S(1)}, f32[1,128]{1,0:T(1,128)S(1)}) custom-call(f32[320,128]{1,0:T(8,128)S(1)} %bitcast.20, f32[320,128]{1,0:T(8,128)S(1)} %collective-permute-done.2.other_ref, f32[128,128]{1,0:T(8,128)S(1)} %get-tuple-element.28.gram_a_ref, f32[256,128]{1,0:T(8,128)S(1)} %get-tuple-element.29.solved_b_ref), custom_call_target="tpu_custom_call" | custom-call | tf_op jit(solution)/shard_map/fourth/pallas_call | solution.py:340
  105.8 1.1 collective-permute-start.5
  106.8 1.7 %collective-permute-start.4 = (f32[1,128]{1,0:T(1,128)S(1)}, f32[1,128]{1,0:T(1,128)S(1)}, u32[]{:S(2)}, u32[]{:S(2)}) collective-permute-start(f32[1,128]{1,0:T(1,128)S(1)} %get-tuple-element.32), channel_id=1, source_target_pairs={{0,2},{1,3},{2,0},{3,1},{4,6},{5,7},{6,4},{7,5},{8,10},{9,11},{10,... | collective-permute-start | bytes 1544 | tf_op jit(solution)/shard_map/ppermute | solution.py:420
  108.5 0.0 collective-permute-start.3
  108.5 0.9 collective-permute-done.5
  109.4 2.5 %collective-permute-done.4 = f32[1,128]{1,0:T(1,128)S(1)} collective-permute-done((f32[1,128]{1,0:T(1,128)S(1)}, f32[1,128]{1,0:T(1,128)S(1)}, u32[]{:S(2)}, u32[]{:S(2)}) %collective-permute-start.4) | collective-permute-done | bytes 544 | tf_op jit(solution)/shard_map/ppermute | solution.py:420
  111.9 1.4 %collective-permute-done.3 = f32[1,128]{1,0:T(1,128)S(1)} collective-permute-done((f32[1,128]{1,0:T(1,128)S(1)}, f32[1,128]{1,0:T(1,128)S(1)}, u32[]{:S(2)}, u32[]{:S(2)}) %collective-permute-start.3) | collective-permute-done | bytes 544 | tf_op jit(solution)/shard_map/ppermute | solution.py:420
  113.3 0.7 broadcast_multiply_fusion
  (3 shorter events, 0.1 us)
Async XLA Ops:
  0.6 39.9 %copy-start.1 = (s32[3,1]{0,1:T(1,128)S(1)}, s32[3,1]{0,1:T(1,128)}, u32[]{:S(2)}) copy-start(s32[3,1]{0,1:T(1,128)} %param.6) | copy-start | bytes 40
  45.2 20.4 %copy-start = (bf16[1,64,64,128]{3,2,1,0:T(8,128)(2,1)S(1)}, bf16[1,64,64,128]{3,2,1,0:T(8,128)(2,1)}, u32[]{:S(2)}) copy-start(bf16[1,64,64,128]{3,2,1,0:T(8,128)(2,1)} %param.5) | copy-start | bytes 3145732
  45.2 1.3 %collective-permute-start = (f32[56,128]{1,0:T(8,128)S(1)}, f32[56,128]{1,0:T(8,128)S(1)}, u32[]{:S(2)}, u32[]{:S(2)}) collective-permute-start(f32[56,128]{1,0:T(8,128)S(1)} %get-tuple-element.23), channel_id=1, source_target_pairs={{0,32},{32,0},{1,33},{33,1},{2,34},{34,2},{3,35},{35,3},{4,36},{36... | collective-permute-start | bytes 86024 | tf_op jit(solution)/shard_map/ppermute | solution.py:357
  64.2 1.4 %collective-permute-start.1 = (f32[192,128]{1,0:T(8,128)S(1)}, f32[192,128]{1,0:T(8,128)S(1)}, u32[]{:S(2)}, u32[]{:S(2)}) collective-permute-start(f32[192,128]{1,0:T(8,128)S(1)} %collect_b.1.same_ref), channel_id=1, source_target_pairs={{0,32},{32,0},{1,33},{33,1},{2,34},{34,2},{3,35},{35,3},{4,36},{36... | collective-permute-start | bytes 294920 | tf_op jit(solution)/shard_map/ppermute | solution.py:357
  100.6 1.4 %collective-permute-start.2 = (f32[320,128]{1,0:T(8,128)S(1)}, f32[320,128]{1,0:T(8,128)S(1)}, u32[]{:S(2)}, u32[]{:S(2)}) collective-permute-start(f32[320,128]{1,0:T(8,128)S(1)} %bitcast.19), channel_id=1, source_target_pairs={{0,32},{32,0},{1,33},{33,1},{2,34},{34,2},{3,35},{35,3},{4,36},{36... | collective-permute-start | bytes 491528 | tf_op jit(solution)/shard_map/ppermute | solution.py:357
  105.8 3.6 %collective-permute-start.5 = (f32[1,128]{1,0:T(1,128)S(1)}, f32[1,128]{1,0:T(1,128)S(1)}, u32[]{:S(2)}, u32[]{:S(2)}) collective-permute-start(f32[1,128]{1,0:T(1,128)S(1)} %get-tuple-element.32), channel_id=1, source_target_pairs={{0,3},{1,0},{2,1},{3,2},{4,7},{5,4},{6,5},{7,6},{8,11},{9,8},{10,9... | collective-permute-start | bytes 1544 | tf_op jit(solution)/shard_map/ppermute | solution.py:420
  106.8 5.1 %collective-permute-start.4 = (f32[1,128]{1,0:T(1,128)S(1)}, f32[1,128]{1,0:T(1,128)S(1)}, u32[]{:S(2)}, u32[]{:S(2)}) collective-permute-start(f32[1,128]{1,0:T(1,128)S(1)} %get-tuple-element.32), channel_id=1, source_target_pairs={{0,2},{1,3},{2,0},{3,1},{4,6},{5,7},{6,4},{7,5},{8,10},{9,11},{10,... | collective-permute-start | bytes 1544 | tf_op jit(solution)/shard_map/ppermute | solution.py:420
  108.5 4.8 %collective-permute-start.3 = (f32[1,128]{1,0:T(1,128)S(1)}, f32[1,128]{1,0:T(1,128)S(1)}, u32[]{:S(2)}, u32[]{:S(2)}) collective-permute-start(f32[1,128]{1,0:T(1,128)S(1)} %get-tuple-element.32), channel_id=1, source_target_pairs={{0,1},{1,2},{2,3},{3,0},{4,5},{5,6},{6,7},{7,4},{8,9},{9,10},{10,1... | collective-permute-start | bytes 1544 | tf_op jit(solution)/shard_map/ppermute | solution.py:420

commit v6 on v5

--- a/solution.py
+++ b/solution.py
@@ -217,23 +217,6 @@
     diagonal_ref[...] = jnp.broadcast_to(rows[12], (8, RANK))
 
 
-def collect_second_kernel(got_ref, half_ref):
-    sums = [jnp.zeros((32, RANK), F32) for _ in range(SLOTS)]
-    for n in range(16):
-        for part in range(2):
-            start = 88 * n + 32 * part
-            rows = got_ref[start : start + 32, :]
-            ids = got_ref[88 * n + 80 + part : 88 * n + 81 + part, :]
-            for slot in range(SLOTS):
-                sums[slot] = sums[slot] + jnp.where(ids == slot, rows, 0.0)
-    for slot in range(SLOTS):
-        half_ref[32 * slot : 32 * slot + 32, :] = sums[slot]
-    for share in range(4):
-        starts = [88 * (4 * n + share) + 64 for n in range(4)]
-        total = [got_ref[start : start + 16, :] for start in starts]
-        half_ref[128 + 16 * share : 144 + 16 * share, :] = (total[0] + total[1]) + (total[2] + total[3])
-
-
 def collect_third_kernel(got_ref, spread_ref):
     rows = collect(got_ref, 64, 4, lower_lanes(strided(got_ref, 3, 64, 4)), 2)
     repeat_rows(spread_ref, rows, 32)
@@ -267,21 +250,44 @@
     core = lax.axis_index("ic")
     for ref, half in ((keep_ref, core), (send_ref, 1 - core)):
         ref[0:32, :] = some_rows(partial_ref, half, 32)
-        ref[32:48, :] = some_rows(raw_ref, 4 * half + at[2], 16)
-        ref[48:56, :] = jnp.full((8, RANK), slot[1].astype(F32))
-
-
-def merge_kernel(keep_ref, other_ref, spread_ref):
+        ref[32:96, :] = some_rows(raw_ref, half, 64)
+        ref[96:104, :] = jnp.full((8, RANK), slot[1].astype(F32))
+
+
+def merge_kernel(keep_ref, other_ref, parts_ref, gram_ref):
     first = lax.broadcasted_iota(jnp.int32, (8, RANK), 0) == 0
-    tile = [
-        keep_ref[0:32, :],
-        other_ref[0:32, :],
-        keep_ref[32:48, :] + other_ref[32:48, :],
-        jnp.where(first, keep_ref[48:56, :], other_ref[48:56, :]),
-    ]
-    tile = jnp.concatenate(tile, axis=0)
-    for n in range(16):
-        spread_ref[88 * n : 88 * n + 88, :] = tile
+    parts_ref[0:32, :] = keep_ref[0:32, :]
+    parts_ref[32:64, :] = other_ref[0:32, :]
+    parts_ref[64:72, :] = jnp.where(first, keep_ref[96:104, :], other_ref[96:104, :])
+    gram_ref[...] = keep_ref[32:96, :] + other_ref[32:96, :]
+
+
+def in_source_order(axis, refs, all_ref):
+    size = refs[0].shape[0]
+    me = lax.axis_index(axis)
+    for step, ref in enumerate(refs):
+        source = lax.rem(me + 4 - step, 4)
+        all_ref[pl.ds(pl.multiple_of(source * size, 8), size), :] = ref[...]
+
+
+def dense_kernel(parts_0, parts_1, parts_2, parts_3, gram_ref, half_ref, all_ref):
+    in_source_order("ka", (parts_0, parts_1, parts_2, parts_3), all_ref)
+    sums = [jnp.zeros((32, RANK), F32) for _ in range(SLOTS)]
+    for n in range(4):
+        for part in range(2):
+            rows = all_ref[72 * n + 32 * part : 72 * n + 32 * part + 32, :]
+            ids = all_ref[72 * n + 64 + part : 72 * n + 65 + part, :]
+            for slot in range(SLOTS):
+                sums[slot] = sums[slot] + jnp.where(ids == slot, rows, 0.0)
+    for slot in range(SLOTS):
+        half_ref[32 * slot : 32 * slot + 32, :] = sums[slot]
+    half_ref[128:192, :] = gram_ref[...]
+
+
+def sum_kernel(half_0, half_1, half_2, half_3, sum_ref, all_ref):
+    in_source_order("iy", (half_0, half_1, half_2, half_3), all_ref)
+    parts = [all_ref[192 * n : 192 * n + 192, :] for n in range(4)]
+    sum_ref[...] = (parts[0] + parts[1]) + (parts[2] + parts[3])
 
 
 def third_kernel(
@@ -357,6 +363,12 @@
     return lax.ppermute(values, "ic", [(0, 1), (1, 0)])
 
 
+def around(axis, values):
+    return [
+        lax.ppermute(values, axis, [(n, (n + step) % 4) for n in range(4)]) for step in (1, 2, 3)
+    ]
+
+
 def on_device(blocks, coords, live, factor_b, factor_c):
     block = blocks[0]
     coords = coords.reshape(3)
@@ -385,14 +397,30 @@
     solved_a, gram_c, keep, send = call(
         second_kernel,
         (coords, got, diagonal, y),
-        [(256, RANK), full, (56, RANK), (56, RANK)],
+        [(256, RANK), full, (104, RANK), (104, RANK)],
         "second",
         1,
         [pltpu.VMEM((BJ, RANK), F32), pltpu.VMEM(full, F32)],
     )
-    (spread,) = call(merge_kernel, (keep, swap_cores(send)), [(1408, RANK)], "merge")
-    got = exchange(spread, ("iy", "ka"), 16, 88, RANK)
-    (half,) = call(collect_second_kernel, (got,), [(192, RANK)], "collect_b")
+    parts, gram_half = call(
+        merge_kernel, (keep, swap_cores(send)), [(72, RANK), (64, RANK)], "merge"
+    )
+    (half,) = call(
+        dense_kernel,
+        (parts, *around("ka", parts), gram_half),
+        [(192, RANK)],
+        "dense",
+        0,
+        [pltpu.VMEM((288, RANK), F32)],
+    )
+    (half,) = call(
+        sum_kernel,
+        (half, *around("iy", half)),
+        [(192, RANK)],
+        "sum",
+        0,
+        [pltpu.VMEM((768, RANK), F32)],
+    )
 
     loading_a, solved_b, chunk, gram_a = call(
         third_kernel,
@@ -415,9 +443,7 @@
         0,
         [pltpu.VMEM((640, RANK), F32)],
     )
-    total = squares
-    for step in (1, 2, 3):
-        total = total + lax.ppermute(squares, "ka", [(n, (n + step) % 4) for n in range(4)])
+    total = squares + sum(around("ka", squares))
     loading_c = solved_c * lax.rsqrt(total / ROWS + EPSILON)
     return (loading_a, loading_b, loading_c)
 

time: 115 us -> 113 us (0.983)
  blocking collectives: 83.2 us -> 66.9 us
  starting transfers between devices: 2.89 us -> 10.6 us
  waiting for transfers between devices: 8.64 us -> 15.8 us
    all_to_all x5 -> x4, blocking collectives: 83.2 us -> 66.9 us  [exchange(): lax.all_to_all(values.reshape(chunk), axes, 0, 0, tiled=True).reshape(shape)]
    ppermute x3 -> x9, starting transfers between devices: 2.71 us -> 10.3 us  [around(): lax.ppermute(values, axis, [(n, (n + step) % 4) for n in range(4)])]
    ppermute x3 -> x9, waiting for transfers between devices: 4.78 us -> 11.9 us  [around(): lax.ppermute(values, axis, [(n, (n + step) % 4) for n in range(4)])]
    pallas_call x8 -> x9, Pallas kernels: 17.8 us -> 17.6 us  [call(): pl.pallas_call(kernel, out_shape=[jax.ShapeDtypeStruct(shape, F32) for sh...]
  transfers between devices with their start and end apart: 6 -> 12, of which waited for: 6 -> 12; matrix products, arithmetic and copies ran while one was open for 0% -> 0% of each run, Pallas kernels for 0% -> 0%
where the time goes in v6:
time: 113 us; the launch traced here: 112 us
  blocking collectives  66.9 us (59%)
  Pallas kernels  17.6 us (16%)
  waiting for transfers between devices  15.8 us (14%)
  starting transfers between devices  10.6 us (9%)
    all_to_all x4, blocking collectives, exchange(): lax.all_to_all(values.reshape(chunk), axes, 0, 0, tiled=True).reshape(shape)  66.9 us
    pallas_call x9, Pallas kernels, call(): pl.pallas_call(kernel, out_shape=[jax.ShapeDtypeStruct(shape, F32) for sh...  17.6 us
    ppermute x9, waiting for transfers between devices, around(): lax.ppermute(values, axis, [(n, (n + step) % 4) for n in range(4)])  11.9 us
    ppermute x9, starting transfers between devices, around(): lax.ppermute(values, axis, [(n, (n + step) % 4) for n in range(4)])  10.3 us
    ppermute x3, waiting for transfers between devices, swap_cores(): return lax.ppermute(values, 'ic', [(0, 1), (1, 0)])  3.9 us
  transfers between devices with their start and end apart: 12, of which 12 were waited for; matrix products, arithmetic and copies ran while one was open for 0% of the time, Pallas kernels for 0%

profile of v6, /device:TPU:8, one launch (start us, length us, event | category | flops | bytes accessed | tf_op | source)
XLA Modules:
  0.0 112.4 jit_solution(17846833294670917403)
XLA Ops:
  0.6 3.8 %first.1 = (f32[256,128]{1,0:T(8,128)S(1)}, f32[64,64,128]{2,1,0:T(8,128)S(1)}) custom-call(s32[3]{0:T(128)} %bitcast.23, bf16[64,64,128]{2,1,0:T(8,128)(2,1)} %bitcast.12, f32[256,128]{1,0:T(8,128)} %b_ref.1, f32[512,128]{1,0:T(8,128)} %c_ref.1), custom_call_target="tpu_custom_call" | custom-call | tf_op jit(solution)/shard_map/first/pallas_call | solution.py:346
  4.4 21.9 %all_to_all.20 = f32[32,8,128]{2,1,0:T(8,128)S(1)} all-to-all(f32[32,8,128]{2,1,0:T(8,128)S(1)} %bitcast.22), channel_id=1, replica_groups=mesh['iy'=4,'ic'=2,'ja'=8,'ka'=4] {'ja','ka'}, dimensions={0} | all-to-all | bytes 262144 | tf_op jit(solution)/shard_map/all_to_all | solution.py:359
  26.4 14.4 %all_to_all.21 = f32[32,3,4,128]{3,2,1,0:T(4,128)S(1)} all-to-all(f32[32,3,4,128]{3,2,1,0:T(4,128)S(1)} %bitcast.20), channel_id=1, replica_groups=mesh['iy'=4,'ic'=2,'ja'=8,'ka'=4] {'ja','ka'}, dimensions={0} | all-to-all | bytes 393216 | tf_op jit(solution)/shard_map/all_to_all | solution.py:359
  40.8 4.7 %second.1 = (f32[256,128]{1,0:T(8,128)S(1)}, f32[128,128]{1,0:T(8,128)S(1)}, f32[104,128]{1,0:T(8,128)S(1)}, f32[104,128]{1,0:T(8,128)S(1)}) custom-call(s32[3]{0:T(128)S(1)} %bitcast.24, f32[384,128]{1,0:T(8,128)S(1)} %bitcast.14, f32[8,128]{1,0:T(8,128)S(1)} %get-tuple-element.22.diagonal_ref, f32[64,64,128]{2,1,0:T(8,128)S(1)} %get-tuple-element.23.y_ref), custom_call_target="tpu_custom_call" | custom-call | tf_op jit(solution)/shard_map/second/pallas_call | solution.py:346
  45.6 1.2 %collective-permute-done.other_ref = f32[104,128]{1,0:T(8,128)S(1)} collective-permute-done((f32[104,128]{1,0:T(8,128)S(1)}, f32[104,128]{1,0:T(8,128)S(1)}, u32[]{:S(2)}, u32[]{:S(2)}) %collective-permute-start) | collective-permute-done | bytes 53280 | tf_op jit(solution)/shard_map/ppermute | solution.py:363
  46.9 1.4 %collective-permute-start.3 = (f32[72,128]{1,0:T(8,128)S(1)}, f32[72,128]{1,0:T(8,128)S(1)}, u32[]{:S(2)}, u32[]{:S(2)}) collective-permute-start(f32[72,128]{1,0:T(8,128)S(1)} %get-tuple-element.26.parts_0), channel_id=1, source_target_pairs={{0,3},{1,0},{2,1},{3,2},{4,7},{5,4},{6,5},{7,6},{8,11},{9,8},{10,9... | collective-permute-start | bytes 110600 | tf_op jit(solution)/shard_map/ppermute | solution.py:368
  48.3 0.5 collective-permute-start.2
  48.8 0.7 collective-permute-start.1
  49.5 1.3 %collective-permute-done.3.parts_3 = f32[72,128]{1,0:T(8,128)S(1)} collective-permute-done((f32[72,128]{1,0:T(8,128)S(1)}, f32[72,128]{1,0:T(8,128)S(1)}, u32[]{:S(2)}, u32[]{:S(2)}) %collective-permute-start.3) | collective-permute-done | bytes 36896 | tf_op jit(solution)/shard_map/ppermute | solution.py:368
  50.9 3.2 %collective-permute-done.2.parts_2 = f32[72,128]{1,0:T(8,128)S(1)} collective-permute-done((f32[72,128]{1,0:T(8,128)S(1)}, f32[72,128]{1,0:T(8,128)S(1)}, u32[]{:S(2)}, u32[]{:S(2)}) %collective-permute-start.2) | collective-permute-done | bytes 36896 | tf_op jit(solution)/shard_map/ppermute | solution.py:368
  54.1 0.2 collective-permute-done.1.parts_1
  54.3 0.5 collective-permute-start.6
  54.8 2.4 %collective-permute-start.5 = (f32[192,128]{1,0:T(8,128)S(1)}, f32[192,128]{1,0:T(8,128)S(1)}, u32[]{:S(2)}, u32[]{:S(2)}) collective-permute-start(f32[192,128]{1,0:T(8,128)S(1)} %dense.1.half_0), channel_id=1, source_target_pairs={{0,128},{64,192},{128,0},{192,64},{1,129},{65,193},{129,1},{193,65... | collective-permute-start | bytes 294920 | tf_op jit(solution)/shard_map/ppermute | solution.py:368
  57.3 1.9 %collective-permute-start.4 = (f32[192,128]{1,0:T(8,128)S(1)}, f32[192,128]{1,0:T(8,128)S(1)}, u32[]{:S(2)}, u32[]{:S(2)}) collective-permute-start(f32[192,128]{1,0:T(8,128)S(1)} %dense.1.half_0), channel_id=1, source_target_pairs={{0,64},{64,128},{128,192},{192,0},{1,65},{65,129},{129,193},{193,1... | collective-permute-start | bytes 294920 | tf_op jit(solution)/shard_map/ppermute | solution.py:368
  59.2 0.4 collective-permute-done.6.half_3
  59.6 1.4 %collective-permute-done.5.half_2 = f32[192,128]{1,0:T(8,128)S(1)} collective-permute-done((f32[192,128]{1,0:T(8,128)S(1)}, f32[192,128]{1,0:T(8,128)S(1)}, u32[]{:S(2)}, u32[]{:S(2)}) %collective-permute-start.5) | collective-permute-done | bytes 98336 | tf_op jit(solution)/shard_map/ppermute | solution.py:368
  61.0 1.2 %collective-permute-done.4.half_1 = f32[192,128]{1,0:T(8,128)S(1)} collective-permute-done((f32[192,128]{1,0:T(8,128)S(1)}, f32[192,128]{1,0:T(8,128)S(1)}, u32[]{:S(2)}, u32[]{:S(2)}) %collective-permute-start.4) | collective-permute-done | bytes 98336 | tf_op jit(solution)/shard_map/ppermute | solution.py:368
  62.2 0.3 collective-permute-start.7
  62.5 1.3 %collective-permute-done.7.other_ref = f32[192,128]{1,0:T(8,128)S(1)} collective-permute-done((f32[192,128]{1,0:T(8,128)S(1)}, f32[192,128]{1,0:T(8,128)S(1)}, u32[]{:S(2)}, u32[]{:S(2)}) %collective-permute-start.7) | collective-permute-done | bytes 98336 | tf_op jit(solution)/shard_map/ppermute | solution.py:363
  63.8 5.1 %third.1 = (f32[256,128]{1,0:T(8,128)}, f32[256,128]{1,0:T(8,128)S(1)}, f32[256,128]{1,0:T(8,128)S(1)}, f32[128,128]{1,0:T(8,128)S(1)}) custom-call(s32[3]{0:T(128)S(1)} %bitcast.25, f32[192,128]{1,0:T(8,128)S(1)} %sum.1.same_ref, f32[192,128]{1,0:T(8,128)S(1)} %collective-permute-done.7.other_ref, f32[128,128]{1,0:T(8,128)S(1)} %get-tuple-element.28.gram_c_ref, ...), custom_call_target="tpu_custom_call" | custom-call | tf_op jit(solution)/shard_map/third/pallas_call | solution.py:346
  68.9 16.4 %all_to_all.22 = f32[64,4,128]{2,1,0:T(4,128)S(1)} all-to-all(f32[64,4,128]{2,1,0:T(4,128)S(1)} %bitcast.21), channel_id=1, replica_groups=mesh['iy'=4,'ic'=2,'ja'=8,'ka'=4] {'iy','ic','ja'}, dimensions={0} | all-to-all | bytes 262144 | tf_op jit(solution)/shard_map/all_to_all | solution.py:359
  85.3 0.1 collect_c.1
  85.4 14.2 %all_to_all.23 = f32[32,5,2,128]{3,2,1,0:T(2,128)S(1)} all-to-all(f32[32,5,2,128]{3,2,1,0:T(2,128)S(1)} %bitcast.17), channel_id=1, replica_groups=mesh['iy'=4,'ic'=2,'ja'=8,'ka'=4] {'iy','ja'}, dimensions={0} | all-to-all | bytes 327680 | tf_op jit(solution)/shard_map/all_to_all | solution.py:359
  99.6 1.4 %collective-permute-done.8.other_ref = f32[320,128]{1,0:T(8,128)S(1)} collective-permute-done((f32[320,128]{1,0:T(8,128)S(1)}, f32[320,128]{1,0:T(8,128)S(1)}, u32[]{:S(2)}, u32[]{:S(2)}) %collective-permute-start.8) | collective-permute-done | bytes 163872 | tf_op jit(solution)/shard_map/ppermute | solution.py:363
  101.0 3.8 %fourth.1 = (f32[256,128]{1,0:T(8,128)}, f32[512,128]{1,0:T(8,128)S(1)}, f32[1,128]{1,0:T(1,128)S(1)}) custom-call(f32[320,128]{1,0:T(8,128)S(1)} %bitcast.16, f32[320,128]{1,0:T(8,128)S(1)} %collective-permute-done.8.other_ref, f32[128,128]{1,0:T(8,128)S(1)} %get-tuple-element.32.gram_a_ref, f32[256,128]{1,0:T(8,128)S(1)} %get-tuple-element.33.solved_b_ref), custom_call_target="tpu_custom_call" | custom-call | tf_op jit(solution)/shard_map/fourth/pallas_call | solution.py:346
  104.8 1.2 %collective-permute-start.11 = (f32[1,128]{1,0:T(1,128)S(1)}, f32[1,128]{1,0:T(1,128)S(1)}, u32[]{:S(2)}, u32[]{:S(2)}) collective-permute-start(f32[1,128]{1,0:T(1,128)S(1)} %get-tuple-element.36), channel_id=1, source_target_pairs={{0,3},{1,0},{2,1},{3,2},{4,7},{5,4},{6,5},{7,6},{8,11},{9,8},{10,9... | collective-permute-start | bytes 1544 | tf_op jit(solution)/shard_map/ppermute | solution.py:368
  106.0 0.9 collective-permute-start.10
  106.9 0.6 collective-permute-start.9
  107.5 0.9 collective-permute-done.11
  108.4 2.7 %collective-permute-done.10 = f32[1,128]{1,0:T(1,128)S(1)} collective-permute-done((f32[1,128]{1,0:T(1,128)S(1)}, f32[1,128]{1,0:T(1,128)S(1)}, u32[]{:S(2)}, u32[]{:S(2)}) %collective-permute-start.10) | collective-permute-done | bytes 544 | tf_op jit(solution)/shard_map/ppermute | solution.py:368
  111.1 0.6 collective-permute-done.9
  111.7 0.7 broadcast_multiply_fusion
  (11 shorter events, 0.3 us)
Async XLA Ops:
  0.6 40.2 %copy-start.1 = (s32[3,1]{0,1:T(1,128)S(1)}, s32[3,1]{0,1:T(1,128)}, u32[]{:S(2)}) copy-start(s32[3,1]{0,1:T(1,128)} %param.6) | copy-start | bytes 40
  4.4 59.4 %copy-start = (bf16[1,64,64,128]{3,2,1,0:T(8,128)(2,1)S(1)}, bf16[1,64,64,128]{3,2,1,0:T(8,128)(2,1)}, u32[]{:S(2)}) copy-start(bf16[1,64,64,128]{3,2,1,0:T(8,128)(2,1)} %param.5) | copy-start | bytes 3145732
  45.5 1.3 %collective-permute-start = (f32[104,128]{1,0:T(8,128)S(1)}, f32[104,128]{1,0:T(8,128)S(1)}, u32[]{:S(2)}, u32[]{:S(2)}) collective-permute-start(f32[104,128]{1,0:T(8,128)S(1)} %get-tuple-element.25), channel_id=1, source_target_pairs={{0,32},{32,0},{1,33},{33,1},{2,34},{34,2},{3,35},{35,3},{4,36},{36... | collective-permute-start | bytes 159752 | tf_op jit(solution)/shard_map/ppermute | solution.py:363
  46.9 4.0 %collective-permute-start.3 = (f32[72,128]{1,0:T(8,128)S(1)}, f32[72,128]{1,0:T(8,128)S(1)}, u32[]{:S(2)}, u32[]{:S(2)}) collective-permute-start(f32[72,128]{1,0:T(8,128)S(1)} %get-tuple-element.26.parts_0), channel_id=1, source_target_pairs={{0,3},{1,0},{2,1},{3,2},{4,7},{5,4},{6,5},{7,6},{8,11},{9,8},{10,9... | collective-permute-start | bytes 110600 | tf_op jit(solution)/shard_map/ppermute | solution.py:368
  48.3 5.8 %collective-permute-start.2 = (f32[72,128]{1,0:T(8,128)S(1)}, f32[72,128]{1,0:T(8,128)S(1)}, u32[]{:S(2)}, u32[]{:S(2)}) collective-permute-start(f32[72,128]{1,0:T(8,128)S(1)} %get-tuple-element.26.parts_0), channel_id=1, source_target_pairs={{0,2},{1,3},{2,0},{3,1},{4,6},{5,7},{6,4},{7,5},{8,10},{9,11},{10,... | collective-permute-start | bytes 110600 | tf_op jit(solution)/shard_map/ppermute | solution.py:368
  48.8 5.4 %collective-permute-start.1 = (f32[72,128]{1,0:T(8,128)S(1)}, f32[72,128]{1,0:T(8,128)S(1)}, u32[]{:S(2)}, u32[]{:S(2)}) collective-permute-start(f32[72,128]{1,0:T(8,128)S(1)} %get-tuple-element.26.parts_0), channel_id=1, source_target_pairs={{0,1},{1,2},{2,3},{3,0},{4,5},{5,6},{6,7},{7,4},{8,9},{9,10},{10,1... | collective-permute-start | bytes 110600 | tf_op jit(solution)/shard_map/ppermute | solution.py:368
  54.3 5.2 %collective-permute-start.6 = (f32[192,128]{1,0:T(8,128)S(1)}, f32[192,128]{1,0:T(8,128)S(1)}, u32[]{:S(2)}, u32[]{:S(2)}) collective-permute-start(f32[192,128]{1,0:T(8,128)S(1)} %dense.1.half_0), channel_id=1, source_target_pairs={{0,192},{64,0},{128,64},{192,128},{1,193},{65,1},{129,65},{193,129... | collective-permute-start | bytes 294920 | tf_op jit(solution)/shard_map/ppermute | solution.py:368
  54.8 6.1 %collective-permute-start.5 = (f32[192,128]{1,0:T(8,128)S(1)}, f32[192,128]{1,0:T(8,128)S(1)}, u32[]{:S(2)}, u32[]{:S(2)}) collective-permute-start(f32[192,128]{1,0:T(8,128)S(1)} %dense.1.half_0), channel_id=1, source_target_pairs={{0,128},{64,192},{128,0},{192,64},{1,129},{65,193},{129,1},{193,65... | collective-permute-start | bytes 294920 | tf_op jit(solution)/shard_map/ppermute | solution.py:368
  57.3 4.9 %collective-permute-start.4 = (f32[192,128]{1,0:T(8,128)S(1)}, f32[192,128]{1,0:T(8,128)S(1)}, u32[]{:S(2)}, u32[]{:S(2)}) collective-permute-start(f32[192,128]{1,0:T(8,128)S(1)} %dense.1.half_0), channel_id=1, source_target_pairs={{0,64},{64,128},{128,192},{192,0},{1,65},{65,129},{129,193},{193,1... | collective-permute-start | bytes 294920 | tf_op jit(solution)/shard_map/ppermute | solution.py:368
  62.2 1.6 %collective-permute-start.7 = (f32[192,128]{1,0:T(8,128)S(1)}, f32[192,128]{1,0:T(8,128)S(1)}, u32[]{:S(2)}, u32[]{:S(2)}) collective-permute-start(f32[192,128]{1,0:T(8,128)S(1)} %sum.1.same_ref), channel_id=1, source_target_pairs={{0,32},{32,0},{1,33},{33,1},{2,34},{34,2},{3,35},{35,3},{4,36},{36... | collective-permute-start | bytes 294920 | tf_op jit(solution)/shard_map/ppermute | solution.py:363
  99.6 1.4 %collective-permute-start.8 = (f32[320,128]{1,0:T(8,128)S(1)}, f32[320,128]{1,0:T(8,128)S(1)}, u32[]{:S(2)}, u32[]{:S(2)}) collective-permute-start(f32[320,128]{1,0:T(8,128)S(1)} %bitcast.15), channel_id=1, source_target_pairs={{0,32},{32,0},{1,33},{33,1},{2,34},{34,2},{3,35},{35,3},{4,36},{36... | collective-permute-start | bytes 491528 | tf_op jit(solution)/shard_map/ppermute | solution.py:363
  104.8 3.6 %collective-permute-start.11 = (f32[1,128]{1,0:T(1,128)S(1)}, f32[1,128]{1,0:T(1,128)S(1)}, u32[]{:S(2)}, u32[]{:S(2)}) collective-permute-start(f32[1,128]{1,0:T(1,128)S(1)} %get-tuple-element.36), channel_id=1, source_target_pairs={{0,3},{1,0},{2,1},{3,2},{4,7},{5,4},{6,5},{7,6},{8,11},{9,8},{10,9... | collective-permute-start | bytes 1544 | tf_op jit(solution)/shard_map/ppermute | solution.py:368
  106.0 5.1 %collective-permute-start.10 = (f32[1,128]{1,0:T(1,128)S(1)}, f32[1,128]{1,0:T(1,128)S(1)}, u32[]{:S(2)}, u32[]{:S(2)}) collective-permute-start(f32[1,128]{1,0:T(1,128)S(1)} %get-tuple-element.36), channel_id=1, source_target_pairs={{0,2},{1,3},{2,0},{3,1},{4,6},{5,7},{6,4},{7,5},{8,10},{9,11},{10,... | collective-permute-start | bytes 1544 | tf_op jit(solution)/shard_map/ppermute | solution.py:368
  106.9 4.8 %collective-permute-start.9 = (f32[1,128]{1,0:T(1,128)S(1)}, f32[1,128]{1,0:T(1,128)S(1)}, u32[]{:S(2)}, u32[]{:S(2)}) collective-permute-start(f32[1,128]{1,0:T(1,128)S(1)} %get-tuple-element.36), channel_id=1, source_target_pairs={{0,1},{1,2},{2,3},{3,0},{4,5},{5,6},{6,7},{7,4},{8,9},{9,10},{10,1... | collective-permute-start | bytes 1544 | tf_op jit(solution)/shard_map/ppermute | solution.py:368

commit v7 on v6

--- a/solution.py
+++ b/solution.py
@@ -5,13 +5,11 @@
 from jax.experimental.pallas import tpu as pltpu
 from jax.sharding import PartitionSpec as P
 
+
 RANK = 128
 BI = 64
 BJ = 64
 BK = 128
-GI_DEV = 4
-GJ_DEV = 4
-GK_DEV = 4
 SLOTS = 4
 ROWS = 2048
 IA = ("iy", "ic")
@@ -127,32 +125,21 @@
 
 
 def first_kernel(
-    coords_ref, block_ref, b_ref, c_ref, chunk_ref, y_ref,
-    x_in, c_in, b_in, share_c, share_b, sems,
+    coords_in, block_ref, b_ref, c_ref, chunk_ref, y_ref,
+    x_in, c_in, b_in, coords_ref, sems,
 ):
-    at, slot = places(coords_ref)
-
-    def window(ref, index, size):
-        return ref.at[pl.ds(pl.multiple_of(index * size, size), size), :]
-
-    small = [
-        (window(c_ref, slot[2], BK), c_in),
-        (window(b_ref, slot[1], BJ), b_in),
-        (window(c_ref, at[1], 64), share_c),
-        (window(b_ref, at[2], 64), share_b),
-    ]
+
     parts = [pl.ds(n * (BI // 4), BI // 4) for n in range(4)]
-    copies = [pltpu.make_async_copy(src, dst, sems.at[n]) for n, (src, dst) in enumerate(small)]
-    copies += [
-        pltpu.make_async_copy(block_ref.at[part], x_in.at[part], sems.at[4 + n])
-        for n, part in enumerate(parts)
-    ]
+    pairs = [(coords_in, coords_ref), (c_ref, c_in), (b_ref, b_in)]
+    pairs += [(block_ref.at[part], x_in.at[part]) for part in parts]
+    copies = [pltpu.make_async_copy(*pair, sems.at[n]) for n, pair in enumerate(pairs)]
     for copy in copies:
         copy.start()
-    for copy in copies[:4]:
+    for copy in copies[:3]:
         copy.wait()
-    part_c = gram(share_c[...]) * (1.0 / ROWS)
-    part_b = gram(share_b[...]) * (1.0 / ROWS)
+    at, slot = places(coords_ref)
+    part_c = gram(some_rows(c_in, at[1], 64)) * (1.0 / ROWS)
+    part_b = gram(some_rows(b_in, at[2], 64)) * (1.0 / ROWS)
     row, col = iotas()
     packed = jnp.where(row <= col, part_b, part_c)
     diagonal = jnp.sum(jnp.where(row == col, part_c, 0.0), axis=0, keepdims=True)
@@ -160,12 +147,12 @@
         put(chunk_ref, 2 + t, 32, 8, packed[32 * t : 32 * t + 32])
     put(chunk_ref, 6, 32, 8, jnp.broadcast_to(diagonal, (32, RANK)))
     put(chunk_ref, 7, 32, 8, jnp.full((32, RANK), slot[0].astype(F32)))
-    high, low = halves(c_in[...])
+    high, low = halves(some_rows(c_in, slot[2], BK))
     both = jnp.concatenate([high, low], axis=0)
-    rows_b = b_in[...]
+    rows_b = some_rows(b_in, slot[1], BJ)
     partial = []
     for n, part in enumerate(parts):
-        copies[4 + n].wait()
+        copies[3 + n].wait()
         block = x_in[part].reshape(BI // 4 * BJ, BK)
         y = jnp.dot(jnp.concatenate([block, block], axis=1), both, preferred_element_type=F32)
         y = y.reshape(BI // 4, BJ, RANK)
@@ -230,7 +217,7 @@
     coords_ref, got_ref, diagonal_ref, y_ref,
     solved_ref, gram_c_ref, keep_ref, send_ref, partial_ref, raw_ref,
 ):
-    at, slot = places(coords_ref)
+    _, slot = places(coords_ref)
     packed = natural(got_ref, 32, 12, 8, 12)
     flipped = packed.T
     row, col = iotas()
@@ -270,7 +257,7 @@
         all_ref[pl.ds(pl.multiple_of(source * size, 8), size), :] = ref[...]
 
 
-def dense_kernel(parts_0, parts_1, parts_2, parts_3, gram_ref, half_ref, all_ref):
+def dense_kernel(parts_0, parts_1, parts_2, parts_3, half_ref, all_ref):
     in_source_order("ka", (parts_0, parts_1, parts_2, parts_3), all_ref)
     sums = [jnp.zeros((32, RANK), F32) for _ in range(SLOTS)]
     for n in range(4):
@@ -281,18 +268,32 @@
                 sums[slot] = sums[slot] + jnp.where(ids == slot, rows, 0.0)
     for slot in range(SLOTS):
         half_ref[32 * slot : 32 * slot + 32, :] = sums[slot]
-    half_ref[128:192, :] = gram_ref[...]
 
 
 def sum_kernel(half_0, half_1, half_2, half_3, sum_ref, all_ref):
     in_source_order("iy", (half_0, half_1, half_2, half_3), all_ref)
-    parts = [all_ref[192 * n : 192 * n + 192, :] for n in range(4)]
+    size = sum_ref.shape[0]
+    parts = [all_ref[size * n : size * n + size, :] for n in range(4)]
     sum_ref[...] = (parts[0] + parts[1]) + (parts[2] + parts[3])
 
 
+def second_inverse_kernel(
+    same_ref, other_ref, gram_c_ref, solved_a_ref,
+    solver_ref, gram_a_ref, scale_ref, loading_a_ref, raw_ref,
+):
+    core = lax.axis_index("ic")
+    for ref, half in ((same_ref, core), (other_ref, 1 - core)):
+        raw_ref[pl.ds(pl.multiple_of(64 * half, 64), 64), :] = ref[...]
+    scale, gram_a = scaled_gram(raw_ref[...])
+    gram_a_ref[...] = gram_a
+    scale_ref[...] = jnp.broadcast_to(scale, (8, RANK))
+    loading_a_ref[...] = solved_a_ref[...] * scale
+    solver_ref[...] = system_inverse(gram_a * gram_c_ref[...])
+
+
 def third_kernel(
-    coords_ref, same_ref, other_ref, gram_c_ref, solved_a_ref, block_ref,
-    loading_a_ref, solved_ref, chunk_ref, gram_a_ref, khatri_ref, rows_ref,
+    coords_ref, same_ref, other_ref, solver_ref, scale_ref, solved_a_ref, block_ref,
+    solved_ref, chunk_ref, khatri_ref, rows_ref,
 ):
     at, slot = places(coords_ref)
     core = lax.axis_index("ic")
@@ -300,14 +301,9 @@
         for n in range(SLOTS):
             place = pl.multiple_of(64 * n + 32 * half, 32)
             rows_ref[pl.ds(place, 32), :] = ref[32 * n : 32 * n + 32, :]
-        rows_ref[pl.ds(pl.multiple_of(256 + 64 * half, 64), 64), :] = ref[128:192, :]
-    scale, gram_a = scaled_gram(rows_ref[256:384, :])
-    gram_a_ref[...] = gram_a
-    loading_a_ref[...] = solved_a_ref[...] * scale
-    solver = system_inverse(gram_a * gram_c_ref[...])
-    solved_ref[...] = exact_dot(rows_ref[0:256, :] * scale, solver)
+    solved_ref[...] = exact_dot(rows_ref[...] * scale_ref[0:1, :], solver_ref[...])
     raw = gram(some_rows(solved_ref, at[0], 32)) * (1.0 / ROWS)
-    own_a = some_rows(loading_a_ref, slot[0], BI)
+    own_a = some_rows(solved_a_ref, slot[0], BI) * scale_ref[0:1, :]
     own_b = some_rows(solved_ref, slot[1], BJ)
     for n in range(BI):
         khatri_ref[n * BJ : (n + 1) * BJ, :] = (own_a[n : n + 1, :] * own_b).astype(BF16)
@@ -340,7 +336,7 @@
     squares_ref[...] = jnp.sum(solved * solved, axis=0, keepdims=True)
 
 
-def call(kernel, operands, outs, name, scalars=0, scratch=(), space=pltpu.VMEM):
+def call(kernel, operands, outs, scalars=0, scratch=(), space=pltpu.VMEM):
     vmem = pl.BlockSpec(memory_space=pltpu.VMEM)
     smem = pl.BlockSpec(memory_space=pltpu.SMEM)
     return pl.pallas_call(
@@ -350,7 +346,6 @@
         out_specs=[vmem] * len(outs),
         scratch_shapes=scratch,
         compiler_params=pltpu.CompilerParams(vmem_limit_bytes=32 << 20),
-        name=name,
     )(*operands)
 
 
@@ -378,60 +373,57 @@
         first_kernel,
         [pltpu.with_memory_space_constraint(v, pltpu.HBM) for v in (coords, block, factor_b, factor_c)],
         [(256, RANK), (BI, BJ, RANK)],
-        "first",
-        1,
+        0,
         [
             pltpu.VMEM((BI, BJ, BK), BF16),
-            pltpu.VMEM((BK, RANK), F32),
-            pltpu.VMEM((BJ, RANK), F32),
-            pltpu.VMEM((64, RANK), F32),
-            pltpu.VMEM((64, RANK), F32),
-            pltpu.SemaphoreType.DMA((8,)),
+            pltpu.VMEM((512, RANK), F32),
+            pltpu.VMEM((256, RANK), F32),
+            pltpu.SMEM((3,), jnp.int32),
+            pltpu.SemaphoreType.DMA((7,)),
         ],
         pltpu.HBM,
     )
     got = exchange(chunk, ("ja", "ka"), 32, 8, RANK)
-    spread, diagonal = call(collect_first_kernel, (got,), [(384, RANK), (8, RANK)], "collect_a")
+    spread, diagonal = call(collect_first_kernel, (got,), [(384, RANK), (8, RANK)])
     got = exchange(spread, ("ja", "ka"), 32, 3, 4, RANK)
 
     solved_a, gram_c, keep, send = call(
         second_kernel,
         (coords, got, diagonal, y),
         [(256, RANK), full, (104, RANK), (104, RANK)],
-        "second",
         1,
         [pltpu.VMEM((BJ, RANK), F32), pltpu.VMEM(full, F32)],
     )
-    parts, gram_half = call(
-        merge_kernel, (keep, swap_cores(send)), [(72, RANK), (64, RANK)], "merge"
-    )
-    (half,) = call(
-        dense_kernel,
-        (parts, *around("ka", parts), gram_half),
-        [(192, RANK)],
-        "dense",
+    parts, gram_half = call(merge_kernel, (keep, swap_cores(send)), [(72, RANK), (64, RANK)])
+    around_x = around("ka", parts)
+    (gram_half,) = call(
+        sum_kernel,
+        (gram_half, *around("iy", gram_half)),
+        [(64, RANK)],
         0,
-        [pltpu.VMEM((288, RANK), F32)],
-    )
-    (half,) = call(
-        sum_kernel,
-        (half, *around("iy", half)),
-        [(192, RANK)],
-        "sum",
+        [pltpu.VMEM((256, RANK), F32)],
+    )
+    (half,) = call(dense_kernel, (parts, *around_x), [full], 0, [pltpu.VMEM((288, RANK), F32)])
+    other = swap_cores(gram_half)
+    around_y = around("iy", half)
+    solver, gram_a, scale, loading_a = call(
+        second_inverse_kernel,
+        (gram_half, other, gram_c, solved_a),
+        [full, full, (8, RANK), (256, RANK)],
         0,
-        [pltpu.VMEM((768, RANK), F32)],
-    )
-
-    loading_a, solved_b, chunk, gram_a = call(
+        [pltpu.VMEM(full, F32)],
+    )
+    (half,) = call(sum_kernel, (half, *around_y), [full], 0, [pltpu.VMEM((512, RANK), F32)])
+
+    solved_b, chunk = call(
         third_kernel,
-        (coords, half, swap_cores(half), gram_c, solved_a, block),
-        [(256, RANK), (256, RANK), (256, RANK), full],
-        "third",
+        (coords, half, swap_cores(half), solver, scale, solved_a, block),
+        [(256, RANK), (256, RANK)],
         1,
-        [pltpu.VMEM((BI * BJ, RANK), BF16), pltpu.VMEM((384, RANK), F32)],
+        [pltpu.VMEM((BI * BJ, RANK), BF16), pltpu.VMEM((256, RANK), F32)],
     )
     got = exchange(chunk, (*IA, "ja"), 64, 4, RANK)
-    (spread,) = call(collect_third_kernel, (got,), [(320, RANK)], "collect_c")
+    (spread,) = call(collect_third_kernel, (got,), [(320, RANK)])
     same = exchange(spread, ("iy", "ja"), 32, 5, 2, RANK)
     other = swap_cores(same)
 
@@ -439,7 +431,6 @@
         fourth_kernel,
         (same, other, gram_a, solved_b),
         [(256, RANK), (512, RANK), (1, RANK)],
-        "fourth",
         0,
         [pltpu.VMEM((640, RANK), F32)],
     )

time: 113 us -> 116 us (1.027)
  starting transfers between devices: 10.6 us -> 14.8 us
    ppermute x9 -> x12, starting transfers between devices: 10.3 us -> 14.5 us  [around(): lax.ppermute(values, axis, [(n, (n + step) % 4) for n in range(4)])]
    ppermute x9 -> x12, waiting for transfers between devices: 11.9 us -> 11.1 us  [around(): lax.ppermute(values, axis, [(n, (n + step) % 4) for n in range(4)])]
    pallas_call x9 -> x11, Pallas kernels: 17.6 us -> 17.4 us  [call(): pl.pallas_call(kernel, out_shape=[jax.ShapeDtypeStruct(shape, F32) for sh...]
    ppermute x3 -> x4, waiting for transfers between devices: 3.9 us -> 3.81 us  [swap_cores(): return lax.ppermute(values, 'ic', [(0, 1), (1, 0)])]
  transfers between devices with their start and end apart: 12 -> 16, of which waited for: 12 -> 11; matrix products, arithmetic and copies ran while one was open for 0% -> 0% of each run, Pallas kernels for 0% -> 3%
where the time goes in v7:
time: 116 us; the launch traced here: 115 us
  blocking collectives  66.8 us (58%)
  Pallas kernels  17.4 us (15%)
  waiting for transfers between devices  14.9 us (13%)
  starting transfers between devices  14.8 us (13%)
    all_to_all x4, blocking collectives, exchange(): lax.all_to_all(values.reshape(chunk), axes, 0, 0, tiled=True).reshape(shape)  66.8 us
    pallas_call x11, Pallas kernels, call(): pl.pallas_call(kernel, out_shape=[jax.ShapeDtypeStruct(shape, F32) for sh...  17.4 us
    ppermute x12, starting transfers between devices, around(): lax.ppermute(values, axis, [(n, (n + step) % 4) for n in range(4)])  14.5 us
    ppermute x12, waiting for transfers between devices, around(): lax.ppermute(values, axis, [(n, (n + step) % 4) for n in range(4)])  11.1 us
    ppermute x4, waiting for transfers between devices, swap_cores(): return lax.ppermute(values, 'ic', [(0, 1), (1, 0)])  3.81 us
  transfers between devices with their start and end apart: 16, of which 11 were waited for; matrix products, arithmetic and copies ran while one was open for 0% of the time, Pallas kernels for 3%

profile of v7, /device:TPU:8, one launch (start us, length us, event | category | flops | bytes accessed | tf_op | source)
XLA Modules:
  0.0 115.4 jit_solution(9079047061979289394)
XLA Ops:
  0.6 3.1 %shard_map.67 = (f32[256,128]{1,0:T(8,128)S(1)}, f32[64,64,128]{2,1,0:T(8,128)S(1)}) custom-call(s32[3]{0:T(128)} %bitcast.23, bf16[64,64,128]{2,1,0:T(8,128)(2,1)} %bitcast.12, f32[256,128]{1,0:T(8,128)} %b_ref.1, f32[512,128]{1,0:T(8,128)} %c_ref.1), custom_call_target="tpu_custom_call" | custom-call | tf_op jit(solution)/shard_map/pallas_call | solution.py:342
  3.8 21.7 %all_to_all.20 = f32[32,8,128]{2,1,0:T(8,128)S(1)} all-to-all(f32[32,8,128]{2,1,0:T(8,128)S(1)} %bitcast.22), channel_id=1, replica_groups=mesh['iy'=4,'ic'=2,'ja'=8,'ka'=4] {'ja','ka'}, dimensions={0} | all-to-all | bytes 262144 | tf_op jit(solution)/shard_map/all_to_all | solution.py:354
  25.5 14.6 %all_to_all.21 = f32[32,3,4,128]{3,2,1,0:T(4,128)S(1)} all-to-all(f32[32,3,4,128]{3,2,1,0:T(4,128)S(1)} %bitcast.20), channel_id=1, replica_groups=mesh['iy'=4,'ic'=2,'ja'=8,'ka'=4] {'ja','ka'}, dimensions={0} | all-to-all | bytes 393216 | tf_op jit(solution)/shard_map/all_to_all | solution.py:354
  40.1 4.7 %shard_map.69 = (f32[256,128]{1,0:T(8,128)S(1)}, f32[128,128]{1,0:T(8,128)S(1)}, f32[104,128]{1,0:T(8,128)S(1)}, f32[104,128]{1,0:T(8,128)S(1)}) custom-call(s32[3]{0:T(128)S(1)} %bitcast.24, f32[384,128]{1,0:T(8,128)S(1)} %bitcast.14, f32[8,128]{1,0:T(8,128)S(1)} %get-tuple-element.24.diagonal_ref, f32[64,64,128]{2,1,0:T(8,128)S(1)} %get-tuple-element.25.y_ref), custom_call_target="tpu_custom_call" | custom-call | tf_op jit(solution)/shard_map/pallas_call | solution.py:342
  44.9 1.2 %collective-permute-done.other_ref = f32[104,128]{1,0:T(8,128)S(1)} collective-permute-done((f32[104,128]{1,0:T(8,128)S(1)}, f32[104,128]{1,0:T(8,128)S(1)}, u32[]{:S(2)}, u32[]{:S(2)}) %collective-permute-start) | collective-permute-done | bytes 53280 | tf_op jit(solution)/shard_map/ppermute | solution.py:358
  46.1 1.3 %collective-permute-start.7 = (f32[72,128]{1,0:T(8,128)S(1)}, f32[72,128]{1,0:T(8,128)S(1)}, u32[]{:S(2)}, u32[]{:S(2)}) collective-permute-start(f32[72,128]{1,0:T(8,128)S(1)} %get-tuple-element.32.parts_0), channel_id=1, source_target_pairs={{0,3},{1,0},{2,1},{3,2},{4,7},{5,4},{6,5},{7,6},{8,11},{9,8},{10,9... | collective-permute-start | bytes 110600 | tf_op jit(solution)/shard_map/ppermute | solution.py:363
  47.4 0.7 collective-permute-start.6
  48.1 0.7 collective-permute-start.5
  48.8 1.3 %collective-permute-done.7.parts_3 = f32[72,128]{1,0:T(8,128)S(1)} collective-permute-done((f32[72,128]{1,0:T(8,128)S(1)}, f32[72,128]{1,0:T(8,128)S(1)}, u32[]{:S(2)}, u32[]{:S(2)}) %collective-permute-start.7) | collective-permute-done | bytes 36896 | tf_op jit(solution)/shard_map/ppermute | solution.py:363
  50.1 3.0 %collective-permute-done.6.parts_2 = f32[72,128]{1,0:T(8,128)S(1)} collective-permute-done((f32[72,128]{1,0:T(8,128)S(1)}, f32[72,128]{1,0:T(8,128)S(1)}, u32[]{:S(2)}, u32[]{:S(2)}) %collective-permute-start.6) | collective-permute-done | bytes 36896 | tf_op jit(solution)/shard_map/ppermute | solution.py:363
  53.2 0.2 collective-permute-done.5.parts_1
  53.5 0.5 collective-permute-start.10
  54.0 2.6 %collective-permute-start.9 = (f32[128,128]{1,0:T(8,128)S(1)}, f32[128,128]{1,0:T(8,128)S(1)}, u32[]{:S(2)}, u32[]{:S(2)}) collective-permute-start(f32[128,128]{1,0:T(8,128)S(1)} %shard_map.73.half_0), channel_id=1, source_target_pairs={{0,128},{64,192},{128,0},{192,64},{1,129},{65,193},{129,1},{193,65... | collective-permute-start | bytes 196616 | tf_op jit(solution)/shard_map/ppermute | solution.py:363
  56.6 1.9 %collective-permute-start.8 = (f32[128,128]{1,0:T(8,128)S(1)}, f32[128,128]{1,0:T(8,128)S(1)}, u32[]{:S(2)}, u32[]{:S(2)}) collective-permute-start(f32[128,128]{1,0:T(8,128)S(1)} %shard_map.73.half_0), channel_id=1, source_target_pairs={{0,64},{64,128},{128,192},{192,0},{1,65},{65,129},{129,193},{193,1... | collective-permute-start | bytes 196616 | tf_op jit(solution)/shard_map/ppermute | solution.py:363
  58.6 1.3 %collective-permute-start.2 = (f32[64,128]{1,0:T(8,128)S(1)}, f32[64,128]{1,0:T(8,128)S(1)}, u32[]{:S(2)}, u32[]{:S(2)}) collective-permute-start(f32[64,128]{1,0:T(8,128)S(1)} %get-tuple-element.28.half_0), channel_id=1, source_target_pairs={{0,128},{64,192},{128,0},{192,64},{1,129},{65,193},{129,1},{193,65... | collective-permute-start | bytes 98312 | tf_op jit(solution)/shard_map/ppermute | solution.py:363
  59.9 2.4 %collective-permute-start.1 = (f32[64,128]{1,0:T(8,128)S(1)}, f32[64,128]{1,0:T(8,128)S(1)}, u32[]{:S(2)}, u32[]{:S(2)}) collective-permute-start(f32[64,128]{1,0:T(8,128)S(1)} %get-tuple-element.28.half_0), channel_id=1, source_target_pairs={{0,64},{64,128},{128,192},{192,0},{1,65},{65,129},{129,193},{193,1... | collective-permute-start | bytes 98312 | tf_op jit(solution)/shard_map/ppermute | solution.py:363
  62.5 1.5 %collective-permute-done.2.half_2 = f32[64,128]{1,0:T(8,128)S(1)} collective-permute-done((f32[64,128]{1,0:T(8,128)S(1)}, f32[64,128]{1,0:T(8,128)S(1)}, u32[]{:S(2)}, u32[]{:S(2)}) %collective-permute-start.2) | collective-permute-done | bytes 32800 | tf_op jit(solution)/shard_map/ppermute | solution.py:363
  64.0 0.8 collective-permute-done.1.half_1
  64.9 1.2 %collective-permute-done.4.other_ref = f32[64,128]{1,0:T(8,128)S(1)} collective-permute-done((f32[64,128]{1,0:T(8,128)S(1)}, f32[64,128]{1,0:T(8,128)S(1)}, u32[]{:S(2)}, u32[]{:S(2)}) %collective-permute-start.4) | collective-permute-done | bytes 32800 | tf_op jit(solution)/shard_map/ppermute | solution.py:358
  66.1 3.9 %shard_map.72 = (f32[128,128]{1,0:T(8,128)S(1)}, f32[128,128]{1,0:T(8,128)S(1)}, f32[8,128]{1,0:T(8,128)S(1)}, f32[256,128]{1,0:T(8,128)}) custom-call(f32[64,128]{1,0:T(8,128)S(1)} %shard_map.71.same_ref, f32[64,128]{1,0:T(8,128)S(1)} %collective-permute-done.4.other_ref, f32[128,128]{1,0:T(8,128)S(1)} %get-tuple-element.29.gram_c_ref, ...), custom_call_target="tpu_custom_call" | custom-call | tf_op jit(solution)/shard_map/pallas_call | solution.py:342
  70.1 1.5 %shard_map.75 = (f32[256,128]{1,0:T(8,128)S(1)}, f32[256,128]{1,0:T(8,128)S(1)}) custom-call(s32[3]{0:T(128)S(1)} %bitcast.25, f32[128,128]{1,0:T(8,128)S(1)} %shard_map.74.same_ref, f32[128,128]{1,0:T(8,128)S(1)} %collective-permute-done.11.other_ref, f32[128,128]{1,0:T(8,128)S(1)} %get-tuple-element.33.solver_ref, ...), custom_call_target="tpu_custom_call" | custom-call | tf_op jit(solution)/shard_map/pallas_call | solution.py:342
  71.6 16.4 %all_to_all.22 = f32[64,4,128]{2,1,0:T(4,128)S(1)} all-to-all(f32[64,4,128]{2,1,0:T(4,128)S(1)} %bitcast.21), channel_id=1, replica_groups=mesh['iy'=4,'ic'=2,'ja'=8,'ka'=4] {'iy','ic','ja'}, dimensions={0} | all-to-all | bytes 262144 | tf_op jit(solution)/shard_map/all_to_all | solution.py:354
  88.1 14.2 %all_to_all.23 = f32[32,5,2,128]{3,2,1,0:T(2,128)S(1)} all-to-all(f32[32,5,2,128]{3,2,1,0:T(2,128)S(1)} %bitcast.17), channel_id=1, replica_groups=mesh['iy'=4,'ic'=2,'ja'=8,'ka'=4] {'iy','ja'}, dimensions={0} | all-to-all | bytes 327680 | tf_op jit(solution)/shard_map/all_to_all | solution.py:354
  102.3 1.4 %collective-permute-done.12.other_ref = f32[320,128]{1,0:T(8,128)S(1)} collective-permute-done((f32[320,128]{1,0:T(8,128)S(1)}, f32[320,128]{1,0:T(8,128)S(1)}, u32[]{:S(2)}, u32[]{:S(2)}) %collective-permute-start.12) | collective-permute-done | bytes 163872 | tf_op jit(solution)/shard_map/ppermute | solution.py:358
  103.7 3.8 %shard_map.77 = (f32[256,128]{1,0:T(8,128)}, f32[512,128]{1,0:T(8,128)S(1)}, f32[1,128]{1,0:T(1,128)S(1)}) custom-call(f32[320,128]{1,0:T(8,128)S(1)} %bitcast.16, f32[320,128]{1,0:T(8,128)S(1)} %collective-permute-done.12.other_ref, f32[128,128]{1,0:T(8,128)S(1)} %get-tuple-element.36.gram_a_ref, f32[256,128]{1,0:T(8,128)S(1)} %get-tuple-element.37.solved_b_ref), custom_call_target="tpu_custom_call" | custom-call | tf_op jit(solution)/shard_map/pallas_call | solution.py:342
  107.5 1.5 %collective-permute-start.15 = (f32[1,128]{1,0:T(1,128)S(1)}, f32[1,128]{1,0:T(1,128)S(1)}, u32[]{:S(2)}, u32[]{:S(2)}) collective-permute-start(f32[1,128]{1,0:T(1,128)S(1)} %get-tuple-element.40), channel_id=1, source_target_pairs={{0,3},{1,0},{2,1},{3,2},{4,7},{5,4},{6,5},{7,6},{8,11},{9,8},{10,9... | collective-permute-start | bytes 1544 | tf_op jit(solution)/shard_map/ppermute | solution.py:363
  109.0 0.9 collective-permute-start.14
  109.9 0.6 collective-permute-start.13
  110.4 0.7 collective-permute-done.15
  111.1 2.9 %collective-permute-done.14 = f32[1,128]{1,0:T(1,128)S(1)} collective-permute-done((f32[1,128]{1,0:T(1,128)S(1)}, f32[1,128]{1,0:T(1,128)S(1)}, u32[]{:S(2)}, u32[]{:S(2)}) %collective-permute-start.14) | collective-permute-done | bytes 544 | tf_op jit(solution)/shard_map/ppermute | solution.py:363
  114.1 0.6 collective-permute-done.13
  114.7 0.7 broadcast_multiply_fusion
  (21 shorter events, 0.8 us)
Async XLA Ops:
  0.6 39.4 %copy-start.1 = (s32[3,1]{0,1:T(1,128)S(1)}, s32[3,1]{0,1:T(1,128)}, u32[]{:S(2)}) copy-start(s32[3,1]{0,1:T(1,128)} %param.6) | copy-start | bytes 40
  3.7 66.3 %copy-start = (bf16[1,64,64,128]{3,2,1,0:T(8,128)(2,1)S(1)}, bf16[1,64,64,128]{3,2,1,0:T(8,128)(2,1)}, u32[]{:S(2)}) copy-start(bf16[1,64,64,128]{3,2,1,0:T(8,128)(2,1)} %param.5) | copy-start | bytes 3145732
  44.8 1.3 %collective-permute-start = (f32[104,128]{1,0:T(8,128)S(1)}, f32[104,128]{1,0:T(8,128)S(1)}, u32[]{:S(2)}, u32[]{:S(2)}) collective-permute-start(f32[104,128]{1,0:T(8,128)S(1)} %get-tuple-element.27), channel_id=1, source_target_pairs={{0,32},{32,0},{1,33},{33,1},{2,34},{34,2},{3,35},{35,3},{4,36},{36... | collective-permute-start | bytes 159752 | tf_op jit(solution)/shard_map/ppermute | solution.py:358
  46.1 4.0 %collective-permute-start.7 = (f32[72,128]{1,0:T(8,128)S(1)}, f32[72,128]{1,0:T(8,128)S(1)}, u32[]{:S(2)}, u32[]{:S(2)}) collective-permute-start(f32[72,128]{1,0:T(8,128)S(1)} %get-tuple-element.32.parts_0), channel_id=1, source_target_pairs={{0,3},{1,0},{2,1},{3,2},{4,7},{5,4},{6,5},{7,6},{8,11},{9,8},{10,9... | collective-permute-start | bytes 110600 | tf_op jit(solution)/shard_map/ppermute | solution.py:363
  47.4 5.8 %collective-permute-start.6 = (f32[72,128]{1,0:T(8,128)S(1)}, f32[72,128]{1,0:T(8,128)S(1)}, u32[]{:S(2)}, u32[]{:S(2)}) collective-permute-start(f32[72,128]{1,0:T(8,128)S(1)} %get-tuple-element.32.parts_0), channel_id=1, source_target_pairs={{0,2},{1,3},{2,0},{3,1},{4,6},{5,7},{6,4},{7,5},{8,10},{9,11},{10,... | collective-permute-start | bytes 110600 | tf_op jit(solution)/shard_map/ppermute | solution.py:363
  48.1 5.3 %collective-permute-start.5 = (f32[72,128]{1,0:T(8,128)S(1)}, f32[72,128]{1,0:T(8,128)S(1)}, u32[]{:S(2)}, u32[]{:S(2)}) collective-permute-start(f32[72,128]{1,0:T(8,128)S(1)} %get-tuple-element.32.parts_0), channel_id=1, source_target_pairs={{0,1},{1,2},{2,3},{3,0},{4,5},{5,6},{6,7},{7,4},{8,9},{9,10},{10,1... | collective-permute-start | bytes 110600 | tf_op jit(solution)/shard_map/ppermute | solution.py:363
  53.5 6.5 %collective-permute-start.10 = (f32[128,128]{1,0:T(8,128)S(1)}, f32[128,128]{1,0:T(8,128)S(1)}, u32[]{:S(2)}, u32[]{:S(2)}) collective-permute-start(f32[128,128]{1,0:T(8,128)S(1)} %shard_map.73.half_0), channel_id=1, source_target_pairs={{0,192},{64,0},{128,64},{192,128},{1,193},{65,1},{129,65},{193,129... | collective-permute-start | bytes 196616 | tf_op jit(solution)/shard_map/ppermute | solution.py:363
  54.0 8.4 %collective-permute-start.9 = (f32[128,128]{1,0:T(8,128)S(1)}, f32[128,128]{1,0:T(8,128)S(1)}, u32[]{:S(2)}, u32[]{:S(2)}) collective-permute-start(f32[128,128]{1,0:T(8,128)S(1)} %shard_map.73.half_0), channel_id=1, source_target_pairs={{0,128},{64,192},{128,0},{192,64},{1,129},{65,193},{129,1},{193,65... | collective-permute-start | bytes 196616 | tf_op jit(solution)/shard_map/ppermute | solution.py:363
  56.6 5.8 %collective-permute-start.8 = (f32[128,128]{1,0:T(8,128)S(1)}, f32[128,128]{1,0:T(8,128)S(1)}, u32[]{:S(2)}, u32[]{:S(2)}) collective-permute-start(f32[128,128]{1,0:T(8,128)S(1)} %shard_map.73.half_0), channel_id=1, source_target_pairs={{0,64},{64,128},{128,192},{192,0},{1,65},{65,129},{129,193},{193,1... | collective-permute-start | bytes 196616 | tf_op jit(solution)/shard_map/ppermute | solution.py:363
  58.5 4.0 %collective-permute-start.3 = (f32[64,128]{1,0:T(8,128)S(1)}, f32[64,128]{1,0:T(8,128)S(1)}, u32[]{:S(2)}, u32[]{:S(2)}) collective-permute-start(f32[64,128]{1,0:T(8,128)S(1)} %get-tuple-element.28.half_0), channel_id=1, source_target_pairs={{0,192},{64,0},{128,64},{192,128},{1,193},{65,1},{129,65},{193,129... | collective-permute-start | bytes 98312 | tf_op jit(solution)/shard_map/ppermute | solution.py:363
  58.6 5.4 %collective-permute-start.2 = (f32[64,128]{1,0:T(8,128)S(1)}, f32[64,128]{1,0:T(8,128)S(1)}, u32[]{:S(2)}, u32[]{:S(2)}) collective-permute-start(f32[64,128]{1,0:T(8,128)S(1)} %get-tuple-element.28.half_0), channel_id=1, source_target_pairs={{0,128},{64,192},{128,0},{192,64},{1,129},{65,193},{129,1},{193,65... | collective-permute-start | bytes 98312 | tf_op jit(solution)/shard_map/ppermute | solution.py:363
  59.9 4.9 %collective-permute-start.1 = (f32[64,128]{1,0:T(8,128)S(1)}, f32[64,128]{1,0:T(8,128)S(1)}, u32[]{:S(2)}, u32[]{:S(2)}) collective-permute-start(f32[64,128]{1,0:T(8,128)S(1)} %get-tuple-element.28.half_0), channel_id=1, source_target_pairs={{0,64},{64,128},{128,192},{192,0},{1,65},{65,129},{129,193},{193,1... | collective-permute-start | bytes 98312 | tf_op jit(solution)/shard_map/ppermute | solution.py:363
  62.4 7.7 %collective-permute-start.11 = (f32[128,128]{1,0:T(8,128)S(1)}, f32[128,128]{1,0:T(8,128)S(1)}, u32[]{:S(2)}, u32[]{:S(2)}) collective-permute-start(f32[128,128]{1,0:T(8,128)S(1)} %shard_map.74.same_ref), channel_id=1, source_target_pairs={{0,32},{32,0},{1,33},{33,1},{2,34},{34,2},{3,35},{35,3},{4,36},{36... | collective-permute-start | bytes 196616 | tf_op jit(solution)/shard_map/ppermute | solution.py:358
  64.8 1.3 %collective-permute-start.4 = (f32[64,128]{1,0:T(8,128)S(1)}, f32[64,128]{1,0:T(8,128)S(1)}, u32[]{:S(2)}, u32[]{:S(2)}) collective-permute-start(f32[64,128]{1,0:T(8,128)S(1)} %shard_map.71.same_ref), channel_id=1, source_target_pairs={{0,32},{32,0},{1,33},{33,1},{2,34},{34,2},{3,35},{35,3},{4,36},{36... | collective-permute-start | bytes 98312 | tf_op jit(solution)/shard_map/ppermute | solution.py:358
  102.3 1.4 %collective-permute-start.12 = (f32[320,128]{1,0:T(8,128)S(1)}, f32[320,128]{1,0:T(8,128)S(1)}, u32[]{:S(2)}, u32[]{:S(2)}) collective-permute-start(f32[320,128]{1,0:T(8,128)S(1)} %bitcast.15), channel_id=1, source_target_pairs={{0,32},{32,0},{1,33},{33,1},{2,34},{34,2},{3,35},{35,3},{4,36},{36... | collective-permute-start | bytes 491528 | tf_op jit(solution)/shard_map/ppermute | solution.py:358
  107.5 3.6 %collective-permute-start.15 = (f32[1,128]{1,0:T(1,128)S(1)}, f32[1,128]{1,0:T(1,128)S(1)}, u32[]{:S(2)}, u32[]{:S(2)}) collective-permute-start(f32[1,128]{1,0:T(1,128)S(1)} %get-tuple-element.40), channel_id=1, source_target_pairs={{0,3},{1,0},{2,1},{3,2},{4,7},{5,4},{6,5},{7,6},{8,11},{9,8},{10,9... | collective-permute-start | bytes 1544 | tf_op jit(solution)/shard_map/ppermute | solution.py:363
  109.0 5.1 %collective-permute-start.14 = (f32[1,128]{1,0:T(1,128)S(1)}, f32[1,128]{1,0:T(1,128)S(1)}, u32[]{:S(2)}, u32[]{:S(2)}) collective-permute-start(f32[1,128]{1,0:T(1,128)S(1)} %get-tuple-element.40), channel_id=1, source_target_pairs={{0,2},{1,3},{2,0},{3,1},{4,6},{5,7},{6,4},{7,5},{8,10},{9,11},{10,... | collective-permute-start | bytes 1544 | tf_op jit(solution)/shard_map/ppermute | solution.py:363
  109.9 4.8 %collective-permute-start.13 = (f32[1,128]{1,0:T(1,128)S(1)}, f32[1,128]{1,0:T(1,128)S(1)}, u32[]{:S(2)}, u32[]{:S(2)}) collective-permute-start(f32[1,128]{1,0:T(1,128)S(1)} %get-tuple-element.40), channel_id=1, source_target_pairs={{0,1},{1,2},{2,3},{3,0},{4,5},{5,6},{6,7},{7,4},{8,9},{9,10},{10,1... | collective-permute-start | bytes 1544 | tf_op jit(solution)/shard_map/ppermute | solution.py:363

commit v8 on v7

--- a/solution.py
+++ b/solution.py
@@ -85,11 +85,16 @@
         rights += [jnp.where(lane < low + 16, panel[h], 0.0) for h in range(2)]
         rows[2 * k : 2 * k + 2] = panel
         leads = [over_rows(panel[s // 8], s % 8) for s in range(16)]
-        for n in range(2 * k + 2, count):
+        for n in range(2 * k + 2, min(2 * k + 4, count)):
             terms = [over_lanes(rows[n], low + s) * leads[s] for s in range(16)]
             while len(terms) > 1:
                 terms = [terms[i] + terms[i + 1] for i in range(0, len(terms), 2)]
             rows[n] = jnp.where(inside, 0.0, rows[n]) - terms[0]
+        if 2 * k + 4 < count:
+            later = jnp.concatenate(rows[2 * k + 4 :], axis=0)
+            update = exact_dot(later[:, low : low + 16], jnp.concatenate(panel, axis=0))
+            for m, n in enumerate(range(2 * k + 4, count)):
+                rows[n] = jnp.where(inside, 0.0, rows[n]) - update[8 * m : 8 * m + 8]
     return across_rows(jnp.concatenate(lefts, axis=0), jnp.concatenate(rights, axis=0))
 
 

time: 116 us -> 115 us (level)
  Pallas kernels: 17.4 us -> 15.9 us
    pallas_call x11, Pallas kernels: 17.4 us -> 15.9 us  [call(): pl.pallas_call(kernel, out_shape=[jax.ShapeDtypeStruct(shape, F32) for sh...]
where the time goes in v8:
time: 115 us; the launch traced here: 114 us
  blocking collectives  66.8 us (58%)
  Pallas kernels  15.9 us (14%)
  starting transfers between devices  15 us (13%)
  waiting for transfers between devices  14.8 us (13%)
    all_to_all x4, blocking collectives, exchange(): lax.all_to_all(values.reshape(chunk), axes, 0, 0, tiled=True).reshape(shape)  66.8 us
    pallas_call x11, Pallas kernels, call(): pl.pallas_call(kernel, out_shape=[jax.ShapeDtypeStruct(shape, F32) for sh...  15.9 us
    ppermute x12, starting transfers between devices, around(): lax.ppermute(values, axis, [(n, (n + step) % 4) for n in range(4)])  14.5 us
    ppermute x12, waiting for transfers between devices, around(): lax.ppermute(values, axis, [(n, (n + step) % 4) for n in range(4)])  11 us
    ppermute x4, waiting for transfers between devices, swap_cores(): return lax.ppermute(values, 'ic', [(0, 1), (1, 0)])  3.81 us
  transfers between devices with their start and end apart: 16, of which 11 were waited for; matrix products, arithmetic and copies ran while one was open for 0% of the time, Pallas kernels for 3%

profile of v8, /device:TPU:8, one launch (start us, length us, event | category | flops | bytes accessed | tf_op | source)
XLA Modules:
  0.0 113.9 jit_solution(3881407552985102863)
XLA Ops:
  0.6 3.1 %shard_map.67 = (f32[256,128]{1,0:T(8,128)S(1)}, f32[64,64,128]{2,1,0:T(8,128)S(1)}) custom-call(s32[3]{0:T(128)} %bitcast.23, bf16[64,64,128]{2,1,0:T(8,128)(2,1)} %bitcast.12, f32[256,128]{1,0:T(8,128)} %b_ref.1, f32[512,128]{1,0:T(8,128)} %c_ref.1), custom_call_target="tpu_custom_call" | custom-call | tf_op jit(solution)/shard_map/pallas_call | solution.py:347
  3.8 21.7 %all_to_all.20 = f32[32,8,128]{2,1,0:T(8,128)S(1)} all-to-all(f32[32,8,128]{2,1,0:T(8,128)S(1)} %bitcast.22), channel_id=1, replica_groups=mesh['iy'=4,'ic'=2,'ja'=8,'ka'=4] {'ja','ka'}, dimensions={0} | all-to-all | bytes 262144 | tf_op jit(solution)/shard_map/all_to_all | solution.py:359
  25.5 14.6 %all_to_all.21 = f32[32,3,4,128]{3,2,1,0:T(4,128)S(1)} all-to-all(f32[32,3,4,128]{3,2,1,0:T(4,128)S(1)} %bitcast.20), channel_id=1, replica_groups=mesh['iy'=4,'ic'=2,'ja'=8,'ka'=4] {'ja','ka'}, dimensions={0} | all-to-all | bytes 393216 | tf_op jit(solution)/shard_map/all_to_all | solution.py:359
  40.1 4.2 %shard_map.69 = (f32[256,128]{1,0:T(8,128)S(1)}, f32[128,128]{1,0:T(8,128)S(1)}, f32[104,128]{1,0:T(8,128)S(1)}, f32[104,128]{1,0:T(8,128)S(1)}) custom-call(s32[3]{0:T(128)S(1)} %bitcast.24, f32[384,128]{1,0:T(8,128)S(1)} %bitcast.14, f32[8,128]{1,0:T(8,128)S(1)} %get-tuple-element.24.diagonal_ref, f32[64,64,128]{2,1,0:T(8,128)S(1)} %get-tuple-element.25.y_ref), custom_call_target="tpu_custom_call" | custom-call | tf_op jit(solution)/shard_map/pallas_call | solution.py:347
  44.4 1.2 %collective-permute-done.other_ref = f32[104,128]{1,0:T(8,128)S(1)} collective-permute-done((f32[104,128]{1,0:T(8,128)S(1)}, f32[104,128]{1,0:T(8,128)S(1)}, u32[]{:S(2)}, u32[]{:S(2)}) %collective-permute-start) | collective-permute-done | bytes 53280 | tf_op jit(solution)/shard_map/ppermute | solution.py:363
  45.6 1.3 %collective-permute-start.7 = (f32[72,128]{1,0:T(8,128)S(1)}, f32[72,128]{1,0:T(8,128)S(1)}, u32[]{:S(2)}, u32[]{:S(2)}) collective-permute-start(f32[72,128]{1,0:T(8,128)S(1)} %get-tuple-element.32.parts_0), channel_id=1, source_target_pairs={{0,3},{1,0},{2,1},{3,2},{4,7},{5,4},{6,5},{7,6},{8,11},{9,8},{10,9... | collective-permute-start | bytes 110600 | tf_op jit(solution)/shard_map/ppermute | solution.py:368
  46.9 0.7 collective-permute-start.6
  47.5 0.7 collective-permute-start.5
  48.3 1.3 %collective-permute-done.7.parts_3 = f32[72,128]{1,0:T(8,128)S(1)} collective-permute-done((f32[72,128]{1,0:T(8,128)S(1)}, f32[72,128]{1,0:T(8,128)S(1)}, u32[]{:S(2)}, u32[]{:S(2)}) %collective-permute-start.7) | collective-permute-done | bytes 36896 | tf_op jit(solution)/shard_map/ppermute | solution.py:368
  49.6 3.0 %collective-permute-done.6.parts_2 = f32[72,128]{1,0:T(8,128)S(1)} collective-permute-done((f32[72,128]{1,0:T(8,128)S(1)}, f32[72,128]{1,0:T(8,128)S(1)}, u32[]{:S(2)}, u32[]{:S(2)}) %collective-permute-start.6) | collective-permute-done | bytes 36896 | tf_op jit(solution)/shard_map/ppermute | solution.py:368
  53.0 0.5 collective-permute-start.10
  53.5 2.6 %collective-permute-start.9 = (f32[128,128]{1,0:T(8,128)S(1)}, f32[128,128]{1,0:T(8,128)S(1)}, u32[]{:S(2)}, u32[]{:S(2)}) collective-permute-start(f32[128,128]{1,0:T(8,128)S(1)} %shard_map.73.half_0), channel_id=1, source_target_pairs={{0,128},{64,192},{128,0},{192,64},{1,129},{65,193},{129,1},{193,65... | collective-permute-start | bytes 196616 | tf_op jit(solution)/shard_map/ppermute | solution.py:368
  56.1 1.9 %collective-permute-start.8 = (f32[128,128]{1,0:T(8,128)S(1)}, f32[128,128]{1,0:T(8,128)S(1)}, u32[]{:S(2)}, u32[]{:S(2)}) collective-permute-start(f32[128,128]{1,0:T(8,128)S(1)} %shard_map.73.half_0), channel_id=1, source_target_pairs={{0,64},{64,128},{128,192},{192,0},{1,65},{65,129},{129,193},{193,1... | collective-permute-start | bytes 196616 | tf_op jit(solution)/shard_map/ppermute | solution.py:368
  58.1 1.3 %collective-permute-start.2 = (f32[64,128]{1,0:T(8,128)S(1)}, f32[64,128]{1,0:T(8,128)S(1)}, u32[]{:S(2)}, u32[]{:S(2)}) collective-permute-start(f32[64,128]{1,0:T(8,128)S(1)} %get-tuple-element.28.half_0), channel_id=1, source_target_pairs={{0,128},{64,192},{128,0},{192,64},{1,129},{65,193},{129,1},{193,65... | collective-permute-start | bytes 98312 | tf_op jit(solution)/shard_map/ppermute | solution.py:368
  59.4 2.4 %collective-permute-start.1 = (f32[64,128]{1,0:T(8,128)S(1)}, f32[64,128]{1,0:T(8,128)S(1)}, u32[]{:S(2)}, u32[]{:S(2)}) collective-permute-start(f32[64,128]{1,0:T(8,128)S(1)} %get-tuple-element.28.half_0), channel_id=1, source_target_pairs={{0,64},{64,128},{128,192},{192,0},{1,65},{65,129},{129,193},{193,1... | collective-permute-start | bytes 98312 | tf_op jit(solution)/shard_map/ppermute | solution.py:368
  61.9 0.3 collective-permute-start.11
  62.2 1.3 %collective-permute-done.2.half_2 = f32[64,128]{1,0:T(8,128)S(1)} collective-permute-done((f32[64,128]{1,0:T(8,128)S(1)}, f32[64,128]{1,0:T(8,128)S(1)}, u32[]{:S(2)}, u32[]{:S(2)}) %collective-permute-start.2) | collective-permute-done | bytes 32800 | tf_op jit(solution)/shard_map/ppermute | solution.py:368
  63.5 0.8 collective-permute-done.1.half_1
  64.4 1.2 %collective-permute-done.4.other_ref = f32[64,128]{1,0:T(8,128)S(1)} collective-permute-done((f32[64,128]{1,0:T(8,128)S(1)}, f32[64,128]{1,0:T(8,128)S(1)}, u32[]{:S(2)}, u32[]{:S(2)}) %collective-permute-start.4) | collective-permute-done | bytes 32800 | tf_op jit(solution)/shard_map/ppermute | solution.py:363
  65.6 3.4 %shard_map.72 = (f32[128,128]{1,0:T(8,128)S(1)}, f32[128,128]{1,0:T(8,128)S(1)}, f32[8,128]{1,0:T(8,128)S(1)}, f32[256,128]{1,0:T(8,128)}) custom-call(f32[64,128]{1,0:T(8,128)S(1)} %shard_map.71.same_ref, f32[64,128]{1,0:T(8,128)S(1)} %collective-permute-done.4.other_ref, f32[128,128]{1,0:T(8,128)S(1)} %get-tuple-element.29.gram_c_ref, ...), custom_call_target="tpu_custom_call" | custom-call | tf_op jit(solution)/shard_map/pallas_call | solution.py:347
  69.0 1.5 %shard_map.75 = (f32[256,128]{1,0:T(8,128)S(1)}, f32[256,128]{1,0:T(8,128)S(1)}) custom-call(s32[3]{0:T(128)S(1)} %bitcast.25, f32[128,128]{1,0:T(8,128)S(1)} %shard_map.74.same_ref, f32[128,128]{1,0:T(8,128)S(1)} %collective-permute-done.11.other_ref, f32[128,128]{1,0:T(8,128)S(1)} %get-tuple-element.33.solver_ref, ...), custom_call_target="tpu_custom_call" | custom-call | tf_op jit(solution)/shard_map/pallas_call | solution.py:347
  70.5 16.4 %all_to_all.22 = f32[64,4,128]{2,1,0:T(4,128)S(1)} all-to-all(f32[64,4,128]{2,1,0:T(4,128)S(1)} %bitcast.21), channel_id=1, replica_groups=mesh['iy'=4,'ic'=2,'ja'=8,'ka'=4] {'iy','ic','ja'}, dimensions={0} | all-to-all | bytes 262144 | tf_op jit(solution)/shard_map/all_to_all | solution.py:359
  87.0 14.2 %all_to_all.23 = f32[32,5,2,128]{3,2,1,0:T(2,128)S(1)} all-to-all(f32[32,5,2,128]{3,2,1,0:T(2,128)S(1)} %bitcast.17), channel_id=1, replica_groups=mesh['iy'=4,'ic'=2,'ja'=8,'ka'=4] {'iy','ja'}, dimensions={0} | all-to-all | bytes 327680 | tf_op jit(solution)/shard_map/all_to_all | solution.py:359
  101.2 1.4 %collective-permute-done.12.other_ref = f32[320,128]{1,0:T(8,128)S(1)} collective-permute-done((f32[320,128]{1,0:T(8,128)S(1)}, f32[320,128]{1,0:T(8,128)S(1)}, u32[]{:S(2)}, u32[]{:S(2)}) %collective-permute-start.12) | collective-permute-done | bytes 163872 | tf_op jit(solution)/shard_map/ppermute | solution.py:363
  102.6 3.4 %shard_map.77 = (f32[256,128]{1,0:T(8,128)}, f32[512,128]{1,0:T(8,128)S(1)}, f32[1,128]{1,0:T(1,128)S(1)}) custom-call(f32[320,128]{1,0:T(8,128)S(1)} %bitcast.16, f32[320,128]{1,0:T(8,128)S(1)} %collective-permute-done.12.other_ref, f32[128,128]{1,0:T(8,128)S(1)} %get-tuple-element.36.gram_a_ref, f32[256,128]{1,0:T(8,128)S(1)} %get-tuple-element.37.solved_b_ref), custom_call_target="tpu_custom_call" | custom-call | tf_op jit(solution)/shard_map/pallas_call | solution.py:347
  106.0 1.5 %collective-permute-start.15 = (f32[1,128]{1,0:T(1,128)S(1)}, f32[1,128]{1,0:T(1,128)S(1)}, u32[]{:S(2)}, u32[]{:S(2)}) collective-permute-start(f32[1,128]{1,0:T(1,128)S(1)} %get-tuple-element.40), channel_id=1, source_target_pairs={{0,3},{1,0},{2,1},{3,2},{4,7},{5,4},{6,5},{7,6},{8,11},{9,8},{10,9... | collective-permute-start | bytes 1544 | tf_op jit(solution)/shard_map/ppermute | solution.py:368
  107.5 0.9 collective-permute-start.14
  108.4 0.5 collective-permute-start.13
  108.9 0.7 collective-permute-done.15
  109.6 2.9 %collective-permute-done.14 = f32[1,128]{1,0:T(1,128)S(1)} collective-permute-done((f32[1,128]{1,0:T(1,128)S(1)}, f32[1,128]{1,0:T(1,128)S(1)}, u32[]{:S(2)}, u32[]{:S(2)}) %collective-permute-start.14) | collective-permute-done | bytes 544 | tf_op jit(solution)/shard_map/ppermute | solution.py:368
  112.5 0.6 collective-permute-done.13
  113.2 0.7 broadcast_multiply_fusion
  (21 shorter events, 0.9 us)
Async XLA Ops:
  0.6 39.4 %copy-start.1 = (s32[3,1]{0,1:T(1,128)S(1)}, s32[3,1]{0,1:T(1,128)}, u32[]{:S(2)}) copy-start(s32[3,1]{0,1:T(1,128)} %param.6) | copy-start | bytes 40
  3.7 65.3 %copy-start = (bf16[1,64,64,128]{3,2,1,0:T(8,128)(2,1)S(1)}, bf16[1,64,64,128]{3,2,1,0:T(8,128)(2,1)}, u32[]{:S(2)}) copy-start(bf16[1,64,64,128]{3,2,1,0:T(8,128)(2,1)} %param.5) | copy-start | bytes 3145732
  44.3 1.3 %collective-permute-start = (f32[104,128]{1,0:T(8,128)S(1)}, f32[104,128]{1,0:T(8,128)S(1)}, u32[]{:S(2)}, u32[]{:S(2)}) collective-permute-start(f32[104,128]{1,0:T(8,128)S(1)} %get-tuple-element.27), channel_id=1, source_target_pairs={{0,32},{32,0},{1,33},{33,1},{2,34},{34,2},{3,35},{35,3},{4,36},{36... | collective-permute-start | bytes 159752 | tf_op jit(solution)/shard_map/ppermute | solution.py:363
  45.6 4.0 %collective-permute-start.7 = (f32[72,128]{1,0:T(8,128)S(1)}, f32[72,128]{1,0:T(8,128)S(1)}, u32[]{:S(2)}, u32[]{:S(2)}) collective-permute-start(f32[72,128]{1,0:T(8,128)S(1)} %get-tuple-element.32.parts_0), channel_id=1, source_target_pairs={{0,3},{1,0},{2,1},{3,2},{4,7},{5,4},{6,5},{7,6},{8,11},{9,8},{10,9... | collective-permute-start | bytes 110600 | tf_op jit(solution)/shard_map/ppermute | solution.py:368
  46.9 5.8 %collective-permute-start.6 = (f32[72,128]{1,0:T(8,128)S(1)}, f32[72,128]{1,0:T(8,128)S(1)}, u32[]{:S(2)}, u32[]{:S(2)}) collective-permute-start(f32[72,128]{1,0:T(8,128)S(1)} %get-tuple-element.32.parts_0), channel_id=1, source_target_pairs={{0,2},{1,3},{2,0},{3,1},{4,6},{5,7},{6,4},{7,5},{8,10},{9,11},{10,... | collective-permute-start | bytes 110600 | tf_op jit(solution)/shard_map/ppermute | solution.py:368
  47.5 5.3 %collective-permute-start.5 = (f32[72,128]{1,0:T(8,128)S(1)}, f32[72,128]{1,0:T(8,128)S(1)}, u32[]{:S(2)}, u32[]{:S(2)}) collective-permute-start(f32[72,128]{1,0:T(8,128)S(1)} %get-tuple-element.32.parts_0), channel_id=1, source_target_pairs={{0,1},{1,2},{2,3},{3,0},{4,5},{5,6},{6,7},{7,4},{8,9},{9,10},{10,1... | collective-permute-start | bytes 110600 | tf_op jit(solution)/shard_map/ppermute | solution.py:368
  53.0 6.5 %collective-permute-start.10 = (f32[128,128]{1,0:T(8,128)S(1)}, f32[128,128]{1,0:T(8,128)S(1)}, u32[]{:S(2)}, u32[]{:S(2)}) collective-permute-start(f32[128,128]{1,0:T(8,128)S(1)} %shard_map.73.half_0), channel_id=1, source_target_pairs={{0,192},{64,0},{128,64},{192,128},{1,193},{65,1},{129,65},{193,129... | collective-permute-start | bytes 196616 | tf_op jit(solution)/shard_map/ppermute | solution.py:368
  53.5 8.4 %collective-permute-start.9 = (f32[128,128]{1,0:T(8,128)S(1)}, f32[128,128]{1,0:T(8,128)S(1)}, u32[]{:S(2)}, u32[]{:S(2)}) collective-permute-start(f32[128,128]{1,0:T(8,128)S(1)} %shard_map.73.half_0), channel_id=1, source_target_pairs={{0,128},{64,192},{128,0},{192,64},{1,129},{65,193},{129,1},{193,65... | collective-permute-start | bytes 196616 | tf_op jit(solution)/shard_map/ppermute | solution.py:368
  56.1 5.8 %collective-permute-start.8 = (f32[128,128]{1,0:T(8,128)S(1)}, f32[128,128]{1,0:T(8,128)S(1)}, u32[]{:S(2)}, u32[]{:S(2)}) collective-permute-start(f32[128,128]{1,0:T(8,128)S(1)} %shard_map.73.half_0), channel_id=1, source_target_pairs={{0,64},{64,128},{128,192},{192,0},{1,65},{65,129},{129,193},{193,1... | collective-permute-start | bytes 196616 | tf_op jit(solution)/shard_map/ppermute | solution.py:368
  58.0 4.2 %collective-permute-start.3 = (f32[64,128]{1,0:T(8,128)S(1)}, f32[64,128]{1,0:T(8,128)S(1)}, u32[]{:S(2)}, u32[]{:S(2)}) collective-permute-start(f32[64,128]{1,0:T(8,128)S(1)} %get-tuple-element.28.half_0), channel_id=1, source_target_pairs={{0,192},{64,0},{128,64},{192,128},{1,193},{65,1},{129,65},{193,129... | collective-permute-start | bytes 98312 | tf_op jit(solution)/shard_map/ppermute | solution.py:368
  58.1 5.4 %collective-permute-start.2 = (f32[64,128]{1,0:T(8,128)S(1)}, f32[64,128]{1,0:T(8,128)S(1)}, u32[]{:S(2)}, u32[]{:S(2)}) collective-permute-start(f32[64,128]{1,0:T(8,128)S(1)} %get-tuple-element.28.half_0), channel_id=1, source_target_pairs={{0,128},{64,192},{128,0},{192,64},{1,129},{65,193},{129,1},{193,65... | collective-permute-start | bytes 98312 | tf_op jit(solution)/shard_map/ppermute | solution.py:368
  59.4 4.9 %collective-permute-start.1 = (f32[64,128]{1,0:T(8,128)S(1)}, f32[64,128]{1,0:T(8,128)S(1)}, u32[]{:S(2)}, u32[]{:S(2)}) collective-permute-start(f32[64,128]{1,0:T(8,128)S(1)} %get-tuple-element.28.half_0), channel_id=1, source_target_pairs={{0,64},{64,128},{128,192},{192,0},{1,65},{65,129},{129,193},{193,1... | collective-permute-start | bytes 98312 | tf_op jit(solution)/shard_map/ppermute | solution.py:368
  61.9 7.1 %collective-permute-start.11 = (f32[128,128]{1,0:T(8,128)S(1)}, f32[128,128]{1,0:T(8,128)S(1)}, u32[]{:S(2)}, u32[]{:S(2)}) collective-permute-start(f32[128,128]{1,0:T(8,128)S(1)} %shard_map.74.same_ref), channel_id=1, source_target_pairs={{0,32},{32,0},{1,33},{33,1},{2,34},{34,2},{3,35},{35,3},{4,36},{36... | collective-permute-start | bytes 196616 | tf_op jit(solution)/shard_map/ppermute | solution.py:363
  64.3 1.3 %collective-permute-start.4 = (f32[64,128]{1,0:T(8,128)S(1)}, f32[64,128]{1,0:T(8,128)S(1)}, u32[]{:S(2)}, u32[]{:S(2)}) collective-permute-start(f32[64,128]{1,0:T(8,128)S(1)} %shard_map.71.same_ref), channel_id=1, source_target_pairs={{0,32},{32,0},{1,33},{33,1},{2,34},{34,2},{3,35},{35,3},{4,36},{36... | collective-permute-start | bytes 98312 | tf_op jit(solution)/shard_map/ppermute | solution.py:363
  101.2 1.4 %collective-permute-start.12 = (f32[320,128]{1,0:T(8,128)S(1)}, f32[320,128]{1,0:T(8,128)S(1)}, u32[]{:S(2)}, u32[]{:S(2)}) collective-permute-start(f32[320,128]{1,0:T(8,128)S(1)} %bitcast.15), channel_id=1, source_target_pairs={{0,32},{32,0},{1,33},{33,1},{2,34},{34,2},{3,35},{35,3},{4,36},{36... | collective-permute-start | bytes 491528 | tf_op jit(solution)/shard_map/ppermute | solution.py:363
  106.0 3.6 %collective-permute-start.15 = (f32[1,128]{1,0:T(1,128)S(1)}, f32[1,128]{1,0:T(1,128)S(1)}, u32[]{:S(2)}, u32[]{:S(2)}) collective-permute-start(f32[1,128]{1,0:T(1,128)S(1)} %get-tuple-element.40), channel_id=1, source_target_pairs={{0,3},{1,0},{2,1},{3,2},{4,7},{5,4},{6,5},{7,6},{8,11},{9,8},{10,9... | collective-permute-start | bytes 1544 | tf_op jit(solution)/shard_map/ppermute | solution.py:368
  107.5 5.1 %collective-permute-start.14 = (f32[1,128]{1,0:T(1,128)S(1)}, f32[1,128]{1,0:T(1,128)S(1)}, u32[]{:S(2)}, u32[]{:S(2)}) collective-permute-start(f32[1,128]{1,0:T(1,128)S(1)} %get-tuple-element.40), channel_id=1, source_target_pairs={{0,2},{1,3},{2,0},{3,1},{4,6},{5,7},{6,4},{7,5},{8,10},{9,11},{10,... | collective-permute-start | bytes 1544 | tf_op jit(solution)/shard_map/ppermute | solution.py:368
  108.4 4.8 %collective-permute-start.13 = (f32[1,128]{1,0:T(1,128)S(1)}, f32[1,128]{1,0:T(1,128)S(1)}, u32[]{:S(2)}, u32[]{:S(2)}) collective-permute-start(f32[1,128]{1,0:T(1,128)S(1)} %get-tuple-element.40), channel_id=1, source_target_pairs={{0,1},{1,2},{2,3},{3,0},{4,5},{5,6},{6,7},{7,4},{8,9},{9,10},{10,1... | collective-permute-start | bytes 1544 | tf_op jit(solution)/shard_map/ppermute | solution.py:368

commit v9 on v8

--- a/solution.py
+++ b/solution.py
@@ -246,12 +246,12 @@
         ref[96:104, :] = jnp.full((8, RANK), slot[1].astype(F32))
 
 
-def merge_kernel(keep_ref, other_ref, parts_ref, gram_ref):
+def merge_kernel(keep_ref, other_ref, parts_ref):
     first = lax.broadcasted_iota(jnp.int32, (8, RANK), 0) == 0
     parts_ref[0:32, :] = keep_ref[0:32, :]
     parts_ref[32:64, :] = other_ref[0:32, :]
     parts_ref[64:72, :] = jnp.where(first, keep_ref[96:104, :], other_ref[96:104, :])
-    gram_ref[...] = keep_ref[32:96, :] + other_ref[32:96, :]
+    parts_ref[72:136, :] = keep_ref[32:96, :] + other_ref[32:96, :]
 
 
 def in_source_order(axis, refs, all_ref):
@@ -262,23 +262,24 @@
         all_ref[pl.ds(pl.multiple_of(source * size, 8), size), :] = ref[...]
 
 
-def dense_kernel(parts_0, parts_1, parts_2, parts_3, half_ref, all_ref):
-    in_source_order("ka", (parts_0, parts_1, parts_2, parts_3), all_ref)
+def dense_kernel(parts_0, parts_1, parts_2, parts_3, half_ref, gram_ref, all_ref):
+    in_source_order("iy", (parts_0, parts_1, parts_2, parts_3), all_ref)
     sums = [jnp.zeros((32, RANK), F32) for _ in range(SLOTS)]
     for n in range(4):
         for part in range(2):
-            rows = all_ref[72 * n + 32 * part : 72 * n + 32 * part + 32, :]
-            ids = all_ref[72 * n + 64 + part : 72 * n + 65 + part, :]
+            rows = all_ref[136 * n + 32 * part : 136 * n + 32 * part + 32, :]
+            ids = all_ref[136 * n + 64 + part : 136 * n + 65 + part, :]
             for slot in range(SLOTS):
                 sums[slot] = sums[slot] + jnp.where(ids == slot, rows, 0.0)
     for slot in range(SLOTS):
         half_ref[32 * slot : 32 * slot + 32, :] = sums[slot]
+    grams = [all_ref[136 * n + 72 : 136 * n + 136, :] for n in range(4)]
+    gram_ref[...] = (grams[0] + grams[1]) + (grams[2] + grams[3])
 
 
 def sum_kernel(half_0, half_1, half_2, half_3, sum_ref, all_ref):
-    in_source_order("iy", (half_0, half_1, half_2, half_3), all_ref)
-    size = sum_ref.shape[0]
-    parts = [all_ref[size * n : size * n + size, :] for n in range(4)]
+    in_source_order("ka", (half_0, half_1, half_2, half_3), all_ref)
+    parts = [all_ref[RANK * n : RANK * n + RANK, :] for n in range(4)]
     sum_ref[...] = (parts[0] + parts[1]) + (parts[2] + parts[3])
 
 
@@ -399,18 +400,16 @@
         1,
         [pltpu.VMEM((BJ, RANK), F32), pltpu.VMEM(full, F32)],
     )
-    parts, gram_half = call(merge_kernel, (keep, swap_cores(send)), [(72, RANK), (64, RANK)])
-    around_x = around("ka", parts)
-    (gram_half,) = call(
-        sum_kernel,
-        (gram_half, *around("iy", gram_half)),
-        [(64, RANK)],
+    (parts,) = call(merge_kernel, (keep, swap_cores(send)), [(136, RANK)])
+    half, gram_half = call(
+        dense_kernel,
+        (parts, *around("iy", parts)),
+        [full, (64, RANK)],
         0,
-        [pltpu.VMEM((256, RANK), F32)],
-    )
-    (half,) = call(dense_kernel, (parts, *around_x), [full], 0, [pltpu.VMEM((288, RANK), F32)])
+        [pltpu.VMEM((544, RANK), F32)],
+    )
     other = swap_cores(gram_half)
-    around_y = around("iy", half)
+    around_x = around("ka", half)
     solver, gram_a, scale, loading_a = call(
         second_inverse_kernel,
         (gram_half, other, gram_c, solved_a),
@@ -418,7 +417,7 @@
         0,
         [pltpu.VMEM(full, F32)],
     )
-    (half,) = call(sum_kernel, (half, *around_y), [full], 0, [pltpu.VMEM((512, RANK), F32)])
+    (half,) = call(sum_kernel, (half, *around_x), [full], 0, [pltpu.VMEM((512, RANK), F32)])
 
     solved_b, chunk = call(
         third_kernel,

time: 115 us -> 111 us (0.965)
  starting transfers between devices: 15 us -> 11 us
    ppermute x12 -> x9, starting transfers between devices: 14.5 us -> 10.3 us  [around(): lax.ppermute(values, axis, [(n, (n + step) % 4) for n in range(4)])]
    ppermute x12 -> x9, waiting for transfers between devices: 11 us -> 11.9 us  [around(): lax.ppermute(values, axis, [(n, (n + step) % 4) for n in range(4)])]
    pallas_call x11 -> x10, Pallas kernels: 15.9 us -> 15.8 us  [call(): pl.pallas_call(kernel, out_shape=[jax.ShapeDtypeStruct(shape, F32) for sh...]
  transfers between devices with their start and end apart: 16 -> 13, of which waited for: 11 -> 11; matrix products, arithmetic and copies ran while one was open for 0% -> 0% of each run, Pallas kernels for 3% -> 3%
where the time goes in v9:
time: 111 us
  blocking collectives  67 us (60%)
  Pallas kernels  15.8 us (14%)
  waiting for transfers between devices  15.5 us (14%)
  starting transfers between devices  11 us (10%)
    all_to_all x4, blocking collectives, exchange(): lax.all_to_all(values.reshape(chunk), axes, 0, 0, tiled=True).reshape(shape)  67 us
    pallas_call x10, Pallas kernels, call(): pl.pallas_call(kernel, out_shape=[jax.ShapeDtypeStruct(shape, F32) for sh...  15.8 us
    ppermute x9, waiting for transfers between devices, around(): lax.ppermute(values, axis, [(n, (n + step) % 4) for n in range(4)])  11.9 us
    ppermute x9, starting transfers between devices, around(): lax.ppermute(values, axis, [(n, (n + step) % 4) for n in range(4)])  10.3 us
    ppermute x4, waiting for transfers between devices, swap_cores(): return lax.ppermute(values, 'ic', [(0, 1), (1, 0)])  3.6 us
  transfers between devices with their start and end apart: 13, of which 11 were waited for; matrix products, arithmetic and copies ran while one was open for 0% of the time, Pallas kernels for 3%

profile of v9, /device:TPU:8, one launch (start us, length us, event | category | flops | bytes accessed | tf_op | source)
XLA Modules:
  0.0 110.8 jit_solution(116784309705495568)
XLA Ops:
  0.6 3.1 %shard_map.67 = (f32[256,128]{1,0:T(8,128)S(1)}, f32[64,64,128]{2,1,0:T(8,128)S(1)}) custom-call(s32[3]{0:T(128)} %bitcast.23, bf16[64,64,128]{2,1,0:T(8,128)(2,1)} %bitcast.12, f32[256,128]{1,0:T(8,128)} %b_ref.1, f32[512,128]{1,0:T(8,128)} %c_ref.1), custom_call_target="tpu_custom_call" | custom-call | tf_op jit(solution)/shard_map/pallas_call | solution.py:348
  3.8 21.7 %all_to_all.20 = f32[32,8,128]{2,1,0:T(8,128)S(1)} all-to-all(f32[32,8,128]{2,1,0:T(8,128)S(1)} %bitcast.22), channel_id=1, replica_groups=mesh['iy'=4,'ic'=2,'ja'=8,'ka'=4] {'ja','ka'}, dimensions={0} | all-to-all | bytes 262144 | tf_op jit(solution)/shard_map/all_to_all | solution.py:360
  25.5 14.6 %all_to_all.21 = f32[32,3,4,128]{3,2,1,0:T(4,128)S(1)} all-to-all(f32[32,3,4,128]{3,2,1,0:T(4,128)S(1)} %bitcast.20), channel_id=1, replica_groups=mesh['iy'=4,'ic'=2,'ja'=8,'ka'=4] {'ja','ka'}, dimensions={0} | all-to-all | bytes 393216 | tf_op jit(solution)/shard_map/all_to_all | solution.py:360
  40.1 4.2 %shard_map.69 = (f32[256,128]{1,0:T(8,128)S(1)}, f32[128,128]{1,0:T(8,128)S(1)}, f32[104,128]{1,0:T(8,128)S(1)}, f32[104,128]{1,0:T(8,128)S(1)}) custom-call(s32[3]{0:T(128)S(1)} %bitcast.24, f32[384,128]{1,0:T(8,128)S(1)} %bitcast.14, f32[8,128]{1,0:T(8,128)S(1)} %get-tuple-element.24.diagonal_ref, f32[64,64,128]{2,1,0:T(8,128)S(1)} %get-tuple-element.25.y_ref), custom_call_target="tpu_custom_call" | custom-call | tf_op jit(solution)/shard_map/pallas_call | solution.py:348
  44.4 1.2 %collective-permute-done.other_ref = f32[104,128]{1,0:T(8,128)S(1)} collective-permute-done((f32[104,128]{1,0:T(8,128)S(1)}, f32[104,128]{1,0:T(8,128)S(1)}, u32[]{:S(2)}, u32[]{:S(2)}) %collective-permute-start) | collective-permute-done | bytes 53280 | tf_op jit(solution)/shard_map/ppermute | solution.py:364
  45.6 0.5 collective-permute-start.3
  46.1 2.6 %collective-permute-start.2 = (f32[136,128]{1,0:T(8,128)S(1)}, f32[136,128]{1,0:T(8,128)S(1)}, u32[]{:S(2)}, u32[]{:S(2)}) collective-permute-start(f32[136,128]{1,0:T(8,128)S(1)} %shard_map.70.parts_0), channel_id=1, source_target_pairs={{0,128},{64,192},{128,0},{192,64},{1,129},{65,193},{129,1},{193,65... | collective-permute-start | bytes 208904 | tf_op jit(solution)/shard_map/ppermute | solution.py:369
  48.7 1.9 %collective-permute-start.1 = (f32[136,128]{1,0:T(8,128)S(1)}, f32[136,128]{1,0:T(8,128)S(1)}, u32[]{:S(2)}, u32[]{:S(2)}) collective-permute-start(f32[136,128]{1,0:T(8,128)S(1)} %shard_map.70.parts_0), channel_id=1, source_target_pairs={{0,64},{64,128},{128,192},{192,0},{1,65},{65,129},{129,193},{193,1... | collective-permute-start | bytes 208904 | tf_op jit(solution)/shard_map/ppermute | solution.py:369
  50.6 1.8 %collective-permute-done.2.parts_2 = f32[136,128]{1,0:T(8,128)S(1)} collective-permute-done((f32[136,128]{1,0:T(8,128)S(1)}, f32[136,128]{1,0:T(8,128)S(1)}, u32[]{:S(2)}, u32[]{:S(2)}) %collective-permute-start.2) | collective-permute-done | bytes 69664 | tf_op jit(solution)/shard_map/ppermute | solution.py:369
  52.4 0.8 collective-permute-done.1.parts_1
  53.3 1.3 %collective-permute-start.7 = (f32[128,128]{1,0:T(8,128)S(1)}, f32[128,128]{1,0:T(8,128)S(1)}, u32[]{:S(2)}, u32[]{:S(2)}) collective-permute-start(f32[128,128]{1,0:T(8,128)S(1)} %get-tuple-element.32.half_0), channel_id=1, source_target_pairs={{0,3},{1,0},{2,1},{3,2},{4,7},{5,4},{6,5},{7,6},{8,11},{9,8},{10,9... | collective-permute-start | bytes 196616 | tf_op jit(solution)/shard_map/ppermute | solution.py:369
  54.6 0.7 collective-permute-start.6
  55.2 0.7 collective-permute-start.5
  56.0 1.7 %collective-permute-done.7.half_3 = f32[128,128]{1,0:T(8,128)S(1)} collective-permute-done((f32[128,128]{1,0:T(8,128)S(1)}, f32[128,128]{1,0:T(8,128)S(1)}, u32[]{:S(2)}, u32[]{:S(2)}) %collective-permute-start.7) | collective-permute-done | bytes 65568 | tf_op jit(solution)/shard_map/ppermute | solution.py:369
  57.6 2.7 %collective-permute-done.6.half_2 = f32[128,128]{1,0:T(8,128)S(1)} collective-permute-done((f32[128,128]{1,0:T(8,128)S(1)}, f32[128,128]{1,0:T(8,128)S(1)}, u32[]{:S(2)}, u32[]{:S(2)}) %collective-permute-start.6) | collective-permute-done | bytes 65568 | tf_op jit(solution)/shard_map/ppermute | solution.py:369
  60.4 0.7 collective-permute-done.5.half_1
  61.2 0.5 collective-permute-start.4
  61.7 1.0 collective-permute-done.4.other_ref
  62.7 3.4 %shard_map.72 = (f32[128,128]{1,0:T(8,128)S(1)}, f32[128,128]{1,0:T(8,128)S(1)}, f32[8,128]{1,0:T(8,128)S(1)}, f32[256,128]{1,0:T(8,128)}) custom-call(f32[64,128]{1,0:T(8,128)S(1)} %get-tuple-element.28.same_ref, f32[64,128]{1,0:T(8,128)S(1)} %collective-permute-done.4.other_ref, f32[128,128]{1,0:T(8,128)S(1)} %get-tuple-element.29.gram_c_ref, ...), custom_call_target="tpu_custom_call" | custom-call | tf_op jit(solution)/shard_map/pallas_call | solution.py:348
  66.0 1.5 %shard_map.74 = (f32[256,128]{1,0:T(8,128)S(1)}, f32[256,128]{1,0:T(8,128)S(1)}) custom-call(s32[3]{0:T(128)S(1)} %bitcast.25, f32[128,128]{1,0:T(8,128)S(1)} %shard_map.73.same_ref, f32[128,128]{1,0:T(8,128)S(1)} %collective-permute-done.8.other_ref, f32[128,128]{1,0:T(8,128)S(1)} %get-tuple-element.33.solver_ref, ...), custom_call_target="tpu_custom_call" | custom-call | tf_op jit(solution)/shard_map/pallas_call | solution.py:348
  67.6 16.6 %all_to_all.22 = f32[64,4,128]{2,1,0:T(4,128)S(1)} all-to-all(f32[64,4,128]{2,1,0:T(4,128)S(1)} %bitcast.21), channel_id=1, replica_groups=mesh['iy'=4,'ic'=2,'ja'=8,'ka'=4] {'iy','ic','ja'}, dimensions={0} | all-to-all | bytes 262144 | tf_op jit(solution)/shard_map/all_to_all | solution.py:360
  84.1 0.1 shard_map.75
  84.3 14.2 %all_to_all.23 = f32[32,5,2,128]{3,2,1,0:T(2,128)S(1)} all-to-all(f32[32,5,2,128]{3,2,1,0:T(2,128)S(1)} %bitcast.17), channel_id=1, replica_groups=mesh['iy'=4,'ic'=2,'ja'=8,'ka'=4] {'iy','ja'}, dimensions={0} | all-to-all | bytes 327680 | tf_op jit(solution)/shard_map/all_to_all | solution.py:360
  98.4 1.4 %collective-permute-done.9.other_ref = f32[320,128]{1,0:T(8,128)S(1)} collective-permute-done((f32[320,128]{1,0:T(8,128)S(1)}, f32[320,128]{1,0:T(8,128)S(1)}, u32[]{:S(2)}, u32[]{:S(2)}) %collective-permute-start.9) | collective-permute-done | bytes 163872 | tf_op jit(solution)/shard_map/ppermute | solution.py:364
  99.8 3.3 %shard_map.76 = (f32[256,128]{1,0:T(8,128)}, f32[512,128]{1,0:T(8,128)S(1)}, f32[1,128]{1,0:T(1,128)S(1)}) custom-call(f32[320,128]{1,0:T(8,128)S(1)} %bitcast.16, f32[320,128]{1,0:T(8,128)S(1)} %collective-permute-done.9.other_ref, f32[128,128]{1,0:T(8,128)S(1)} %get-tuple-element.36.gram_a_ref, f32[256,128]{1,0:T(8,128)S(1)} %get-tuple-element.37.solved_b_ref), custom_call_target="tpu_custom_call" | custom-call | tf_op jit(solution)/shard_map/pallas_call | solution.py:348
  103.2 1.2 %collective-permute-start.12 = (f32[1,128]{1,0:T(1,128)S(1)}, f32[1,128]{1,0:T(1,128)S(1)}, u32[]{:S(2)}, u32[]{:S(2)}) collective-permute-start(f32[1,128]{1,0:T(1,128)S(1)} %get-tuple-element.40), channel_id=1, source_target_pairs={{0,3},{1,0},{2,1},{3,2},{4,7},{5,4},{6,5},{7,6},{8,11},{9,8},{10,9... | collective-permute-start | bytes 1544 | tf_op jit(solution)/shard_map/ppermute | solution.py:369
  104.4 0.9 collective-permute-start.11
  105.3 0.6 collective-permute-start.10
  105.8 1.0 collective-permute-done.12
  106.8 2.6 %collective-permute-done.11 = f32[1,128]{1,0:T(1,128)S(1)} collective-permute-done((f32[1,128]{1,0:T(1,128)S(1)}, f32[1,128]{1,0:T(1,128)S(1)}, u32[]{:S(2)}, u32[]{:S(2)}) %collective-permute-start.11) | collective-permute-done | bytes 544 | tf_op jit(solution)/shard_map/ppermute | solution.py:369
  109.4 0.6 collective-permute-done.10
  110.1 0.7 broadcast_multiply_fusion
  (14 shorter events, 0.4 us)
Async XLA Ops:
  0.6 39.4 %copy-start.1 = (s32[3,1]{0,1:T(1,128)S(1)}, s32[3,1]{0,1:T(1,128)}, u32[]{:S(2)}) copy-start(s32[3,1]{0,1:T(1,128)} %param.6) | copy-start | bytes 40
  3.7 62.3 %copy-start = (bf16[1,64,64,128]{3,2,1,0:T(8,128)(2,1)S(1)}, bf16[1,64,64,128]{3,2,1,0:T(8,128)(2,1)}, u32[]{:S(2)}) copy-start(bf16[1,64,64,128]{3,2,1,0:T(8,128)(2,1)} %param.5) | copy-start | bytes 3145732
  44.3 1.3 %collective-permute-start = (f32[104,128]{1,0:T(8,128)S(1)}, f32[104,128]{1,0:T(8,128)S(1)}, u32[]{:S(2)}, u32[]{:S(2)}) collective-permute-start(f32[104,128]{1,0:T(8,128)S(1)} %get-tuple-element.27), channel_id=1, source_target_pairs={{0,32},{32,0},{1,33},{33,1},{2,34},{34,2},{3,35},{35,3},{4,36},{36... | collective-permute-start | bytes 159752 | tf_op jit(solution)/shard_map/ppermute | solution.py:364
  45.6 5.0 %collective-permute-start.3 = (f32[136,128]{1,0:T(8,128)S(1)}, f32[136,128]{1,0:T(8,128)S(1)}, u32[]{:S(2)}, u32[]{:S(2)}) collective-permute-start(f32[136,128]{1,0:T(8,128)S(1)} %shard_map.70.parts_0), channel_id=1, source_target_pairs={{0,192},{64,0},{128,64},{192,128},{1,193},{65,1},{129,65},{193,129... | collective-permute-start | bytes 208904 | tf_op jit(solution)/shard_map/ppermute | solution.py:369
  46.1 6.3 %collective-permute-start.2 = (f32[136,128]{1,0:T(8,128)S(1)}, f32[136,128]{1,0:T(8,128)S(1)}, u32[]{:S(2)}, u32[]{:S(2)}) collective-permute-start(f32[136,128]{1,0:T(8,128)S(1)} %shard_map.70.parts_0), channel_id=1, source_target_pairs={{0,128},{64,192},{128,0},{192,64},{1,129},{65,193},{129,1},{193,65... | collective-permute-start | bytes 208904 | tf_op jit(solution)/shard_map/ppermute | solution.py:369
  48.7 4.5 %collective-permute-start.1 = (f32[136,128]{1,0:T(8,128)S(1)}, f32[136,128]{1,0:T(8,128)S(1)}, u32[]{:S(2)}, u32[]{:S(2)}) collective-permute-start(f32[136,128]{1,0:T(8,128)S(1)} %shard_map.70.parts_0), channel_id=1, source_target_pairs={{0,64},{64,128},{128,192},{192,0},{1,65},{65,129},{129,193},{193,1... | collective-permute-start | bytes 208904 | tf_op jit(solution)/shard_map/ppermute | solution.py:369
  53.3 4.3 %collective-permute-start.7 = (f32[128,128]{1,0:T(8,128)S(1)}, f32[128,128]{1,0:T(8,128)S(1)}, u32[]{:S(2)}, u32[]{:S(2)}) collective-permute-start(f32[128,128]{1,0:T(8,128)S(1)} %get-tuple-element.32.half_0), channel_id=1, source_target_pairs={{0,3},{1,0},{2,1},{3,2},{4,7},{5,4},{6,5},{7,6},{8,11},{9,8},{10,9... | collective-permute-start | bytes 196616 | tf_op jit(solution)/shard_map/ppermute | solution.py:369
  54.6 5.8 %collective-permute-start.6 = (f32[128,128]{1,0:T(8,128)S(1)}, f32[128,128]{1,0:T(8,128)S(1)}, u32[]{:S(2)}, u32[]{:S(2)}) collective-permute-start(f32[128,128]{1,0:T(8,128)S(1)} %get-tuple-element.32.half_0), channel_id=1, source_target_pairs={{0,2},{1,3},{2,0},{3,1},{4,6},{5,7},{6,4},{7,5},{8,10},{9,11},{10,... | collective-permute-start | bytes 196616 | tf_op jit(solution)/shard_map/ppermute | solution.py:369
  55.2 5.8 %collective-permute-start.5 = (f32[128,128]{1,0:T(8,128)S(1)}, f32[128,128]{1,0:T(8,128)S(1)}, u32[]{:S(2)}, u32[]{:S(2)}) collective-permute-start(f32[128,128]{1,0:T(8,128)S(1)} %get-tuple-element.32.half_0), channel_id=1, source_target_pairs={{0,1},{1,2},{2,3},{3,0},{4,5},{5,6},{6,7},{7,4},{8,9},{9,10},{10,1... | collective-permute-start | bytes 196616 | tf_op jit(solution)/shard_map/ppermute | solution.py:369
  61.1 4.9 %collective-permute-start.8 = (f32[128,128]{1,0:T(8,128)S(1)}, f32[128,128]{1,0:T(8,128)S(1)}, u32[]{:S(2)}, u32[]{:S(2)}) collective-permute-start(f32[128,128]{1,0:T(8,128)S(1)} %shard_map.73.same_ref), channel_id=1, source_target_pairs={{0,32},{32,0},{1,33},{33,1},{2,34},{34,2},{3,35},{35,3},{4,36},{36... | collective-permute-start | bytes 196616 | tf_op jit(solution)/shard_map/ppermute | solution.py:364
  61.2 1.5 %collective-permute-start.4 = (f32[64,128]{1,0:T(8,128)S(1)}, f32[64,128]{1,0:T(8,128)S(1)}, u32[]{:S(2)}, u32[]{:S(2)}) collective-permute-start(f32[64,128]{1,0:T(8,128)S(1)} %get-tuple-element.28.same_ref), channel_id=1, source_target_pairs={{0,32},{32,0},{1,33},{33,1},{2,34},{34,2},{3,35},{35,3},{4,36},{36... | collective-permute-start | bytes 98312 | tf_op jit(solution)/shard_map/ppermute | solution.py:364
  98.4 1.4 %collective-permute-start.9 = (f32[320,128]{1,0:T(8,128)S(1)}, f32[320,128]{1,0:T(8,128)S(1)}, u32[]{:S(2)}, u32[]{:S(2)}) collective-permute-start(f32[320,128]{1,0:T(8,128)S(1)} %bitcast.15), channel_id=1, source_target_pairs={{0,32},{32,0},{1,33},{33,1},{2,34},{34,2},{3,35},{35,3},{4,36},{36... | collective-permute-start | bytes 491528 | tf_op jit(solution)/shard_map/ppermute | solution.py:364
  103.2 3.6 %collective-permute-start.12 = (f32[1,128]{1,0:T(1,128)S(1)}, f32[1,128]{1,0:T(1,128)S(1)}, u32[]{:S(2)}, u32[]{:S(2)}) collective-permute-start(f32[1,128]{1,0:T(1,128)S(1)} %get-tuple-element.40), channel_id=1, source_target_pairs={{0,3},{1,0},{2,1},{3,2},{4,7},{5,4},{6,5},{7,6},{8,11},{9,8},{10,9... | collective-permute-start | bytes 1544 | tf_op jit(solution)/shard_map/ppermute | solution.py:369
  104.4 5.1 %collective-permute-start.11 = (f32[1,128]{1,0:T(1,128)S(1)}, f32[1,128]{1,0:T(1,128)S(1)}, u32[]{:S(2)}, u32[]{:S(2)}) collective-permute-start(f32[1,128]{1,0:T(1,128)S(1)} %get-tuple-element.40), channel_id=1, source_target_pairs={{0,2},{1,3},{2,0},{3,1},{4,6},{5,7},{6,4},{7,5},{8,10},{9,11},{10,... | collective-permute-start | bytes 1544 | tf_op jit(solution)/shard_map/ppermute | solution.py:369
  105.3 4.8 %collective-permute-start.10 = (f32[1,128]{1,0:T(1,128)S(1)}, f32[1,128]{1,0:T(1,128)S(1)}, u32[]{:S(2)}, u32[]{:S(2)}) collective-permute-start(f32[1,128]{1,0:T(1,128)S(1)} %get-tuple-element.40), channel_id=1, source_target_pairs={{0,1},{1,2},{2,3},{3,0},{4,5},{5,6},{6,7},{7,4},{8,9},{9,10},{10,1... | collective-permute-start | bytes 1544 | tf_op jit(solution)/shard_map/ppermute | solution.py:369
